TPU v7x, 32 devices: a whole 2x2x4 slice. The times are simulated.
32 devices in a mesh: dp: 4 (over y, x), mp: 8 (over z, core).
Axes of the slice: x: 2, y: 2, z: 4, core: 2. Of those that a mesh axis runs over, the one named last changes fastest.
Arguments:
- tokens: bfloat16 [4096, 2048], P(('dp', 'mp')), may hold values from -9 to 9
- seg_ids: int32 [4096], P('dp'), may hold values from 0 to 12, as said below
- positions: int32 [4096], P('dp'), may hold values from 0 to 1023, as said below
- w_query: bfloat16 [2048, 2048], P(None, 'mp'), may hold values from -0.125 to 0.125
- w_key: bfloat16 [2048, 512], replicated, may hold values from -0.125 to 0.125
- w_value: bfloat16 [2048, 512], replicated, may hold values from -0.125 to 0.125
- w_output: bfloat16 [2048, 2048], P('mp'), may hold values from -0.75 to 0.75
- w_gate: bfloat16 [2048, 8192], P(None, 'mp'), may hold values from -0.125 to 0.125
- w_up: bfloat16 [2048, 8192], P(None, 'mp'), may hold values from -0.125 to 0.125
- w_down: bfloat16 [8192, 2048], P('mp'), may hold values from -0.0625 to 0.0625
- attn_gain: float32 [2048], replicated, may hold values from 0.5 to 1.5
- ffn_gain: float32 [2048], replicated, may hold values from 0.5 to 1.5
- query_gain: float32 [64], replicated, may hold values from 0.1 to 1.9
- key_gain: float32 [64], replicated, may hold values from 0.1 to 1.9
- out_grad: bfloat16 [4096, 2048], P(('dp', 'mp')), may hold values from -6 to 6
Outputs:
- output: bfloat16 [4096, 2048], P(('dp', 'mp'))
- grad_tokens: bfloat16 [4096, 2048], P(('dp', 'mp'))
- grad_w_query: float32 [2048, 2048], P(None, 'mp')
- grad_w_key: float32 [2048, 512], replicated
- grad_w_value: float32 [2048, 512], replicated
- grad_w_output: float32 [2048, 2048], P('mp')
- grad_w_gate: float32 [2048, 8192], P(None, 'mp')
- grad_w_up: float32 [2048, 8192], P(None, 'mp')
- grad_w_down: float32 [8192, 2048], P('mp')
- grad_attn_gain: float32 [2048], replicated
- grad_ffn_gain: float32 [2048], replicated
- grad_query_gain: float32 [64], replicated
- grad_key_gain: float32 [64], replicated
- residual_rms: float32 [1], replicated
- branch_rms: float32 [2, 4096], P(None, ('dp', 'mp'))
Inputs may be any that keep to these rules, and one draw needn't show every extreme that they name: `seg_ids`: never falling along the tokens; the first token of every block of 1024 consecutive tokens starts a new segment; the first block is one segment, every other block holds exactly 4. `positions`: 0 at the first token of a segment, one more at each following token of it.
All inputs are finite; a program needn't handle non-finite values.
Results may differ from a plain program's by a relative error of at most 0.015.
Values may be sent and summed in bfloat16 or wider, within the bound.
A program may use at most 256 MiB of HBM per device.

v0:
```python
import jax
import jax.numpy as jnp
from jax import lax
from jax.sharding import PartitionSpec as P

HEADS = 32
KV = 8
HD = 64


EPSILON = 1e-06
ROPE_BASE = 10000.0
MASKED = -1e30


def matmul(left, right):
    return jnp.dot(left, right, preferred_element_type=jnp.float32)


def matmul_left_t(left, right):
    return lax.dot_general(
        left, right, (((0,), (0,)), ((), ())), preferred_element_type=jnp.float32
    )


def matmul_right_t(left, right):
    return lax.dot_general(
        left, right, (((1,), (1,)), ((), ())), preferred_element_type=jnp.float32
    )


def rope_tables(position_row):
    half = HD // 2
    freq = ROPE_BASE ** (-jnp.arange(half, dtype=jnp.float32) / half)
    angle = position_row.astype(jnp.float32)[:, None] * freq[None, :]
    return (jnp.cos(angle)[:, None, :], jnp.sin(angle)[:, None, :])


def rotate(values, cosine, sine):
    half = HD // 2
    first_half = values[..., :half]
    second_half = values[..., half:]
    return jnp.concatenate(
        [first_half * cosine - second_half * sine, second_half * cosine + first_half * sine], -1
    )


def unrotate(grads, cosine, sine):
    half = HD // 2
    first_half = grads[..., :half]
    second_half = grads[..., half:]
    return jnp.concatenate(
        [first_half * cosine + second_half * sine, second_half * cosine - first_half * sine], -1
    )


def norm_back(grad_normed, unit, inverse, gain):
    scaled = grad_normed * gain
    return inverse * (scaled - unit * jnp.mean(scaled * unit, -1, keepdims=True))


def per_device(
    tokens,
    seg_ids,
    positions,
    w_query,
    w_key,
    w_value,
    w_output,
    w_gate,
    w_up,
    w_down,
    attn_gain,
    ffn_gain,
    query_gain,
    key_gain,
    out_grad,
):
    tok_count = tokens.shape[0]
    model_width = tokens.shape[1]
    row_count = tok_count * lax.axis_size("mp")
    query_width = w_query.shape[1]
    heads_dev = query_width // HD
    ffn_width = w_gate.shape[1]
    group = lax.axis_index("mp") * heads_dev // (HEADS // KV)
    score_scale = HD ** (-0.5)
    tokens_f = tokens.astype(jnp.float32)
    inv_one = lax.rsqrt(jnp.mean(tokens_f * tokens_f, -1, keepdims=True) + EPSILON)
    normed_one = tokens_f * inv_one
    h_one = (normed_one * attn_gain).astype(jnp.bfloat16)
    key_cols = lax.dynamic_slice_in_dim(w_key, group * HD, HD, 1)
    value_cols = lax.dynamic_slice_in_dim(w_value, group * HD, HD, 1)
    w_attn = jnp.concatenate([w_query, key_cols, value_cols], 1)
    gathered_one = lax.all_gather(h_one, "mp", axis=0, tiled=True)
    projected = matmul(gathered_one, w_attn)
    query = projected[:, :query_width].reshape(row_count, heads_dev, HD)
    key_proj = projected[:, query_width : query_width + HD]
    value_low = projected[:, query_width + HD :].astype(jnp.bfloat16)
    query_inv = lax.rsqrt(jnp.mean(query * query, -1, keepdims=True) + EPSILON)
    query_unit = query * query_inv
    key_inv = lax.rsqrt(jnp.mean(key_proj * key_proj, -1, keepdims=True) + EPSILON)
    key_unit = key_proj * key_inv
    cosine, sine = rope_tables(positions)
    query_rot = rotate(query_unit * query_gain, cosine, sine).astype(jnp.bfloat16)
    key_rot = rotate((key_unit * key_gain)[:, None, :], cosine, sine)[:, 0, :].astype(jnp.bfloat16)
    block = min(512, row_count)
    block_count = row_count // block
    token_index = jnp.arange(row_count, dtype=jnp.int32)
    starts = jnp.arange(block_count, dtype=jnp.int32) * block
    query_blocks = query_rot.reshape(block_count, block, heads_dev, HD)

    def block_scores(query_block, start):
        scores = (
            jnp.einsum("qhd,kd->hqk", query_block, key_rot, preferred_element_type=jnp.float32)
            * score_scale
        )
        segment_block = lax.dynamic_slice_in_dim(seg_ids, start, block)
        index_block = start + jnp.arange(block, dtype=jnp.int32)
        allowed = (segment_block[:, None] == seg_ids[None, :]) & (
            token_index[None, :] <= index_block[:, None]
        )
        return jnp.where(allowed[None], scores, MASKED)

    def forward_block(inputs):
        query_block, start = inputs
        scores = block_scores(query_block, start)
        top = jnp.max(scores, -1, keepdims=True)
        expo = jnp.exp(scores - top)
        total = jnp.sum(expo, -1, keepdims=True)
        probs = (expo / total).astype(jnp.bfloat16)
        context_block = jnp.einsum(
            "hqk,kd->qhd", probs, value_low, preferred_element_type=jnp.float32
        )
        return (context_block.astype(jnp.bfloat16), (top + jnp.log(total))[..., 0])

    context_blocks, lse_blocks = lax.map(forward_block, (query_blocks, starts))
    context = context_blocks.reshape(row_count, query_width)
    attn_branch = lax.psum_scatter(matmul(context, w_output), "mp", scatter_dimension=0, tiled=True)
    residual_mid = tokens_f + attn_branch
    inv_two = lax.rsqrt(jnp.mean(residual_mid * residual_mid, -1, keepdims=True) + EPSILON)
    normed_two = residual_mid * inv_two
    h_two = (normed_two * ffn_gain).astype(jnp.bfloat16)
    w_ffn = jnp.concatenate([w_gate, w_up], 1)
    gathered_two = lax.all_gather(h_two, "mp", axis=0, tiled=True)
    gate_up = matmul(gathered_two, w_ffn)
    gate = gate_up[:, :ffn_width]
    up = gate_up[:, ffn_width:]
    sigma = jax.nn.sigmoid(gate)
    silu_gate = gate * sigma
    hidden = (silu_gate * up).astype(jnp.bfloat16)
    ffn_branch = lax.psum_scatter(
        matmul(hidden, w_down).astype(jnp.bfloat16), "mp", scatter_dimension=0, tiled=True
    ).astype(jnp.float32)
    output = (residual_mid + ffn_branch).astype(jnp.bfloat16)
    branch_rms = jnp.stack(
        [
            jnp.sqrt(jnp.mean(attn_branch * attn_branch, -1)),
            jnp.sqrt(jnp.mean(ffn_branch * ffn_branch, -1)),
        ]
    )
    squares_local = jnp.sum(tokens_f * tokens_f)
    squares_total = lax.psum(squares_local, ("dp", "mp"))
    grad_out = out_grad.astype(jnp.float32)
    grad_ffn_rows = lax.all_gather(out_grad, "mp", axis=0, tiled=True)
    grad_hidden = matmul_right_t(grad_ffn_rows, w_down)
    grad_w_down = matmul_left_t(hidden, grad_ffn_rows)
    grad_gate = grad_hidden * up * sigma * (1.0 + gate * (1.0 - sigma))
    grad_up = grad_hidden * silu_gate
    grad_gate_up = jnp.concatenate([grad_gate, grad_up], 1).astype(jnp.bfloat16)
    grad_w_ffn = matmul_left_t(gathered_two, grad_gate_up)
    grad_h_two = lax.psum_scatter(
        matmul_right_t(grad_gate_up, w_ffn), "mp", scatter_dimension=0, tiled=True
    )
    grad_ffn_gain = jnp.sum(grad_h_two * normed_two, 0)
    grad_mid = grad_out + norm_back(grad_h_two, normed_two, inv_two, ffn_gain)
    grad_attn_rows = lax.all_gather(grad_mid.astype(jnp.bfloat16), "mp", axis=0, tiled=True)
    grad_w_output = matmul_left_t(context, grad_attn_rows)
    grad_context = matmul_right_t(grad_attn_rows, w_output).astype(jnp.bfloat16)
    grad_context_blocks = grad_context.reshape(block_count, block, heads_dev, HD)

    def backward_block(carry, inputs):
        grad_key_acc, grad_value_acc = carry
        query_block, grad_block, lse_block, start = inputs
        scores = block_scores(query_block, start)
        exact = jnp.exp(scores - lse_block[..., None])
        grad_probs = jnp.einsum(
            "qhd,kd->hqk", grad_block, value_low, preferred_element_type=jnp.float32
        )
        delta = jnp.sum(exact * grad_probs, -1, keepdims=True)
        grad_scores = (exact * (grad_probs - delta)).astype(jnp.bfloat16)
        grad_query_block = (
            jnp.einsum("hqk,kd->qhd", grad_scores, key_rot, preferred_element_type=jnp.float32)
            * score_scale
        )
        grad_key_acc = (
            grad_key_acc
            + jnp.einsum(
                "hqk,qhd->kd", grad_scores, query_block, preferred_element_type=jnp.float32
            )
            * score_scale
        )
        grad_value_acc = grad_value_acc + jnp.einsum(
            "hqk,qhd->kd",
            exact.astype(jnp.bfloat16),
            grad_block,
            preferred_element_type=jnp.float32,
        )
        return ((grad_key_acc, grad_value_acc), grad_query_block)

    zero_rows = jnp.zeros((row_count, HD), jnp.float32)
    (grad_key_rot, grad_value), grad_query_blocks = lax.scan(
        backward_block,
        (zero_rows, zero_rows),
        (query_blocks, grad_context_blocks, lse_blocks, starts),
    )
    grad_query_rot = grad_query_blocks.reshape(row_count, heads_dev, HD)
    grad_query_normed = unrotate(grad_query_rot, cosine, sine)
    grad_key_normed = unrotate(grad_key_rot[:, None, :], cosine, sine)[:, 0, :]
    grad_query_gain = jnp.sum(grad_query_normed * query_unit, (0, 1))
    grad_key_gain = jnp.sum(grad_key_normed * key_unit, 0)
    grad_query = norm_back(grad_query_normed, query_unit, query_inv, query_gain)
    grad_key = norm_back(grad_key_normed, key_unit, key_inv, key_gain)
    grad_proj = jnp.concatenate(
        [grad_query.reshape(row_count, query_width), grad_key, grad_value], 1
    ).astype(jnp.bfloat16)
    grad_w_attn = matmul_left_t(gathered_one, grad_proj)
    grad_h_one = lax.psum_scatter(
        matmul_right_t(grad_proj, w_attn), "mp", scatter_dimension=0, tiled=True
    )
    grad_attn_gain = jnp.sum(grad_h_one * normed_one, 0)
    grad_tokens = (grad_mid + norm_back(grad_h_one, normed_one, inv_one, attn_gain)).astype(
        jnp.bfloat16
    )
    grad_w_query = grad_w_attn[:, :query_width]
    key_zeros = jnp.zeros(w_key.shape, jnp.float32)
    grad_w_key = lax.dynamic_update_slice_in_dim(
        key_zeros, grad_w_attn[:, query_width : query_width + HD], group * HD, 1
    )
    grad_w_value = lax.dynamic_update_slice_in_dim(
        key_zeros, grad_w_attn[:, query_width + HD :], group * HD, 1
    )
    grad_w_gate = grad_w_ffn[:, :ffn_width]
    grad_w_up = grad_w_ffn[:, ffn_width:]
    summed = lax.psum((grad_w_query, grad_w_output, grad_w_gate, grad_w_up, grad_w_down), "dp")
    shared = lax.psum(
        (grad_w_key, grad_w_value, grad_attn_gain, grad_ffn_gain, grad_query_gain, grad_key_gain),
        ("dp", "mp"),
    )
    entry_count = tok_count * model_width * lax.axis_size("dp") * lax.axis_size("mp")
    residual_rms = jnp.sqrt(squares_total / entry_count).reshape(1)
    return (
        output,
        grad_tokens,
        summed[0],
        shared[0],
        shared[1],
        summed[1],
        summed[2],
        summed[3],
        summed[4],
        shared[2],
        shared[3],
        shared[4],
        shared[5],
        residual_rms,
        branch_rms,
    )


def solution(mesh):
    return jax.shard_map(
        per_device,
        mesh=mesh,
        in_specs=(
            P(("dp", "mp"), None),
            P("dp"),
            P("dp"),
            P(None, "mp"),
            P(),
            P(),
            P("mp", None),
            P(None, "mp"),
            P(None, "mp"),
            P("mp", None),
            P(),
            P(),
            P(),
            P(),
            P(("dp", "mp"), None),
        ),
        out_specs=(
            P(("dp", "mp"), None),
            P(("dp", "mp"), None),
            P(None, "mp"),
            P(),
            P(),
            P("mp", None),
            P(None, "mp"),
            P(None, "mp"),
            P("mp", None),
            P(),
            P(),
            P(),
            P(),
            P(),
            P(None, ("dp", "mp")),
        ),
        check_vma=False,
    )
```

profile of v0, /device:TPU:10, one launch (start us, length us, event | category | flops | bytes accessed | tf_op | source)
XLA Modules:
  0.0 1434.2 jit_solution(14209004250411522282)
XLA Ops:
  15.5 42.6 %all-gather.5.cloned.1.call-done = bf16[1024,2048]{1,0:T(8,128)(2,1)} async-done(((bf16[128,2048]{1,0:T(8,128)(2,1)}), bf16[1024,2048]{1,0:T(8,128)(2,1)}) %all-gather.5.cloned.1.call-update) | async-done | bytes 4194320 | tf_op jit(solution)/shard_map/all_gather | solution.py:94
  67.8 25.0 %while.28 = (s32[]{:T(128)}, bf16[2,512,4,64]{1,3,2,0:T(8,128)(2,1)}, f32[2,4,512]{2,1,0:T(4,128)}, s32[2]{0:T(128)}, s32[1024]{0:T(1024)S(1)}, /*index=5*/bf16[...) while((s32[]{:T(128)}, ...), condition=%wide.region_6.7_spmd.clone, body=%wide.region_3.6_spmd.clone.sunk | while | flops 563739136 | bytes 32454952 | solution.py:136
  94.6 4.7 fusion.102
  99.8 86.7 %reduce-scatter.5.cloned.1.call-done = f32[128,2048]{1,0:T(8,128)} async-done(((f32[1024,2048]{1,0:T(8,128)}), f32[128,2048]{1,0:T(8,128)}) %reduce-scatter.5.cloned.1.call-update) | async-done | bytes 1048592 | tf_op jit(solution)/shard_map/reduce_scatter | solution.py:138
  190.4 4.8 constant_dynamic-update-slice_fusion.1
  197.6 39.0 %all-gather.7.cloned.1.call-done = bf16[1024,2048]{1,0:T(8,128)(2,1)} async-done(((bf16[128,2048]{1,0:T(8,128)(2,1)}), bf16[1024,2048]{1,0:T(8,128)(2,1)}) %all-gather.7.cloned.1.call-update) | async-done | bytes 4194320 | tf_op jit(solution)/shard_map/all_gather | solution.py:144
  236.6 14.5 %fusion.103 = f32[1024,2048]{1,0:T(8,128)} fusion(bf16[1024,2048]{1,0:T(8,128)(2,1)} %all-gather.7.cloned.1.call-done, bf16[2048,2048]{1,0:T(8,128)(2,1)} %constant_dynamic-update-slice_fusion), kind=kOutput, calls=%fused_computation.175 | convolution fusion | flops 8589934592 | bytes 20971520 | tf_op jit(solution)/shard_map/dot_general | solution.py:17
  251.1 32.9 %all-gather.9.cloned.1.call-done = bf16[1024,2048]{1,0:T(8,128)(2,1)} async-done(((bf16[128,2048]{1,0:T(8,128)(2,1)}), bf16[1024,2048]{1,0:T(8,128)(2,1)}) %all-gather.9.cloned.1.call-update) | async-done | bytes 4194320 | tf_op jit(solution)/shard_map/all_gather | solution.py:164
  284.0 13.1 multiply_convert_fusion.1
  299.1 13.3 fusion.58
  312.7 87.0 %reduce-scatter.9.cloned.1.call-done = f32[128,2048]{1,0:T(8,128)} async-done(((f32[1024,2048]{1,0:T(8,128)}), f32[128,2048]{1,0:T(8,128)}) %reduce-scatter.9.cloned.1.call-update) | async-done | bytes 1048592 | tf_op jit(solution)/shard_map/reduce_scatter | solution.py:171
  405.0 46.1 %all-gather.11.cloned.1.call-done = bf16[1024,2048]{1,0:T(8,128)(2,1)} async-done(((bf16[128,2048]{1,0:T(8,128)(2,1)}), bf16[1024,2048]{1,0:T(8,128)(2,1)}) %all-gather.11.cloned.1.call-update) | async-done | bytes 4194320 | tf_op jit(solution)/shard_map/all_gather | solution.py:176
  456.3 80.9 %while.29 = (s32[]{:T(128)}, f32[1024,64]{0,1:T(8,128)S(1)}, f32[1024,64]{0,1:T(8,128)}, f32[2,512,4,64]{1,0,3,2:T(2,128)}, s32[2]{0:T(128)S(1)}, /*index=5*/s32...) while((s32[]{:T(128)}, f32[1024,64]{0,1:T(8,128)S(1)}, ...), condition=%wide.region_14.15_spmd.clone, body=%wide.region_12.14_spmd.clone.sunk | while | flops 1375664640 | bytes 114825640 | solution.py:211
  464.9 5.7 fusion.159
  477.7 5.9 fusion.162
  486.3 10.4 dynamic_update_slice.30
  505.3 5.7 fusion.159
  518.1 5.9 fusion.162
  526.6 10.4 dynamic_update_slice.30
  546.3 5.8 fusion.77
  552.2 9.3 convolution_convert_fusion
  562.0 10.9 fusion.105
  573.0 11.7 fusion.57
  584.7 6.8 fusion.100
  604.6 5.8 dynamic_update_slice.18
  613.0 5.9 dynamic_update_slice.19
  619.6 19.8 %reduce-scatter.11.cloned.1.call-done = f32[128,2048]{1,0:T(8,128)} async-done(((f32[1024,2048]{1,0:T(8,128)}), f32[128,2048]{1,0:T(8,128)}) %reduce-scatter.11.cloned.1.call-update) | async-done | bytes 1048592 | tf_op jit(solution)/shard_map/reduce_scatter | solution.py:227
  641.7 44.9 %all-reduce = (f32[2048]{0:T(1024)}, f32[2048]{0:T(1024)}, f32[64]{0:T(128)}, f32[64]{0:T(128)}, f32[]{:T(128)}) all-reduce(f32[2048]{0:T(1024)S(1)} %get-tuple-element.286, f32[2048]{0:T(1024)S(1)} %copy-done.44, f32[64]{0:T(128)S(1)} %reduce_sum.172, f32[64]{0:T(128)S(1)} %copy-done.55, ...), channel_id=1, replica_groups=mesh['dp'=4,'mp'=8] {'dp','mp'}, use_global_device_ids=true, to_apply=%region_27.28 | all-reduce | flops 4225 | bytes 33800 | tf_op jit(solution)/shard_map/psum | solution.py:245
  694.8 518.0 %all-reduce.8.cloned.1.call-done = (f32[2048,256]{0,1:T(8,128)}, f32[256,2048]{1,0:T(8,128)}, f32[2048,1024]{1,0:T(8,128)}, f32[2048,1024]{1,0:T(8,128)}, f32[1024,2048]{1,0:T(8,128)}) async-done(((f32[2048,256]{0,1:T(8,128)}, f32[256,2048]{1,0:T(8,128)}, f32[2048,1024]{1,0:T(8,128)}, f32[2048,1024]{1,0:T(8,128)}, f32[1024,2048]{1,0:T(8,128)}), (f32[2048,256]{0,1:T(8,128)}, f32[256,2048]{1,0:T(8,128)}, ...) | async-done | bytes 29360144 | tf_op jit(solution)/shard_map/psum | solution.py:244
  1215.7 183.4 %all-reduce.6.cloned.1.call-done = (f32[2048,512]{1,0:T(8,128)}, f32[2048,512]{1,0:T(8,128)}) async-done(((f32[2048,512]{1,0:T(8,128)}, f32[2048,512]{1,0:T(8,128)}), (f32[2048,512]{1,0:T(8,128)}, f32[2048,512]{1,0:T(8,128)})) %all-reduce.6.cloned.1.call-update) | async-done | bytes 8388624 | tf_op jit(solution)/shard_map/psum | solution.py:245
  1399.1 4.8 copy.117
  1408.3 9.1 copy.120
  (292 shorter events, 143.8 us)
Async XLA Ops:
  7.2 87.4 %copy-start = (bf16[256,2048]{1,0:T(8,128)(2,1)S(1)}, bf16[256,2048]{1,0:T(8,128)(2,1)}, u32[]{:S(2)}) copy-start(bf16[256,2048]{1,0:T(8,128)(2,1)} %param.25) | copy-start | bytes 3145732
  7.2 50.9 %all-gather.5.cloned.1.call-start = ((), (), s32[]{:S(2)}) async-start(), calls=%async_computation.4 | async-start | bytes 4718592 | tf_op jit(solution)/shard_map/all_gather | solution.py:94
  11.2 175.4 %reduce-scatter.5.cloned.1.call-start = ((), (), s32[]{:S(2)}) async-start(), calls=%async_computation.5 | async-start | bytes 9437184 | tf_op jit(solution)/shard_map/reduce_scatter | solution.py:138
  12.0 55.2 %copy-start.42 = (f32[1024]{0:T(1024)}, f32[1024]{0:T(1024)S(1)}, u32[]{:S(2)}) copy-start(f32[1024]{0:T(1024)S(1)} %convert_element_type.62) | copy-start | bytes 12292
  12.5 54.7 %copy-start.49 = (f32[32]{0:T(128)}, f32[32]{0:T(128)S(1)}, u32[]{:S(2)}) copy-start(f32[32]{0:T(128)S(1)} %multiply_power_fusion) | copy-start | bytes 388
  13.0 50.1 %copy-start.23 = (f32[1024,32]{0,1:T(8,128)}, f32[1024,32]{0,1:T(8,128)S(1)}, u32[]{:S(2)}) copy-start(f32[1024,32]{0,1:T(8,128)S(1)} %get-tuple-element.368) | copy-start | bytes 393220
  13.0 50.1 %copy-start.25 = (f32[1024,32]{0,1:T(8,128)}, f32[1024,32]{0,1:T(8,128)S(1)}, u32[]{:S(2)}) copy-start(f32[1024,32]{0,1:T(8,128)S(1)} %get-tuple-element.369) | copy-start | bytes 393220
  15.5 47.1 %copy-start.17 = (bf16[2048,64]{1,0:T(8,128)(2,1)}, bf16[2048,64]{1,0:T(8,128)(2,1)S(1)}, u32[]{:S(2)}) copy-start(bf16[2048,64]{1,0:T(8,128)(2,1)S(1)} %get-tuple-element.370) | copy-start | bytes 786436
  99.3 87.3 %copy-start.7 = (bf16[128,2048]{1,0:T(8,128)(2,1)S(1)}, bf16[128,2048]{1,0:T(8,128)(2,1)}, u32[]{:S(2)}) copy-start(bf16[128,2048]{1,0:T(8,128)(2,1)} %param.19) | copy-start | bytes 1572868
  99.3 89.3 %copy-start.36 = (f32[2048]{0:T(1024)S(1)}, f32[2048]{0:T(1024)}, u32[]{:S(2)}) copy-start(f32[2048]{0:T(1024)} %param.30) | copy-start | bytes 24580
  99.3 137.3 %all-gather.7.cloned.1.call-start = ((), (), s32[]{:S(2)}) async-start(), calls=%async_computation.6 | async-start | bytes 4718592 | tf_op jit(solution)/shard_map/all_gather | solution.py:144
  188.6 213.2 %copy-start.3 = (f32[128,2048]{1,0:T(8,128)}, f32[128,2048]{1,0:T(8,128)S(1)}, u32[]{:S(2)}) copy-start(f32[128,2048]{1,0:T(8,128)S(1)} %get-tuple-element.340) | copy-start | bytes 3145732
  188.6 213.2 %copy-start.45 = (f32[128]{0:T(128)}, f32[128]{0:T(128)S(1)}, u32[]{:S(2)}) copy-start(f32[128]{0:T(128)S(1)} %add_rsqrt_fusion.2) | copy-start | bytes 1540
  189.7 94.3 %all-gather.9.cloned.1.call-start = ((), (), s32[]{:S(2)}) async-start(), calls=%async_computation.8 | async-start | bytes 4718592 | tf_op jit(solution)/shard_map/all_gather | solution.py:164
  190.3 209.3 %reduce-scatter.9.cloned.1.call-start = ((), (), s32[]{:S(2)}) async-start(), calls=%async_computation.9 | async-start | bytes 9437184 | tf_op jit(solution)/shard_map/reduce_scatter | solution.py:171
  312.4 89.4 %copy-start.12 = (bf16[128,2048]{1,0:T(8,128)(2,1)S(1)}, bf16[128,2048]{1,0:T(8,128)(2,1)}, u32[]{:S(2)}) copy-start(bf16[128,2048]{1,0:T(8,128)(2,1)} %param.33) | copy-start | bytes 1572868
  312.4 91.9 %copy-start.51 = (f32[64]{0:T(128)S(1)}, f32[64]{0:T(128)}, u32[]{:S(2)}) copy-start(f32[64]{0:T(128)} %param.31) | copy-start | bytes 772
  312.4 138.7 %all-gather.11.cloned.1.call-start = ((), (), s32[]{:S(2)}) async-start(), calls=%async_computation.10 | async-start | bytes 4718592 | tf_op jit(solution)/shard_map/all_gather | solution.py:176
  404.2 235.2 %reduce-scatter.11.cloned.1.call-start = ((), (), s32[]{:S(2)}) async-start(), calls=%async_computation.11 | async-start | bytes 9437184 | tf_op jit(solution)/shard_map/reduce_scatter | solution.py:227
  405.0 51.4 %copy-start.58 = (s32[2]{0:T(128)S(1)}, s32[2]{0:T(128)}, u32[]{:S(2)}) copy-start(s32[2]{0:T(128)} %get-tuple-element.654) | copy-start | bytes 28
  456.3 83.9 %copy-start.6 = (f32[1024,384]{0,1:T(8,128)S(1)}, f32[1024,384]{0,1:T(8,128)}, u32[]{:S(2)}) copy-start(f32[1024,384]{0,1:T(8,128)} %copy-done.5) | copy-start | bytes 4718596
  552.2 139.0 %reduce-scatter.7.cloned.1.call-start = ((), (), s32[]{:S(2)}) async-start(), calls=%async_computation.7 | async-start | bytes 4718592 | tf_op jit(solution)/shard_map/reduce_scatter | solution.py:151
  561.6 651.2 %all-reduce.8.cloned.1.call-start = ((), (), s32[]{:S(2)}) async-start(), calls=%async_computation.13 | async-start | bytes 58720256 | tf_op jit(solution)/shard_map/psum | solution.py:244
  599.8 799.2 %all-reduce.6.cloned.1.call-start = ((), (), s32[]{:S(2)}) async-start(), calls=%async_computation.12 | async-start | bytes 16777216 | tf_op jit(solution)/shard_map/psum | solution.py:245
  618.9 22.8 %copy-start.44 = (f32[2048]{0:T(1024)S(1)}, f32[2048]{0:T(1024)}, u32[]{:S(2)}) copy-start(f32[2048]{0:T(1024)} %get-tuple-element.282) | copy-start | bytes 24580
  618.9 22.8 %copy-start.55 = (f32[64]{0:T(128)S(1)}, f32[64]{0:T(128)}, u32[]{:S(2)}) copy-start(f32[64]{0:T(128)} %get-tuple-element.284) | copy-start | bytes 772
  618.9 72.2 %copy-start.4 = (f32[128,2048]{1,0:T(8,128)S(1)}, f32[128,2048]{1,0:T(8,128)}, u32[]{:S(2)}) copy-start(f32[128,2048]{1,0:T(8,128)} %copy-done.3) | copy-start | bytes 3145732
  618.9 72.2 %copy-start.9 = (f32[128,2048]{1,0:T(8,128)S(1)}, f32[128,2048]{1,0:T(8,128)}, u32[]{:S(2)}) copy-start(f32[128,2048]{1,0:T(8,128)} %reduce-scatter.9.cloned.1.call-done) | copy-start | bytes 3145732
  618.9 72.2 %copy-start.13 = (bf16[128,2048]{1,0:T(8,128)(2,1)S(1)}, bf16[128,2048]{1,0:T(8,128)(2,1)}, u32[]{:S(2)}) copy-start(bf16[128,2048]{1,0:T(8,128)(2,1)} %param.33) | copy-start | bytes 1572868
  618.9 72.2 %copy-start.37 = (f32[2048]{0:T(1024)S(1)}, f32[2048]{0:T(1024)}, u32[]{:S(2)}) copy-start(f32[2048]{0:T(1024)} %param.30) | copy-start | bytes 24580
  618.9 72.2 %copy-start.46 = (f32[128]{0:T(128)S(1)}, f32[128]{0:T(128)}, u32[]{:S(2)}) copy-start(f32[128]{0:T(128)} %copy-done.45) | copy-start | bytes 1540
  618.9 72.2 %copy-start.54 = (f32[128]{0:T(128)S(1)}, f32[128]{0:T(128)}, u32[]{:S(2)}) copy-start(f32[128]{0:T(128)} %copy-done.53) | copy-start | bytes 1540
  (57 other events, 293.7 us)
Sparse Core Ops, SparseCore 0:
  11.3 46.7 all-gather.4
  99.4 87.0 reduce-scatter.4
  189.9 46.7 all-gather.6
  238.1 45.8 all-gather.8
  312.6 87.0 reduce-scatter.8
  404.3 46.7 all-gather.10
  552.3 87.0 reduce-scatter.10
  642.2 48.8 reduce-scatter.6
  696.0 516.7 all-reduce.7
  1220.1 178.9 all-reduce.5
where the time goes:
time: 1450 us; the launch traced here: 1430 us
  waiting for transfers between devices  1060 us (73%)
  matrix products  149 us (10%)
  local copies, waits for them, and re-layouts  107 us (7%)
  other arithmetic  46.2 us (3%)
  blocking collectives  44.9 us (3%)
  between operations  17 us (1%)
    psum x1, waiting for transfers between devices, per_device(): lax.psum((grad_w_query, grad_w_output, grad_w_gate, grad_w_up, grad_w_dow...  518 us
    psum x1, waiting for transfers between devices, per_device(): lax.psum((grad_w_key, grad_w_value, grad_attn_gain, grad_ffn_gain, grad_q...  183 us
    reduce_scatter x1, waiting for transfers between devices, per_device(): lax.psum_scatter(matmul_right_t(grad_gate_up, w_ffn), 'mp', scatter_dimen...  87 us
    reduce_scatter x1, waiting for transfers between devices, per_device(): lax.psum_scatter(matmul(context, w_output), 'mp', scatter_dimension=0, ti...  86.7 us
    all_gather x1, waiting for transfers between devices, per_device(): lax.all_gather(grad_mid.astype(jnp.bfloat16), 'mp', axis=0, tiled=True)  46.1 us
    psum x1, blocking collectives, per_device(): lax.psum((grad_w_key, grad_w_value, grad_attn_gain, grad_ffn_gain, grad_q...  44.9 us
    all_gather x1, waiting for transfers between devices, per_device(): gathered_one = lax.all_gather(h_one, 'mp', axis=0, tiled=True)  42.6 us
    unnamed x125, local copies, waits for them, and re-layouts  39.9 us
  transfers between devices with their start and end apart: 10, of which 10 were waited for; matrix products, arithmetic and copies ran while one was open for 7% of the time, Pallas kernels for 0%

commit v1 on v0

v1 whole, which is shorter than its diff:
```python
import functools

import jax
import jax.numpy as jnp
from jax import lax
from jax.experimental import pallas as pl
from jax.experimental.pallas import tpu as pltpu
from jax.sharding import PartitionSpec as P

HEADS = 32
KV = 8
HD = 64
EPSILON = 1e-06
ROPE_BASE = 10000.0
BLOCK = 256
F32 = jnp.float32
BF16 = jnp.bfloat16
MESH = pl.DeviceIdType.MESH


ANY = pl.BlockSpec(memory_space=pl.ANY)
VMEM = pl.BlockSpec(memory_space=pltpu.VMEM)


class Place:
    def __init__(self, members, parts):
        me = lax.axis_index("mp")
        self.dp, self.pos, self.core = lax.axis_index("dp"), me // 2, lax.rem(me, 2)
        self.length, self.parts = members // 2, parts
        self.last = self.length - 1

    def at(self, pos, core):
        return (self.dp, pos * 2 + core)

    def partner(self, bit):
        mine = lax.rem(self.dp // (1 << bit), 2)
        return mine, (self.dp + (1 - 2 * mine) * (1 << bit), self.pos * 2 + self.core)

    def bits(self):
        return self.parts.bit_length() - 1

    def meet(self, line, across):
        barrier = pltpu.get_barrier_semaphore()

        def tell(device):
            pl.semaphore_signal(barrier, inc=1, device_id=device, device_id_type=MESH)

        peers = 0
        if line:
            tell(self.at(self.pos, 1 - self.core))

            @pl.when(self.pos > 0)
            def _():
                tell(self.at(self.pos - 1, self.core))

            @pl.when(self.pos < self.last)
            def _():
                tell(self.at(self.pos + 1, self.core))

            peers = 1 + jnp.minimum(self.pos, 1) + jnp.minimum(self.last - self.pos, 1)
        if across:
            for bit in range(self.bits()):
                tell(self.partner(bit)[1])
            peers = peers + self.bits()
        pl.semaphore_wait(barrier, peers)


def remote(src, dst, send_sem, recv_sem, device):
    return pltpu.make_async_remote_copy(
        src_ref=src, dst_ref=dst, send_sem=send_sem, recv_sem=recv_sem, device_id=device, device_id_type=MESH
    )


class Gather:
    line, across = True, False

    def __init__(self, x, members):
        length = members // 2
        sems = pltpu.SemaphoreType.DMA((length,))
        self.inputs = [(x, ANY)]
        self.outputs = [(jax.ShapeDtypeStruct((members * x.shape[0],) + x.shape[1:], x.dtype), ANY)]
        self.scratch = [pltpu.SemaphoreType.DMA, sems, sems, sems, pltpu.SemaphoreType.DMA((members,))]

    def run(self, here, x_ref, o_ref, own_sem, left_sem, right_sem, side_sem, recv_sem):
        pos, core, length = here.pos, here.core, here.length
        rows = x_ref.shape[0]

        def block(p, c):
            return o_ref.at[pl.ds(pl.multiple_of((p * 2 + c) * rows, rows), rows)]

        def send(src, p, sem, to_p, to_c):
            remote(src, block(p, core), sem.at[p], recv_sem.at[p * 2 + core], here.at(to_p, to_c)).start()

        def arrived(p, c):
            pltpu.make_async_copy(x_ref, block(p, c), recv_sem.at[p * 2 + c]).wait()

        def sent(sem, p):
            pltpu.make_async_copy(x_ref, block(pos, core), sem.at[p]).wait()

        @pl.when(pos > 0)
        def _():
            send(x_ref, pos, left_sem, pos - 1, core)

        @pl.when(pos < here.last)
        def _():
            send(x_ref, pos, right_sem, pos + 1, core)

        send(x_ref, pos, side_sem, pos, 1 - core)
        own = pltpu.make_async_copy(x_ref, block(pos, core), own_sem)
        own.start()
        for step in range(1, length):
            yield
            right, left = pos + step, pos - step

            @pl.when(right < length)
            def _():
                arrived(right, core)

                @pl.when(pos > 0)
                def _():
                    send(block(right, core), right, left_sem, pos - 1, core)

                send(block(right, core), right, side_sem, pos, 1 - core)

            @pl.when(left >= 0)
            def _():
                arrived(left, core)

                @pl.when(pos < here.last)
                def _():
                    send(block(left, core), left, right_sem, pos + 1, core)

                send(block(left, core), left, side_sem, pos, 1 - core)

        yield
        own.wait()

        def drain(p, carry):
            arrived(p, 1 - core)
            sent(side_sem, p)

            @pl.when((p >= pos) & (pos > 0))
            def _():
                sent(left_sem, p)

            @pl.when((p <= pos) & (pos < here.last))
            def _():
                sent(right_sem, p)

            return carry

        lax.fori_loop(0, length, drain, 0)


class Scatter:
    line, across = True, False

    def __init__(self, parts, members):
        length = members // 2
        rows, width = parts.shape[0] // members, parts.shape[1]
        self.rows = rows
        self.inputs = [(parts, VMEM)]
        self.outputs = [(jax.ShapeDtypeStruct((rows, width), F32), VMEM)]
        self.scratch = [pltpu.VMEM((length, rows, width), parts.dtype)] * 5
        self.scratch += [pltpu.SemaphoreType.DMA((length,))] * 6

    def run(self, here, p_ref, o_ref, side_buf, left_in, right_in, left_out, right_out,
            side_send, side_recv, right_send, right_recv, left_send, left_recv):
        pos, core, length, last = here.pos, here.core, here.length, here.last
        rows, tile = self.rows, 32

        def side_copy(p):
            block = p_ref.at[pl.ds(pl.multiple_of((p * 2 + 1 - core) * rows, rows), rows)]
            return remote(block, side_buf.at[p], side_send.at[p], side_recv.at[p], here.at(pos, 1 - core))

        def line_copy(p, right):
            if right:
                return remote(right_out.at[p], right_in.at[p], right_send.at[p], right_recv.at[p], here.at(pos + 1, core))
            return remote(left_out.at[p], left_in.at[p], left_send.at[p], left_recv.at[p], here.at(pos - 1, core))

        def push(i, carry):
            @pl.when(last - i > pos)
            def _():
                side_copy(last - i).start()

            @pl.when(i < pos)
            def _():
                side_copy(i).start()

            return carry

        lax.fori_loop(0, length, push, 0)
        side_copy(pos).start()

        def add(p, incoming, out):
            def body(r, carry):
                s = pl.ds(pl.multiple_of(r * tile, tile), tile)
                mine = pl.ds(pl.multiple_of((p * 2 + core) * rows + r * tile, tile), tile)
                total = p_ref[mine].astype(F32) + side_buf[p, s].astype(F32)
                for ref in incoming:
                    total = total + ref[p, s].astype(F32)
                if out is None:
                    o_ref[s] = total
                else:
                    out[p, s] = total.astype(out.dtype)
                return carry

            lax.fori_loop(0, rows // tile, body, 0)

        def move(p, right, first, source, target):
            side_copy(p).wait_recv()

            @pl.when(first)
            def _():
                add(p, [], target)

            @pl.when(jnp.logical_not(first))
            def _():
                line_copy(p, right).wait_recv()
                add(p, [source], target)

            line_copy(p, right).start()

        def slot(t):
            right_p, left_p = last - t + pos, t - (last - pos)

            @pl.when(t >= pos)
            def _():
                move(right_p, True, pos == 0, right_in, right_out)

            @pl.when(left_p >= 0)
            def _():
                move(left_p, False, pos == last, left_in, left_out)

        for t in range(last):
            yield
            slot(t)
        yield
        side_copy(pos).wait_recv()

        @pl.when(pos == 0)
        def _():
            line_copy(pos, False).wait_recv()
            add(pos, [left_in], None)

        @pl.when(pos == last)
        def _():
            line_copy(pos, True).wait_recv()
            add(pos, [right_in], None)

        @pl.when((pos > 0) & (pos < last))
        def _():
            line_copy(pos, False).wait_recv()
            line_copy(pos, True).wait_recv()
            add(pos, [left_in, right_in], None)

        def drain(p, carry):
            side_copy(p).wait_send()

            @pl.when(p > pos)
            def _():
                line_copy(p, True).wait_send()

            @pl.when(p < pos)
            def _():
                line_copy(p, False).wait_send()

            return carry

        lax.fori_loop(0, length, drain, 0)


class Across:
    line, across = False, True

    def __init__(self, x, parts, backwards):
        self.bits = parts.bit_length() - 1
        self.order = list(range(self.bits))[:: -1 if backwards else 1]
        rows, width = x.shape
        self.inputs = [(x, VMEM)]
        self.outputs = [(jax.ShapeDtypeStruct(x.shape, x.dtype), VMEM)]
        self.scratch = [pltpu.VMEM((rows, width), x.dtype)]
        self.scratch += [pltpu.VMEM((rows >> (s + 1), width), x.dtype) for s in range(self.bits)]
        self.scratch += [pltpu.SemaphoreType.DMA((2 * self.bits,))] * 2

    def run(self, here, x_ref, o_ref, sum_ref, *rest):
        taken, (send_sem, recv_sem) = rest[: self.bits], rest[self.bits :]
        rows = x_ref.shape[0]
        start, size, copies, tile = 0, rows, [], 16

        def part(ref, at, count):
            return ref.at[pl.ds(pl.multiple_of(at, count), count)]

        for s, bit in enumerate(self.order):
            mine, device = here.partner(bit)
            half = size // 2
            keep, give = start + mine * half, start + (1 - mine) * half
            source = x_ref if s == 0 else sum_ref
            target = o_ref if s == self.bits - 1 else sum_ref
            copy = remote(part(source, give, half), taken[s], send_sem.at[s], recv_sem.at[s], device)
            copy.start()
            copies.append(copy)
            yield
            copy.wait_recv()

            def body(r, carry):
                at = pl.ds(pl.multiple_of(keep + r * tile, tile), tile)
                got = taken[s][pl.ds(pl.multiple_of(r * tile, tile), tile)]
                target[at] = (source[at].astype(F32) + got.astype(F32)).astype(target.dtype)
                return carry

            lax.fori_loop(0, half // tile, body, 0)
            start, size = keep, half
        for s, bit in enumerate(self.order[::-1]):
            mine, device = here.partner(bit)
            n = self.bits + s
            copy = remote(part(o_ref, start, size), part(o_ref, start, size), send_sem.at[n], recv_sem.at[n], device)
            copy.start()
            copies.append(copy)
            yield
            copy.wait_recv()
            start, size = start - mine * size, size * 2
        yield
        for copy in copies:
            copy.wait_send()


def together(steps, members, parts, collective_id, vmem=48):
    counts = [(len(s.inputs), len(s.outputs), len(s.scratch)) for s in steps]

    def kernel(*refs):
        refs = list(refs)
        given = [[refs.pop(0) for _ in range(c[0])] for c in counts]
        made = [[refs.pop(0) for _ in range(c[1])] for c in counts]
        held = [[refs.pop(0) for _ in range(c[2])] for c in counts]
        here = Place(members, parts)
        here.meet(any(s.line for s in steps), any(s.across for s in steps))
        live = [s.run(here, *g, *m, *h) for s, g, m, h in zip(steps, given, made, held)]
        while live:
            live = [r for r in live if next(r, live) is not live]

    return pl.pallas_call(
        kernel,
        out_shape=[o for s in steps for o, _ in s.outputs],
        in_specs=[m for s in steps for _, m in s.inputs],
        out_specs=[m for s in steps for _, m in s.outputs],
        scratch_shapes=[h for s in steps for h in s.scratch],
        compiler_params=pltpu.CompilerParams(
            collective_id=collective_id, has_side_effects=True, vmem_limit_bytes=vmem << 20
        ),
        cost_estimate=pl.CostEstimate(flops=1, bytes_accessed=1, transcendentals=0),
    )(*[x for s in steps for x, _ in s.inputs])


def dot_nn(a, b):
    return lax.dot_general(a, b, (((1,), (0,)), ((), ())), preferred_element_type=F32)

def dot_nt(a, b):
    return lax.dot_general(a, b, (((1,), (1,)), ((), ())), preferred_element_type=F32)

def group_mean(x):
    width = x.shape[1]
    row = lax.broadcasted_iota(jnp.int32, (width, width), 0) // HD
    col = lax.broadcasted_iota(jnp.int32, (width, width), 1) // HD
    ones = jnp.where(row == col, 1.0 / HD, 0.0).astype(F32)
    return jnp.dot(x, ones, precision=lax.Precision.HIGHEST, preferred_element_type=F32)

def half_turn(x):
    width = x.shape[1]
    lane = lax.broadcasted_iota(jnp.int32, (1, width), 1)
    first = lax.rem(lane, HD) < HD // 2
    up = pltpu.roll(x, HD // 2, 1)
    down = pltpu.roll(x, width - HD // 2, 1)
    return jnp.where(first, -down, up)

def wide(table, width):
    return jnp.concatenate([table] * (width // table.shape[1]), 1)

def normed(x):
    inv = lax.rsqrt(group_mean(x * x) + EPSILON)
    return x * inv, inv

def turn(x, cosine, sine):
    return x * cosine + half_turn(x) * sine

def turn_back(x, cosine, sine):
    return x * cosine - half_turn(x) * sine

def attend_kernel(heads, proj_ref, cos_ref, sin_ref, gain_ref, pos_ref, ctx_ref, lse_ref, k_ref, v_ref, acc_ref):
    width = heads * HD
    scale = HD ** -0.5
    count = proj_ref.shape[0] // BLOCK
    lane = lax.broadcasted_iota(jnp.int32, (1, HD), 1)
    def outer(i, carry):
        rows = pl.ds(pl.multiple_of(i * BLOCK, BLOCK), BLOCK)
        x = proj_ref[rows]
        cosine, sine = wide(cos_ref[rows], width + 2 * HD), wide(sin_ref[rows], width + 2 * HD)
        unit, _ = normed(x)
        spun = turn(unit * gain_ref[...], cosine, sine)
        query = spun[:, :width].astype(BF16) * scale
        query = query.astype(BF16)
        stacked = jnp.concatenate([query[:, h * HD:(h + 1) * HD] for h in range(heads)], 0)
        k_ref[rows] = spun[:, width:width + HD].astype(BF16)
        value = x[:, width + HD:].astype(BF16)
        ones = jnp.broadcast_to(jnp.where(lane == 0, 1.0, 0.0), (BLOCK, HD)).astype(BF16)
        v_ref[rows] = jnp.concatenate([value, ones], 1)
        acc_ref[...] = jnp.zeros_like(acc_ref)
        index = i * BLOCK + lax.broadcasted_iota(jnp.int32, (BLOCK, 1), 0)
        start = index - pos_ref[rows]
        def inner(j, c):
            cols = pl.ds(pl.multiple_of(j * BLOCK, BLOCK), BLOCK)
            scores = dot_nt(stacked, k_ref[cols])
            place = j * BLOCK + lax.broadcasted_iota(jnp.int32, (1, BLOCK), 1)
            seen = (place >= start) & (place <= index)
            expo = jnp.concatenate(
                [jnp.where(seen, jnp.exp(scores[h * BLOCK:(h + 1) * BLOCK]), 0.0).astype(BF16) for h in range(heads)], 0)
            acc_ref[...] += dot_nn(expo, v_ref[cols])
            return c
        lax.fori_loop(0, i + 1, inner, 0)
        outs, logs = [], []
        for h in range(heads):
            acc = acc_ref[pl.ds(h * BLOCK, BLOCK)]
            total = acc[:, HD:HD + 1]
            outs.append((acc[:, :HD] * (1.0 / total)).astype(BF16))
            logs.append(jnp.log(acc.T[HD:HD + 1]))
        ctx_ref[rows] = jnp.concatenate(outs, 1)
        lse_ref[i] = jnp.concatenate(logs, 1)
        return carry
    lax.fori_loop(0, count, outer, 0)

def attend(proj, cosine, sine, gain, positions, heads):
    size = proj.shape[0]
    count = size // BLOCK
    vm = pl.BlockSpec(memory_space=pltpu.VMEM)
    return pl.pallas_call(
        functools.partial(attend_kernel, heads),
        out_shape=(jax.ShapeDtypeStruct((size, heads * HD), BF16), jax.ShapeDtypeStruct((count, 1, heads * BLOCK), F32)),
        in_specs=[vm] * 5, out_specs=(vm, vm),
        scratch_shapes=[pltpu.VMEM((size, HD), BF16), pltpu.VMEM((size, 2 * HD), BF16), pltpu.VMEM((heads * BLOCK, 2 * HD), F32)],
        compiler_params=pltpu.CompilerParams(vmem_limit_bytes=40 << 20),
        cost_estimate=pl.CostEstimate(flops=1, bytes_accessed=1, transcendentals=0),
    )(proj, cosine, sine, gain, positions.reshape(size, 1))

def stack_lanes(x, heads):
    return jnp.concatenate([x[h * HD:(h + 1) * HD] for h in range(heads)], 1)

def attend_back_kernel(heads, proj_ref, cos_ref, sin_ref, gain_ref, pos_ref, ctx_ref, grad_ref, lse_ref,
                       out_ref, sums_ref, k_ref, kt_ref, v_ref, dk_ref, dv_ref, dq_ref):
    width = heads * HD
    scale = HD ** -0.5
    count = proj_ref.shape[0] // BLOCK
    gain = gain_ref[...]
    def prepare(i, carry):
        rows = pl.ds(pl.multiple_of(i * BLOCK, BLOCK), BLOCK)
        x = proj_ref[rows, width:]
        unit, _ = normed(x)
        spun = turn(unit * gain[:, width:], cos_ref[rows], sin_ref[rows])
        k_ref[rows] = spun[:, :HD].astype(BF16)
        kt_ref[i] = spun.T[:HD].astype(BF16)
        v_ref[rows] = x[:, HD:].astype(BF16)
        dk_ref[rows] = jnp.zeros((BLOCK, HD), F32)
        dv_ref[rows] = jnp.zeros((BLOCK, HD), F32)
        return carry
    lax.fori_loop(0, count, prepare, 0)
    sums_ref[...] = jnp.zeros_like(sums_ref)
    def outer(i, carry):
        rows = pl.ds(pl.multiple_of(i * BLOCK, BLOCK), BLOCK)
        x = proj_ref[rows, :width]
        cosine, sine = wide(cos_ref[rows], width), wide(sin_ref[rows], width)
        unit, inv = normed(x)
        query = (turn(unit * gain[:, :width], cosine, sine).astype(BF16).astype(F32) * scale)
        query_t = stack_lanes(query.T, heads).astype(BF16)
        query = query.astype(BF16)
        query_s = jnp.concatenate([query[:, h * HD:(h + 1) * HD] for h in range(heads)], 0)
        grad = grad_ref[rows]
        grad_s = jnp.concatenate([grad[:, h * HD:(h + 1) * HD] for h in range(heads)], 0)
        grad_t = stack_lanes(grad.astype(F32).T, heads)
        ctx_t = stack_lanes(ctx_ref[rows].astype(F32).T, heads)
        delta = jnp.sum(grad_t * ctx_t, 0, keepdims=True)
        grad_t = grad_t.astype(BF16)
        lse = lse_ref[i]
        index = i * BLOCK + lax.broadcasted_iota(jnp.int32, (1, BLOCK), 1)
        start = index - pos_ref[i]
        dq_ref[...] = jnp.zeros_like(dq_ref)
        def inner(j, c):
            cols = pl.ds(pl.multiple_of(j * BLOCK, BLOCK), BLOCK)
            scores = dot_nn(k_ref[cols], query_t)
            grad_probs = dot_nn(v_ref[cols], grad_t)
            place = j * BLOCK + lax.broadcasted_iota(jnp.int32, (BLOCK, 1), 0)
            seen = (place >= start) & (place <= index)
            probs, back = [], []
            for h in range(heads):
                s = slice(h * BLOCK, (h + 1) * BLOCK)
                exact = jnp.where(seen, jnp.exp(scores[:, s] - lse[:, s]), 0.0)
                probs.append(exact.astype(BF16))
                back.append((exact * (grad_probs[:, s] - delta[:, s])).astype(BF16))
            probs = jnp.concatenate(probs, 1)
            back = jnp.concatenate(back, 1)
            dv_ref[cols] += dot_nn(probs, grad_s)
            dk_ref[cols] += dot_nn(back, query_s)
            dq_ref[...] += dot_nn(kt_ref[j], back)
            return c
        lax.fori_loop(0, i + 1, inner, 0)
        dq = jnp.concatenate([dq_ref[:, h * BLOCK:(h + 1) * BLOCK] for h in range(heads)], 0).T * scale
        dqn = turn_back(dq, cosine, sine)
        sums_ref[:, :width] += jnp.sum(dqn * unit, 0, keepdims=True)
        e = dqn * gain[:, :width]
        out_ref[rows, :width] = (inv * (e - unit * group_mean(e * unit))).astype(BF16)
        return carry
    lax.fori_loop(0, count, outer, 0)
    def finish(i, carry):
        rows = pl.ds(pl.multiple_of(i * BLOCK, BLOCK), BLOCK)
        x = proj_ref[rows, width:]
        unit, inv = normed(x)
        dv = dv_ref[rows]
        dk = jnp.concatenate([dk_ref[rows], dv], 1)
        dkn = turn_back(dk, cos_ref[rows], sin_ref[rows])
        sums_ref[:, width:] += jnp.sum(dkn * unit, 0, keepdims=True)
        e = dkn * gain[:, width:]
        dkp = inv * (e - unit * group_mean(e * unit))
        lane = lax.broadcasted_iota(jnp.int32, (1, 2 * HD), 1)
        out_ref[rows, width:] = jnp.where(lane < HD, dkp, dk).astype(BF16)
        return carry
    lax.fori_loop(0, count, finish, 0)

def attend_back(proj, cosine, sine, gain, positions, context, grad_context, lse, heads):
    size = proj.shape[0]
    count = size // BLOCK
    vm = pl.BlockSpec(memory_space=pltpu.VMEM)
    return pl.pallas_call(
        functools.partial(attend_back_kernel, heads),
        out_shape=(jax.ShapeDtypeStruct(proj.shape, BF16), jax.ShapeDtypeStruct((1, proj.shape[1]), F32)),
        in_specs=[vm] * 8, out_specs=(vm, vm),
        scratch_shapes=[pltpu.VMEM((size, HD), BF16), pltpu.VMEM((count, HD, BLOCK), BF16), pltpu.VMEM((size, HD), BF16),
                        pltpu.VMEM((size, HD), F32), pltpu.VMEM((size, HD), F32), pltpu.VMEM((HD, heads * BLOCK), F32)],
        compiler_params=pltpu.CompilerParams(vmem_limit_bytes=40 << 20),
        cost_estimate=pl.CostEstimate(flops=1, bytes_accessed=1, transcendentals=0),
    )(proj, cosine, sine, gain, positions.reshape(count, 1, BLOCK), context, grad_context, lse)


def matmul(left, right):
    return jnp.dot(left, right, preferred_element_type=F32)


def matmul_left_t(left, right):
    return lax.dot_general(left, right, (((0,), (0,)), ((), ())), preferred_element_type=F32)


def matmul_right_t(left, right):
    return lax.dot_general(left, right, (((1,), (1,)), ((), ())), preferred_element_type=F32)


def rope_tables(position_row):
    half = HD // 2
    freq = ROPE_BASE ** (-jnp.arange(half, dtype=F32) / half)
    angle = position_row.astype(F32)[:, None] * freq[None, :]
    return jnp.tile(jnp.cos(angle), (1, 4)), jnp.tile(jnp.sin(angle), (1, 4))


def norm_back(grad_normed, unit, inverse, gain):
    scaled = grad_normed * gain
    return inverse * (scaled - unit * jnp.mean(scaled * unit, -1, keepdims=True))


def after(first, *later):
    return lax.optimization_barrier((first,) + later)


def per_device(
    tokens,
    seg_ids,
    positions,
    w_query,
    w_key,
    w_value,
    w_output,
    w_gate,
    w_up,
    w_down,
    attn_gain,
    ffn_gain,
    query_gain,
    key_gain,
    out_grad,
):
    members, parts = lax.axis_size("mp"), lax.axis_size("dp")
    width = tokens.shape[1]
    query_width = w_query.shape[1]
    heads = query_width // HD
    ffn_width = w_gate.shape[1]
    share = members // KV
    group = lax.axis_index("mp") // share

    tokens_f = tokens.astype(F32)
    inv_one = lax.rsqrt(jnp.mean(tokens_f * tokens_f, -1, keepdims=True) + EPSILON)
    normed_one = tokens_f * inv_one
    h_one = (normed_one * attn_gain).astype(BF16)
    key_cols = lax.dynamic_slice_in_dim(w_key, group * HD, HD, 1)
    value_cols = lax.dynamic_slice_in_dim(w_value, group * HD, HD, 1)
    w_attn = jnp.concatenate([w_query, key_cols, value_cols], 1)
    cosine, sine = rope_tables(positions)
    gain = jnp.concatenate([jnp.tile(query_gain, heads), key_gain, jnp.ones(HD, F32)])[None]

    rows_one = together([Gather(h_one, members)], members, parts, 0)[0]
    rows_one, out_grad_late = after(rows_one, out_grad)
    grad_rows = lax.all_gather(out_grad_late, "mp", axis=0, tiled=True)
    projected = matmul(rows_one, w_attn)
    context, lse = attend(projected, cosine, sine, gain, positions, heads)
    attn_part = matmul(context, w_output).astype(BF16)
    attn_branch = together([Scatter(attn_part, members)], members, parts, 1)[0]
    residual_mid = tokens_f + attn_branch
    inv_two = lax.rsqrt(jnp.mean(residual_mid * residual_mid, -1, keepdims=True) + EPSILON)
    normed_two = residual_mid * inv_two
    h_two = (normed_two * ffn_gain).astype(BF16)
    w_ffn = jnp.concatenate([w_gate, w_up], 1)
    rows_two = together([Gather(h_two, members)], members, parts, 0)[0]
    gate_up = matmul(rows_two, w_ffn)
    gate = gate_up[:, :ffn_width]
    up = gate_up[:, ffn_width:]
    sigma = jax.nn.sigmoid(gate)
    silu_gate = gate * sigma
    hidden = (silu_gate * up).astype(BF16)
    grad_hidden = matmul_right_t(grad_rows, w_down)
    grad_gate = (grad_hidden * up * sigma * (1.0 + gate * (1.0 - sigma))).astype(BF16)
    grad_up = (grad_hidden * silu_gate).astype(BF16)
    grad_gate_up = jnp.concatenate([grad_gate, grad_up], 1)
    down_part = matmul_left_t(hidden, grad_rows).astype(BF16)
    gate_part = matmul_left_t(rows_two, grad_gate).astype(BF16)
    up_part = matmul_left_t(rows_two, grad_up).astype(BF16)
    down_part, gate_part, up_part, grad_gate_up, hidden = lax.optimization_barrier(
        (down_part, gate_part, up_part, grad_gate_up, hidden)
    )
    grad_w_down, grad_w_gate, grad_w_up = lax.psum((down_part, gate_part, up_part), "dp")

    grad_h_two_part = matmul_right_t(grad_gate_up, w_ffn).astype(BF16)
    grad_h_two = together([Scatter(grad_h_two_part, members)], members, parts, 1)[0]
    grad_ffn_gain = jnp.sum(grad_h_two * normed_two, 0)
    grad_mid = out_grad.astype(F32) + norm_back(grad_h_two, normed_two, inv_two, ffn_gain)
    ffn_part = matmul(hidden, w_down).astype(BF16)
    grad_attn_rows, ffn_branch = together(
        [Gather(grad_mid.astype(BF16), members), Scatter(ffn_part, members)], members, parts, 2
    )
    grad_context = matmul_right_t(grad_attn_rows, w_output).astype(BF16)
    grad_proj, gain_sums = attend_back(
        projected, cosine, sine, gain, positions, context, grad_context, lse, heads
    )
    output_part = matmul_left_t(context, grad_attn_rows).astype(BF16)
    grad_w_attn = matmul_left_t(rows_one, grad_proj)
    grad_attn_gain = jnp.sum(w_attn.astype(F32) * grad_w_attn, 1) / attn_gain

    small = jnp.concatenate(
        [
            grad_attn_gain,
            grad_ffn_gain,
            jnp.sum(gain_sums[0, :query_width].reshape(heads, HD), 0),
            gain_sums[0, query_width : query_width + HD],
            jnp.sum(tokens_f * tokens_f)[None],
        ]
    )
    columns = w_attn.shape[1]
    unit = 16 * parts
    extra = -(-small.shape[0] // (unit * columns)) * unit
    small_rows = jnp.pad(small, (0, extra * columns - small.shape[0])).reshape(extra, columns)
    attn_part = jnp.concatenate([grad_w_attn, small_rows], 0).astype(BF16)
    grad_h_one_part = matmul_right_t(grad_proj, w_attn).astype(BF16)
    grad_w_output, attn_sum, grad_h_one = together(
        [
            Across(output_part, parts, False),
            Across(attn_part, parts, True),
            Scatter(grad_h_one_part, members),
        ],
        members,
        parts,
        3,
    )
    payload = jnp.concatenate(
        [attn_sum[:width, query_width:], attn_sum[width:].reshape(-1, 2 * HD)], 0
    )
    every = together([Gather(payload, members)], members, parts, 4)[0]
    every = every.reshape(members, payload.shape[0], 2 * HD)
    kv = every[:, :width].astype(F32).reshape(KV, share, width, 2 * HD).sum(1)
    kv = jnp.transpose(kv, (1, 0, 2))
    grad_w_key = kv[:, :, :HD].reshape(width, KV * HD)
    grad_w_value = kv[:, :, HD:].reshape(width, KV * HD)
    small_sum = every[:, width:].astype(F32).sum(0).reshape(-1)
    entry_count = tokens.size * parts * members
    at = 2 * width
    residual_rms = jnp.sqrt(small_sum[at + 2 * HD : at + 2 * HD + 1] / entry_count)

    grad_tokens = (grad_mid + norm_back(grad_h_one, normed_one, inv_one, attn_gain)).astype(BF16)
    output = (residual_mid + ffn_branch).astype(BF16)
    branch_rms = jnp.stack(
        [
            jnp.sqrt(jnp.mean(attn_branch * attn_branch, -1)),
            jnp.sqrt(jnp.mean(ffn_branch * ffn_branch, -1)),
        ]
    )
    return (
        output,
        grad_tokens,
        attn_sum[:width, :query_width].astype(F32),
        grad_w_key,
        grad_w_value,
        grad_w_output.astype(F32),
        grad_w_gate.astype(F32),
        grad_w_up.astype(F32),
        grad_w_down.astype(F32),
        small_sum[:width],
        small_sum[width:at],
        small_sum[at : at + HD],
        small_sum[at + HD : at + 2 * HD],
        residual_rms,
        branch_rms,
    )


def solution(mesh):
    row, whole, column = P(("dp", "mp"), None), P(), P(None, "mp")
    lead = P("mp", None)
    return jax.shard_map(
        per_device,
        mesh=mesh,
        in_specs=(row, P("dp"), P("dp"), column, whole, whole, lead, column, column, lead)
        + (whole,) * 4
        + (row,),
        out_specs=(row, row, column, whole, whole, lead, column, column, lead)
        + (whole,) * 5
        + (P(None, ("dp", "mp")),),
        check_vma=False,
    )
```

time: 1450 us -> 606 us (0.42)
  waiting for transfers between devices: 1060 us -> 0.04 us
  Pallas kernels: 0 us -> 406 us
  matrix products: 149 us -> 83.4 us
  local copies, waits for them, and re-layouts: 107 us -> 49.8 us
  blocking collectives: 44.9 us -> 0 us
    psum x2 -> x1, waiting for transfers between devices: 701 us -> 0.01 us  [per_device(): lax.psum((down_part, gate_part, up_part), 'dp')]
    pallas_call x0 -> x9, Pallas kernels: none -> 406 us  [the longest x7 377 us: together(): pl.pallas_call(kernel, out_shape=[o for s in steps for o, _ in s.outputs]...]
    reduce_scatter x4 -> x0, waiting for transfers between devices: 197 us -> none  [the longest x1 87 us: per_device(): lax.psum_scatter(matmul_right_t(grad_gate_up, w_ffn), 'mp', scatter_dimen...]
    all_gather x4 -> x1, waiting for transfers between devices: 161 us -> 0.01 us  [per_device(): grad_rows = lax.all_gather(out_grad_late, 'mp', axis=0, tiled=True)]
    dot_general x18 -> x4, matrix products: 84.1 us -> 23.6 us  [matmul(): return jnp.dot(left, right, preferred_element_type=F32)]
    psum x1 -> x0, blocking collectives: 44.9 us -> none  [per_device(): lax.psum((grad_w_key, grad_w_value, grad_attn_gain, grad_ffn_gain, grad_q...]
    dynamic_update_slice x6 -> x0, local copies, waits for them, and re-layouts: 33.6 us -> none  [the longest x4 21.9 us: per_device(): lax.scan(backward_block, (zero_rows, zero_rows), (query_blocks, grad_cont...]
    unnamed x125 -> x98, local copies, waits for them, and re-layouts: 39.9 us -> 36.1 us
  transfers between devices with their start and end apart: 10 -> 2, of which waited for: 10 -> 0; matrix products, arithmetic and copies ran while one was open for 7% -> 17% of each run, Pallas kernels for 0% -> 62%
where the time goes in v1:
time: 606 us; the launch traced here: 595 us
  Pallas kernels  406 us (67%)
  matrix products  83.4 us (14%)
  local copies, waits for them, and re-layouts  49.8 us (8%)
  other arithmetic  38 us (6%)
  between operations  17 us (3%)
    pallas_call x7, Pallas kernels, together(): pl.pallas_call(kernel, out_shape=[o for s in steps for o, _ in s.outputs]...  377 us
    unnamed x98, local copies, waits for them, and re-layouts  36.1 us
    dot_general x4, matrix products, matmul_right_t(): lax.dot_general(left, right, (((1,), (1,)), ((), ())), preferred_element_...  30.3 us
    dot_general x5, matrix products, matmul_left_t(): lax.dot_general(left, right, (((0,), (0,)), ((), ())), preferred_element_...  29.5 us
    dot_general x4, matrix products, matmul(): return jnp.dot(left, right, preferred_element_type=F32)  23.6 us
    pallas_call x1, Pallas kernels, attend_back(): pl.pallas_call(functools.partial(attend_back_kernel, heads), out_shape=(j...  17.7 us
  transfers between devices with their start and end apart: 2, of which 0 were waited for; matrix products, arithmetic and copies ran while one was open for 17% of the time, Pallas kernels for 62%

profile of v1, /device:TPU:10, one launch (start us, length us, event | category | flops | bytes accessed | tf_op | source)
XLA Modules:
  0.0 594.6 jit_solution(13808620172385257414)
XLA Ops:
  11.0 38.1 %shard_map.253 = bf16[1024,2048]{1,0:T(8,128)(2,1)S(1)} custom-call(bf16[128,2048]{1,0:T(8,128)(2,1)S(1)} %fusion.6.refs_0_), custom_call_target="tpu_custom_call" | custom-call | flops 1 | bytes 1 | tf_op jit(solution)/shard_map/pallas_call | solution.py:342
  54.9 5.2 fusion.14.proj_ref
  63.5 11.5 %shard_map.254 = (bf16[1024,256]{1,0:T(8,128)(2,1)S(1)}, f32[4,1,1024]{2,1,0:T(1,128)S(1)}) custom-call(f32[1024,384]{1,0:T(8,128)S(1)} %fusion.14.proj_ref, f32[1024,128]{1,0:T(8,128)S(1)} %copy-done.3, f32[1024,128]{1,0:T(8,128)S(1)} %copy.34.sin_ref, f32[1,384]{1,0:T(1,128)S(1)} %broadcast_in_dim.8.gain_ref, s32[1024,1]{1,0:T(8,128)S(1)} %copy-done.11), custom_call_target="tpu_custom_call" | custom-call | flops 1 | bytes 1 | tf_op jit(solution)/shard_map/pallas_call | solution.py:435
  77.1 57.5 %shard_map.255 = f32[128,2048]{1,0:T(8,128)S(1)} custom-call(bf16[1024,2048]{1,0:T(8,128)(2,1)S(1)} %convolution_convert_fusion.2.refs_0_), custom_call_target="tpu_custom_call" | custom-call | flops 1 | bytes 1 | tf_op jit(solution)/shard_map/pallas_call | solution.py:342
  135.1 35.5 %shard_map.256 = bf16[1024,2048]{1,0:T(8,128)(2,1)S(1)} custom-call(bf16[128,2048]{1,0:T(8,128)(2,1)S(1)} %multiply_convert_fusion.3.refs_0_), custom_call_target="tpu_custom_call" | custom-call | flops 1 | bytes 1 | tf_op jit(solution)/shard_map/pallas_call | solution.py:342
  171.1 3.2 copy-done.30
  175.0 3.4 copy-done.31
  178.4 11.1 %fusion.18 = f32[1024,2048]{1,0:T(8,128)} fusion(bf16[1024,2048]{1,0:T(8,128)(2,1)S(1)} %shard_map.256, bf16[2048,2048]{1,0:T(8,128)(2,1)S(1)} %constant_dynamic-update-slice_fusion), kind=kOutput, calls=%fused_computation.70 | convolution fusion | flops 8589934592 | bytes 20971520 | tf_op jit(solution)/shard_map/dot_general | solution.py:542
  189.4 12.0 %multiply_convert_fusion = (bf16[1024,1024]{1,0:T(8,128)(2,1)S(1)}, bf16[1024,1024]{1,0:T(8,128)(2,1)S(1)}, bf16[1024,1024]{1,0:T(8,128)(2,1)S(1)}) fusion(f32[1024,2048]{1,0:T(8,128)} %fusion.18, bf16[1024,2048]{1,0:T(8,128)(2,1)} %all-gather.2.cloned.1.call-done, bf16[1024,2048]{1,0:T(8,128)(2,1)} %param.23), kind=kOutput, calls=%fused_computation.2 | convolution fusion | flops 4310695936 | bytes 23068672 | tf_op jit(solution)/shard_map/dot_general | solution.py:550
  201.5 6.2 %convolution_convert_fusion.5 = bf16[2048,1024]{1,0:T(8,128)(2,1)} fusion(bf16[1024,2048]{1,0:T(8,128)(2,1)S(1)} %copy-done.7, bf16[1024,1024]{1,0:T(8,128)(2,1)S(1)} %get-tuple-element.72), kind=kOutput, calls=%fused_computation.12 | convolution fusion | flops 4297064448 | bytes 10485760 | tf_op jit(solution)/shard_map/dot_general | solution.py:546
  210.0 6.4 %convolution_convert_fusion.4 = bf16[2048,1024]{1,0:T(8,128)(2,1)} fusion(bf16[1024,2048]{1,0:T(8,128)(2,1)S(1)} %copy-done.7, bf16[1024,1024]{1,0:T(8,128)(2,1)S(1)} %get-tuple-element.71), kind=kOutput, calls=%fused_computation.11 | convolution fusion | flops 4297064448 | bytes 10485760 | tf_op jit(solution)/shard_map/dot_general | solution.py:546
  216.4 6.3 %convolution_convert_fusion.6 = bf16[1024,2048]{1,0:T(8,128)(2,1)} fusion(bf16[1024,1024]{1,0:T(8,128)(2,1)S(1)} %get-tuple-element.35, bf16[1024,2048]{1,0:T(8,128)(2,1)S(1)} %copy-done.43), kind=kOutput, calls=%fused_computation.13 | convolution fusion | flops 4297064448 | bytes 10485760 | tf_op jit(solution)/shard_map/dot_general | solution.py:546
  222.7 12.6 %convolution_convert_fusion.1.refs_0_ = bf16[1024,2048]{1,0:T(8,128)(2,1)S(1)} fusion(bf16[1024,2048]{1,0:T(8,128)(2,1)} %pad_maximum_fusion, bf16[2048,2048]{1,0:T(8,128)(2,1)} %copy-done.31), kind=kOutput, calls=%fused_computation.8 | convolution fusion | flops 8592031744 | bytes 16777216 | tf_op jit(solution)/shard_map/dot_general | solution.py:550
  235.3 45.0 %shard_map.257 = f32[128,2048]{1,0:T(8,128)S(1)} custom-call(bf16[1024,2048]{1,0:T(8,128)(2,1)S(1)} %convolution_convert_fusion.1.refs_0_), custom_call_target="tpu_custom_call" | custom-call | flops 1 | bytes 1 | tf_op jit(solution)/shard_map/pallas_call | solution.py:342
  280.7 6.0 %convolution_convert_fusion.3.refs_1_ = bf16[1024,2048]{1,0:T(8,128)(2,1)} fusion(bf16[1024,1024]{1,0:T(8,128)(2,1)S(1)} %copy-done.46, bf16[1024,2048]{1,0:T(8,128)(2,1)S(1)} %copy-done.42), kind=kOutput, calls=%fused_computation.10 | convolution fusion | flops 4297064448 | bytes 10485760 | tf_op jit(solution)/shard_map/dot_general | solution.py:542
  287.0 54.8 %shard_map.258 = (bf16[1024,2048]{1,0:T(8,128)(2,1)S(1)}, f32[128,2048]{1,0:T(8,128)S(1)}) custom-call(bf16[128,2048]{1,0:T(8,128)(2,1)S(1)} %fusion.13.refs_0_, bf16[1024,2048]{1,0:T(8,128)(2,1)} %convolution_convert_fusion.3.refs_1_), custom_call_target="tpu_custom_call" | custom-call | flops 1 | bytes 1 | tf_op jit(solution)/shard_map/pallas_call | solution.py:342
  345.4 17.7 %shard_map.259 = (bf16[1024,384]{1,0:T(8,128)(2,1)S(1)}, f32[1,384]{1,0:T(1,128)S(1)}) custom-call(f32[1024,384]{1,0:T(8,128)S(1)} %copy-done.2, f32[1024,128]{1,0:T(8,128)S(1)} %copy-done.4, f32[1024,128]{1,0:T(8,128)S(1)} %copy.34.sin_ref, f32[1,384]{1,0:T(1,128)S(1)} %broadcast_in_dim.8.gain_ref, s32[4,1,256]{2,1,0:T(1,128)S(1)} %bitcast.48, ...), custom_call_target="tpu_custom_call" | custom-call | flops 1 | bytes 1 | tf_op jit(solution)/shard_map/pallas_call | solution.py:530
  364.1 7.0 %fusion.16 = (bf16[2048,384]{1,0:T(8,128)(2,1)}, f32[2048]{0:T(1024)S(1)}) fusion(bf16[2048,64]{1,0:T(8,128)(2,1)} %copy-done.32, bf16[2048,64]{1,0:T(8,128)(2,1)} %copy-done.34, bf16[2048,256]{1,0:T(8,128)(2,1)} %param.17, bf16[1024,2048]{1,0:T(8,128)(2,1)} %copy-done.5, bf16[1024,384]{1,0:T(8,128)(2,1)} %copy-done.19), kind=kOutput, calls=%fused_computation.68 | convolution fusion | flops 1617688576 | bytes 8134656 | tf_op jit(solution)/shard_map/dot_general | solution.py:546
  371.9 2.7 pad_maximum_fusion.1.refs_1_
  374.7 3.7 convolution_convert_fusion.7.refs_0_
  378.4 4.4 convolution_convert_fusion.refs_2_
  382.7 105.8 %shard_map.260 = (bf16[256,2048]{1,0:T(8,128)(2,1)S(1)}, bf16[2112,384]{1,0:T(8,128)(2,1)S(1)}, f32[128,2048]{1,0:T(8,128)S(1)}) custom-call(bf16[256,2048]{1,0:T(8,128)(2,1)S(1)} %convolution_convert_fusion.7.refs_0_, bf16[2112,384]{1,0:T(8,128)(2,1)} %pad_maximum_fusion.1.refs_1_, bf16[1024,2048]{1,0:T(8,128)(2,1)} %convolution_convert_fusion.refs_2_), custom_call_target="tpu_custom_call" | custom-call | flops 1 | bytes 1 | tf_op jit(solution)/shard_map/pallas_call | solution.py:342
  491.8 40.6 %shard_map.261 = bf16[17920,128]{1,0:T(8,128)(2,1)S(1)} custom-call(bf16[2240,128]{1,0:T(8,128)(2,1)S(1)} %pad_maximum_fusion.3.refs_0_), custom_call_target="tpu_custom_call" | custom-call | flops 1 | bytes 1 | tf_op jit(solution)/shard_map/pallas_call | solution.py:342
  537.6 6.4 %copy.44 = bf16[8,2048,128]{1,2,0:T(8,128)(2,1)} copy(bf16[8,2048,128]{2,1,0:T(8,128)(2,1)} %slice.76) | data formatting | bytes 8388608
  544.0 3.2 convert_bitcast_fusion
  547.2 4.0 fusion.15
  551.2 5.3 copy.42
  556.6 5.4 copy.41
  563.7 3.6 multiply_reduce_fusion.1
  570.5 6.8 %convert_element_type.108 = f32[2048,1024]{1,0:T(8,128)} convert(bf16[2048,1024]{1,0:T(8,128)(2,1)} %get-tuple-element.66) | non-fusion elementwise | flops 2097152 | bytes 12582912 | tf_op jit(solution)/shard_map/convert_element_type | solution.py:705
  577.3 4.4 convert_element_type.109
  581.8 4.4 convert_element_type.110
  (150 shorter events, 37.4 us)
Async XLA Ops:
  7.2 67.8 %copy-start = (bf16[256,2048]{1,0:T(8,128)(2,1)S(1)}, bf16[256,2048]{1,0:T(8,128)(2,1)}, u32[]{:S(2)}) copy-start(bf16[256,2048]{1,0:T(8,128)(2,1)} %param.20) | copy-start | bytes 3145732
  7.2 44.0 %copy-start.40 = (f32[64]{0:T(128)S(1)}, f32[64]{0:T(128)}, u32[]{:S(2)}) copy-start(f32[64]{0:T(128)} %param.26) | copy-start | bytes 772
  7.2 44.1 %copy-start.41 = (f32[64]{0:T(128)S(1)}, f32[64]{0:T(128)}, u32[]{:S(2)}) copy-start(f32[64]{0:T(128)} %param.27) | copy-start | bytes 772
  7.2 44.2 %copy-start.17 = (s32[1024]{0:T(1024)S(1)}, s32[1024]{0:T(1024)}, u32[]{:S(2)}) copy-start(s32[1024]{0:T(1024)} %param.16) | copy-start | bytes 12292
  7.2 182.2 %all-gather.2.cloned.1.call-start = ((), (), s32[]{:S(2)}) async-start(), calls=%async_computation | async-start | bytes 4718592 | tf_op jit(solution)/shard_map/all_gather | solution.py:606
  51.2 519.4 %all-reduce.4.cloned.1.call-start = ((), (), s32[]{:S(2)}) async-start(), calls=%async_computation.1 | async-start | bytes 25165824 | tf_op jit(solution)/shard_map/psum | solution.py:633
  54.9 5.3 copy-start.32
  54.9 5.3 copy-start.34
  60.2 16.1 %copy-start.1 = (f32[1024,384]{1,0:T(8,128)}, f32[1024,384]{1,0:T(8,128)S(1)}, u32[]{:S(2)}) copy-start(f32[1024,384]{1,0:T(8,128)S(1)} %fusion.14.proj_ref) | copy-start | bytes 4718596
  77.1 57.5 %copy-start.23 = (bf16[128,2048]{1,0:T(8,128)(2,1)S(1)}, bf16[128,2048]{1,0:T(8,128)(2,1)}, u32[]{:S(2)}) copy-start(bf16[128,2048]{1,0:T(8,128)(2,1)} %param.15) | copy-start | bytes 1572868
  77.1 57.8 %copy-start.36 = (f32[2048]{0:T(1024)S(1)}, f32[2048]{0:T(1024)}, u32[]{:S(2)}) copy-start(f32[2048]{0:T(1024)} %param.25) | copy-start | bytes 24580
  134.6 36.0 %copy-start.29 = (bf16[2048,1024]{1,0:T(8,128)(2,1)S(1)}, bf16[2048,1024]{1,0:T(8,128)(2,1)}, u32[]{:S(2)}) copy-start(bf16[2048,1024]{1,0:T(8,128)(2,1)} %param.21) | copy-start | bytes 12582916
  134.9 36.2 %copy-start.21 = (f32[128,2048]{1,0:T(8,128)}, f32[128,2048]{1,0:T(8,128)S(1)}, u32[]{:S(2)}) copy-start(f32[128,2048]{1,0:T(8,128)S(1)} %get-tuple-element.70) | copy-start | bytes 3145732
  170.6 4.4 copy-start.6
  170.6 3.7 copy-start.30
  189.4 12.0 %copy-start.7 = (bf16[1024,2048]{1,0:T(8,128)(2,1)S(1)}, bf16[1024,2048]{1,0:T(8,128)(2,1)}, u32[]{:S(2)}) copy-start(bf16[1024,2048]{1,0:T(8,128)(2,1)} %copy-done.6) | copy-start | bytes 12582916
  201.5 14.9 %copy-start.45 = (bf16[1024,1024]{1,0:T(8,128)(2,1)}, bf16[1024,1024]{1,0:T(8,128)(2,1)S(1)}, u32[]{:S(2)}) copy-start(bf16[1024,1024]{1,0:T(8,128)(2,1)S(1)} %get-tuple-element.35) | copy-start | bytes 6291460
  210.0 6.4 %copy-start.43 = (bf16[1024,2048]{1,0:T(8,128)(2,1)S(1)}, bf16[1024,2048]{1,0:T(8,128)(2,1)}, u32[]{:S(2)}) copy-start(bf16[1024,2048]{1,0:T(8,128)(2,1)} %all-gather.2.cloned.1.call-done) | copy-start | bytes 12582916
  235.3 45.0 %copy-start.22 = (f32[128,2048]{1,0:T(8,128)S(1)}, f32[128,2048]{1,0:T(8,128)}, u32[]{:S(2)}) copy-start(f32[128,2048]{1,0:T(8,128)} %copy-done.21) | copy-start | bytes 3145732
  235.3 45.4 %copy-start.42 = (bf16[1024,2048]{1,0:T(8,128)(2,1)S(1)}, bf16[1024,2048]{1,0:T(8,128)(2,1)}, u32[]{:S(2)}) copy-start(bf16[1024,2048]{1,0:T(8,128)(2,1)} %param.23) | copy-start | bytes 12582916
  235.3 45.4 %copy-start.46 = (bf16[1024,1024]{1,0:T(8,128)(2,1)S(1)}, bf16[1024,1024]{1,0:T(8,128)(2,1)}, u32[]{:S(2)}) copy-start(bf16[1024,1024]{1,0:T(8,128)(2,1)} %copy-done.45) | copy-start | bytes 6291460
  280.7 6.0 %copy-start.25 = (bf16[128,2048]{1,0:T(8,128)(2,1)S(1)}, bf16[128,2048]{1,0:T(8,128)(2,1)}, u32[]{:S(2)}) copy-start(bf16[128,2048]{1,0:T(8,128)(2,1)} %param.28) | copy-start | bytes 1572868
  341.8 21.3 %copy-start.18 = (bf16[1024,2048]{1,0:T(8,128)(2,1)}, bf16[1024,2048]{1,0:T(8,128)(2,1)S(1)}, u32[]{:S(2)}) copy-start(bf16[1024,2048]{1,0:T(8,128)(2,1)S(1)} %get-tuple-element.37) | copy-start | bytes 12582916
  364.1 7.0 %copy-start.37 = (f32[2048]{0:T(1024)S(1)}, f32[2048]{0:T(1024)}, u32[]{:S(2)}) copy-start(f32[2048]{0:T(1024)} %param.24) | copy-start | bytes 24580
  374.7 3.7 copy-start.44
  491.8 40.7 %copy-start.15 = (bf16[256,2048]{1,0:T(8,128)(2,1)S(1)}, bf16[256,2048]{1,0:T(8,128)(2,1)}, u32[]{:S(2)}) copy-start(bf16[256,2048]{1,0:T(8,128)(2,1)} %copy-done.14) | copy-start | bytes 3145732
  556.6 5.4 copy-start.24
  556.6 5.4 copy-start.39
  556.6 7.1 %copy-start.26 = (bf16[128,2048]{1,0:T(8,128)(2,1)S(1)}, bf16[128,2048]{1,0:T(8,128)(2,1)}, u32[]{:S(2)}) copy-start(bf16[128,2048]{1,0:T(8,128)(2,1)} %param.28) | copy-start | bytes 1572868
  562.0 7.1 %copy-start.13 = (bf16[2112,384]{1,0:T(8,128)(2,1)S(1)}, bf16[2112,384]{1,0:T(8,128)(2,1)}, u32[]{:S(2)}) copy-start(bf16[2112,384]{1,0:T(8,128)(2,1)} %copy-done.12) | copy-start | bytes 4866052
  570.5 6.8 %copy-start.28 = (bf16[2048,1024]{1,0:T(8,128)(2,1)S(1)}, bf16[2048,1024]{1,0:T(8,128)(2,1)}, u32[]{:S(2)}) copy-start(bf16[2048,1024]{1,0:T(8,128)(2,1)} %get-tuple-element.67) | copy-start | bytes 12582916
  577.3 4.4 copy-start.27
  (17 other events, 34.5 us)
Sparse Core Ops, SparseCore 0:
  51.3 61.2 all-gather.1
  222.8 280.9 all-reduce.3

commit v2 on v1

--- a/solution.py
+++ b/solution.py
@@ -152,22 +152,153 @@
         lax.fori_loop(0, length, drain, 0)
 
 
+class GatherFfn:
+    line, across = True, False
+
+    def __init__(self, x, grad_rows, w_gate, w_up, w_down, members):
+        length, (rows, width), units = members // 2, x.shape, w_gate.shape[1]
+        total = members * rows
+        sems = pltpu.SemaphoreType.DMA((length,))
+        self.units = units
+        self.inputs = [(v, ANY) for v in (x, grad_rows, w_gate, w_up, w_down)]
+        self.outputs = [
+            (jax.ShapeDtypeStruct((total, width), BF16), VMEM),
+            (jax.ShapeDtypeStruct((total, units), BF16), VMEM),
+            (jax.ShapeDtypeStruct((total, 2 * units), BF16), VMEM),
+        ]
+        self.scratch = [pltpu.VMEM(v.shape, v.dtype) for v in (grad_rows, w_gate, w_up, w_down)]
+        self.scratch += [pltpu.SemaphoreType.DMA((5,)), sems, sems, sems, pltpu.SemaphoreType.DMA((members,))]
+
+    def run(self, here, x_ref, gr_ref, wg_ref, wu_ref, wd_ref, o_ref, hid_ref, ggu_ref,
+            gr, wg, wu, wd, load_sem, left_sem, right_sem, side_sem, recv_sem):
+        pos, core, length = here.pos, here.core, here.length
+        rows, units, wide = x_ref.shape[0], self.units, 256
+
+        def block(p, c):
+            return o_ref.at[pl.ds(pl.multiple_of((p * 2 + c) * rows, rows), rows)]
+
+        def send(src, p, sem, to_p, to_c):
+            remote(src, block(p, core), sem.at[p], recv_sem.at[p * 2 + core], here.at(to_p, to_c)).start()
+
+        def arrived(p, c):
+            pltpu.make_async_copy(x_ref, block(p, c), recv_sem.at[p * 2 + c]).wait()
+
+        def sent(sem, p):
+            pltpu.make_async_copy(x_ref, block(pos, core), sem.at[p]).wait()
+
+        @pl.when(pos > 0)
+        def _():
+            send(x_ref, pos, left_sem, pos - 1, core)
+
+        @pl.when(pos < here.last)
+        def _():
+            send(x_ref, pos, right_sem, pos + 1, core)
+
+        send(x_ref, pos, side_sem, pos, 1 - core)
+        pairs = [(x_ref, block(pos, core)), (wg_ref, wg), (wu_ref, wu), (gr_ref, gr), (wd_ref, wd)]
+        loads = [pltpu.make_async_copy(a, b, load_sem.at[i]) for i, (a, b) in enumerate(pairs)]
+        for load in loads:
+            load.start()
+        yield
+        for load in loads:
+            load.wait()
+
+        def use(p):
+            at = pl.ds(pl.multiple_of(p * 2 * rows, 2 * rows), 2 * rows)
+
+            def body(c, carry):
+                cols = pl.ds(pl.multiple_of(c * wide, wide), wide)
+                gate = dot_nn(o_ref[at], wg[:, cols])
+                up = dot_nn(o_ref[at], wu[:, cols])
+                back = dot_nt(gr[at], wd[cols])
+                sigma = 1.0 / (1.0 + jnp.exp(-gate))
+                silu = gate * sigma
+                hid_ref[at, cols] = (silu * up).astype(BF16)
+                ggu_ref[at, cols] = (back * up * sigma * (1.0 + gate * (1.0 - sigma))).astype(BF16)
+                ggu_ref[at, pl.ds(pl.multiple_of(units + c * wide, wide), wide)] = (back * silu).astype(BF16)
+                return carry
+
+            lax.fori_loop(0, units // wide, body, 0)
+
+        def hop(step, carry):
+            right, left = pos + step, pos - step
+
+            @pl.when((step > 0) & (right < length))
+            def _():
+                arrived(right, core)
+
+                @pl.when(pos > 0)
+                def _():
+                    send(block(right, core), right, left_sem, pos - 1, core)
+
+                send(block(right, core), right, side_sem, pos, 1 - core)
+
+            @pl.when((step > 0) & (left >= 0))
+            def _():
+                arrived(left, core)
+
+                @pl.when(pos < here.last)
+                def _():
+                    send(block(left, core), left, right_sem, pos + 1, core)
+
+                send(block(left, core), left, side_sem, pos, 1 - core)
+
+            def side(k, c):
+                p = pos + (1 - 2 * k) * step
+
+                @pl.when((p >= 0) & (p < length) & (step >= k))
+                def _():
+                    arrived(p, 1 - core)
+                    use(p)
+
+                return c
+
+            lax.fori_loop(0, 2, side, 0)
+            return carry
+
+        lax.fori_loop(0, length, hop, 0)
+
+        def drain(p, carry):
+            sent(side_sem, p)
+
+            @pl.when((p >= pos) & (pos > 0))
+            def _():
+                sent(left_sem, p)
+
+            @pl.when((p <= pos) & (pos < here.last))
+            def _():
+                sent(right_sem, p)
+
+            return carry
+
+        lax.fori_loop(0, length, drain, 0)
+
+
 class Scatter:
     line, across = True, False
 
-    def __init__(self, parts, members):
+    def __init__(self, terms, members):
         length = members // 2
-        rows, width = parts.shape[0] // members, parts.shape[1]
-        self.rows = rows
-        self.inputs = [(parts, VMEM)]
+        left, right, turned = terms[0]
+        rows, width = left.shape[0] // members, right.shape[0 if turned else 1]
+        self.rows, self.width, self.turned = rows, width, [t for _, _, t in terms]
+        self.inputs = [(x, VMEM) for x, _, _ in terms] + [(w, ANY) for _, w, _ in terms]
         self.outputs = [(jax.ShapeDtypeStruct((rows, width), F32), VMEM)]
-        self.scratch = [pltpu.VMEM((length, rows, width), parts.dtype)] * 5
+        self.scratch = [pltpu.VMEM(w.shape, w.dtype) for _, w, _ in terms]
+        self.scratch += [pltpu.SemaphoreType.DMA((len(terms),)), pltpu.VMEM((members * rows, width), BF16)]
+        self.scratch += [pltpu.VMEM((length, rows, width), BF16)] * 5
         self.scratch += [pltpu.SemaphoreType.DMA((length,))] * 6
 
-    def run(self, here, p_ref, o_ref, side_buf, left_in, right_in, left_out, right_out,
-            side_send, side_recv, right_send, right_recv, left_send, left_recv):
+    def run(self, here, *refs):
+        n = len(self.turned)
+        lefts, rights, (o_ref,), helds = refs[:n], refs[n : 2 * n], refs[2 * n : 2 * n + 1], refs[2 * n + 1 : 3 * n + 1]
+        (load_sem, p_ref, side_buf, left_in, right_in, left_out, right_out,
+         side_send, side_recv, right_send, right_recv, left_send, left_recv) = refs[3 * n + 1 :]
         pos, core, length, last = here.pos, here.core, here.length, here.last
-        rows, tile = self.rows, 32
+        rows, tile, wide = self.rows, 32, 256
+        loads = [pltpu.make_async_copy(w, h, load_sem.at[i]) for i, (w, h) in enumerate(zip(rights, helds))]
+        for load in loads:
+            load.start()
 
         def side_copy(p):
             block = p_ref.at[pl.ds(pl.multiple_of((p * 2 + 1 - core) * rows, rows), rows)]
@@ -178,19 +309,20 @@
                 return remote(right_out.at[p], right_in.at[p], right_send.at[p], right_recv.at[p], here.at(pos + 1, core))
             return remote(left_out.at[p], left_in.at[p], left_send.at[p], left_recv.at[p], here.at(pos - 1, core))
 
-        def push(i, carry):
-            @pl.when(last - i > pos)
-            def _():
-                side_copy(last - i).start()
-
-            @pl.when(i < pos)
-            def _():
-                side_copy(i).start()
-
-            return carry
-
-        lax.fori_loop(0, length, push, 0)
-        side_copy(pos).start()
+        def multiply(p):
+            at = pl.ds(pl.multiple_of(p * 2 * rows, 2 * rows), 2 * rows)
+
+            def body(c, carry):
+                cols = pl.ds(pl.multiple_of(c * wide, wide), wide)
+                total = None
+                for left, held, turned in zip(lefts, helds, self.turned):
+                    part = dot_nt(left[at], held[cols]) if turned else dot_nn(left[at], held[:, cols])
+                    total = part if total is None else total + part
+                p_ref[at, cols] = total.astype(BF16)
+                return carry
+
+            lax.fori_loop(0, self.width // wide, body, 0)
+            side_copy(p).start()
 
         def add(p, incoming, out):
             def body(r, carry):
@@ -221,7 +353,21 @@
 
             line_copy(p, right).start()
 
-        def slot(t):
+        for load in loads:
+            load.wait()
+        for t in range(last):
+
+            def side(k, carry):
+                p = k * t + (1 - k) * (last - t)
+
+                @pl.when((1 - 2 * k) * (p - pos) > 0)
+                def _():
+                    multiply(p)
+
+                return carry
+
+            lax.fori_loop(0, 2, side, 0)
+            yield
             right_p, left_p = last - t + pos, t - (last - pos)
 
             @pl.when(t >= pos)
@@ -232,9 +378,7 @@
             def _():
                 move(left_p, False, pos == last, left_in, left_out)
 
-        for t in range(last):
-            yield
-            slot(t)
+        multiply(pos)
         yield
         side_copy(pos).wait_recv()
 
@@ -606,39 +750,32 @@
     grad_rows = lax.all_gather(out_grad_late, "mp", axis=0, tiled=True)
     projected = matmul(rows_one, w_attn)
     context, lse = attend(projected, cosine, sine, gain, positions, heads)
-    attn_part = matmul(context, w_output).astype(BF16)
-    attn_branch = together([Scatter(attn_part, members)], members, parts, 1)[0]
+    attn_branch = together([Scatter([(context, w_output, False)], members)], members, parts, 1)[0]
     residual_mid = tokens_f + attn_branch
     inv_two = lax.rsqrt(jnp.mean(residual_mid * residual_mid, -1, keepdims=True) + EPSILON)
     normed_two = residual_mid * inv_two
     h_two = (normed_two * ffn_gain).astype(BF16)
-    w_ffn = jnp.concatenate([w_gate, w_up], 1)
-    rows_two = together([Gather(h_two, members)], members, parts, 0)[0]
-    gate_up = matmul(rows_two, w_ffn)
-    gate = gate_up[:, :ffn_width]
-    up = gate_up[:, ffn_width:]
-    sigma = jax.nn.sigmoid(gate)
-    silu_gate = gate * sigma
-    hidden = (silu_gate * up).astype(BF16)
-    grad_hidden = matmul_right_t(grad_rows, w_down)
-    grad_gate = (grad_hidden * up * sigma * (1.0 + gate * (1.0 - sigma))).astype(BF16)
-    grad_up = (grad_hidden * silu_gate).astype(BF16)
-    grad_gate_up = jnp.concatenate([grad_gate, grad_up], 1)
-    down_part = matmul_left_t(hidden, grad_rows).astype(BF16)
-    gate_part = matmul_left_t(rows_two, grad_gate).astype(BF16)
-    up_part = matmul_left_t(rows_two, grad_up).astype(BF16)
-    down_part, gate_part, up_part, grad_gate_up, hidden = lax.optimization_barrier(
-        (down_part, gate_part, up_part, grad_gate_up, hidden)
-    )
-    grad_w_down, grad_w_gate, grad_w_up = lax.psum((down_part, gate_part, up_part), "dp")
-
-    grad_h_two_part = matmul_right_t(grad_gate_up, w_ffn).astype(BF16)
-    grad_h_two = together([Scatter(grad_h_two_part, members)], members, parts, 1)[0]
+    rows_two, hidden, grad_gate_up = together(
+        [GatherFfn(h_two, grad_rows, w_gate, w_up, w_down, members)], members, parts, 5, 58
+    )
+    ffn_parts = (
+        matmul_left_t(rows_two, grad_gate_up).astype(BF16),
+        matmul_left_t(hidden, grad_rows).astype(BF16),
+    )
+    ffn_parts, grad_gate_up, hidden = lax.optimization_barrier((ffn_parts, grad_gate_up, hidden))
+    grad_w_ffn, grad_w_down = lax.psum(ffn_parts, "dp")
+
+    grad_gate, grad_up = grad_gate_up[:, :ffn_width], grad_gate_up[:, ffn_width:]
+    grad_h_two = together(
+        [Scatter([(grad_gate, w_gate, True), (grad_up, w_up, True)], members)], members, parts, 6, 58
+    )[0]
     grad_ffn_gain = jnp.sum(grad_h_two * normed_two, 0)
     grad_mid = out_grad.astype(F32) + norm_back(grad_h_two, normed_two, inv_two, ffn_gain)
-    ffn_part = matmul(hidden, w_down).astype(BF16)
     grad_attn_rows, ffn_branch = together(
-        [Gather(grad_mid.astype(BF16), members), Scatter(ffn_part, members)], members, parts, 2
+        [Gather(grad_mid.astype(BF16), members), Scatter([(hidden, w_down, False)], members)],
+        members,
+        parts,
+        2,
     )
     grad_context = matmul_right_t(grad_attn_rows, w_output).astype(BF16)
     grad_proj, gain_sums = attend_back(
@@ -662,12 +799,11 @@
     extra = -(-small.shape[0] // (unit * columns)) * unit
     small_rows = jnp.pad(small, (0, extra * columns - small.shape[0])).reshape(extra, columns)
     attn_part = jnp.concatenate([grad_w_attn, small_rows], 0).astype(BF16)
-    grad_h_one_part = matmul_right_t(grad_proj, w_attn).astype(BF16)
     grad_w_output, attn_sum, grad_h_one = together(
         [
             Across(output_part, parts, False),
             Across(attn_part, parts, True),
-            Scatter(grad_h_one_part, members),
+            Scatter([(grad_proj, w_attn, True)], members),
         ],
         members,
         parts,
@@ -702,8 +838,8 @@
         grad_w_key,
         grad_w_value,
         grad_w_output.astype(F32),
-        grad_w_gate.astype(F32),
-        grad_w_up.astype(F32),
+        grad_w_ffn[:, :ffn_width].astype(F32),
+        grad_w_ffn[:, ffn_width:].astype(F32),
         grad_w_down.astype(F32),
         small_sum[:width],
         small_sum[width:at],

time: 606 us -> 580 us (0.957)
  the two profiles are of different devices: /device:TPU:10 before, /device:TPU:0 now
where the time goes in v2:
time: 580 us; the launch traced here: 573 us
  Pallas kernels  433 us (75%)
  local copies, waits for them, and re-layouts  47.7 us (8%)
  other arithmetic  39.5 us (7%)
  matrix products  36.5 us (6%)
  between operations  16.8 us (3%)
    pallas_call x7, Pallas kernels, together(): pl.pallas_call(kernel, out_shape=[o for s in steps for o, _ in s.outputs]...  403 us
    dot_general x4, matrix products, matmul_left_t(): lax.dot_general(left, right, (((0,), (0,)), ((), ())), preferred_element_...  30.2 us
    unnamed x73, local copies, waits for them, and re-layouts  27.2 us
    pallas_call x1, Pallas kernels, attend_back(): pl.pallas_call(functools.partial(attend_back_kernel, heads), out_shape=(j...  17.8 us
    convert_element_type x1, other arithmetic, per_device(): grad_w_ffn[:, ffn_width:].astype(F32)  11.8 us
    pallas_call x1, Pallas kernels, attend(): pl.pallas_call(functools.partial(attend_kernel, heads), out_shape=(jax.Sh...  11.6 us
  transfers between devices with their start and end apart: 2, of which 0 were waited for; matrix products, arithmetic and copies ran while one was open for 13% of the time, Pallas kernels for 60%

profile of v2, /device:TPU:0, one launch (start us, length us, event | category | flops | bytes accessed | tf_op | source)
XLA Modules:
  0.0 573.4 jit_solution(10894392023445217345)
XLA Ops:
  7.3 1.9 fusion.3
  10.4 43.1 %shard_map.253 = bf16[1024,2048]{1,0:T(8,128)(2,1)S(1)} custom-call(bf16[128,2048]{1,0:T(8,128)(2,1)S(1)} %fusion.5.refs_0_), custom_call_target="tpu_custom_call" | custom-call | flops 1 | bytes 1 | tf_op jit(solution)/shard_map/pallas_call | solution.py:486
  53.6 2.0 copy-done.4
  58.5 1.7 constant_dynamic-slice_fusion
  61.1 2.3 fusion.17.proj_ref
  67.6 11.6 %shard_map.254 = (bf16[1024,256]{1,0:T(8,128)(2,1)S(1)}, f32[4,1,1024]{2,1,0:T(1,128)S(1)}) custom-call(f32[1024,384]{1,0:T(8,128)S(1)} %fusion.17.proj_ref, f32[1024,128]{1,0:T(8,128)S(1)} %copy-done.2, f32[1024,128]{1,0:T(8,128)S(1)} %copy-done, f32[1,384]{1,0:T(1,128)S(1)} %broadcast_in_dim.8.gain_ref, s32[1024,1]{1,0:T(8,128)S(1)} %copy-done.6), custom_call_target="tpu_custom_call" | custom-call | flops 1 | bytes 1 | tf_op jit(solution)/shard_map/pallas_call | solution.py:579
  80.6 54.7 %shard_map.255 = f32[128,2048]{1,0:T(8,128)S(1)} custom-call(bf16[1024,256]{1,0:T(8,128)(2,1)S(1)} %get-tuple-element.34.refs_0_.ctx_ref, bf16[256,2048]{1,0:T(8,128)(2,1)S(1)} %copy-done.14), custom_call_target="tpu_custom_call" | custom-call | flops 1 | bytes 1 | tf_op jit(solution)/shard_map/pallas_call | solution.py:486
  137.6 47.4 %shard_map.256 = (bf16[1024,2048]{1,0:T(8,128)(2,1)}, bf16[1024,1024]{1,0:T(8,128)(2,1)}, bf16[1024,2048]{1,0:T(8,128)(2,1)}) custom-call(bf16[128,2048]{1,0:T(8,128)(2,1)} %multiply_convert_fusion.refs_0_, bf16[1024,2048]{1,0:T(8,128)(2,1)} %all-gather.2.cloned.1.call-done.refs_1_, bf16[2048,1024]{1,0:T(8,128)(2,1)} %refs_2_.4, bf16[2048,1024]{1,0:T(8,128)(2,1)} %refs_3_.3, ...), custom_call_target="tpu_custom_call" | custom-call | flops 1 | bytes 1 | tf_op jit(solution)/shard_map/pallas_call | solution.py:486
  185.0 14.2 %convolution_convert_fusion = bf16[2048,2048]{1,0:T(8,128)(2,1)} fusion(bf16[1024,2048]{1,0:T(8,128)(2,1)} %get-tuple-element.36, bf16[1024,2048]{1,0:T(8,128)(2,1)} %get-tuple-element.39), kind=kOutput, calls=%fused_computation.1 | convolution fusion | flops 8594128896 | bytes 16777216 | tf_op jit(solution)/shard_map/dot_general | solution.py:690
  199.2 6.2 %convolution_convert_fusion.1 = bf16[1024,2048]{1,0:T(8,128)(2,1)} fusion(bf16[1024,1024]{1,0:T(8,128)(2,1)S(1)} %copy-done.7, bf16[1024,2048]{1,0:T(8,128)(2,1)S(1)} %copy-done.27), kind=kOutput, calls=%fused_computation.4 | convolution fusion | flops 4297064448 | bytes 10485760 | tf_op jit(solution)/shard_map/dot_general | solution.py:690
  205.4 4.7 fusion.14
  210.1 53.7 %shard_map.257 = f32[128,2048]{1,0:T(8,128)} custom-call(bf16[1024,1024]{1,0:T(8,128)(2,1)} %get-tuple-element.79.refs_0_, bf16[1024,1024]{1,0:T(8,128)(2,1)} %get-tuple-element.78.refs_1_, bf16[2048,1024]{1,0:T(8,128)(2,1)} %refs_2_.4, bf16[2048,1024]{1,0:T(8,128)(2,1)} %refs_3_.3), custom_call_target="tpu_custom_call" | custom-call | flops 1 | bytes 1 | tf_op jit(solution)/shard_map/pallas_call | solution.py:486
  263.8 1.7 multiply_reduce_fusion.3
  265.6 1.8 fusion.12.refs_0_
  267.4 52.3 %shard_map.258 = (bf16[1024,2048]{1,0:T(8,128)(2,1)}, f32[128,2048]{1,0:T(8,128)S(1)}) custom-call(bf16[128,2048]{1,0:T(8,128)(2,1)S(1)} %fusion.12.refs_0_, bf16[1024,1024]{1,0:T(8,128)(2,1)S(1)} %copy-done.8, bf16[1024,2048]{1,0:T(8,128)(2,1)} %refs_2_.5), custom_call_target="tpu_custom_call" | custom-call | flops 1 | bytes 1 | tf_op jit(solution)/shard_map/pallas_call | solution.py:486
  319.7 4.0 convolution_convert_fusion.3.grad_ref
  323.8 17.8 %shard_map.259 = (bf16[1024,384]{1,0:T(8,128)(2,1)S(1)}, f32[1,384]{1,0:T(1,128)S(1)}) custom-call(f32[1024,384]{1,0:T(8,128)S(1)} %fusion.17.proj_ref, f32[1024,128]{1,0:T(8,128)S(1)} %copy-done.3, f32[1024,128]{1,0:T(8,128)S(1)} %copy-done.1, f32[1,384]{1,0:T(1,128)S(1)} %broadcast_in_dim.8.gain_ref, s32[4,1,256]{2,1,0:T(1,128)S(1)} %bitcast.36, ...), custom_call_target="tpu_custom_call" | custom-call | flops 1 | bytes 1 | tf_op jit(solution)/shard_map/pallas_call | solution.py:674
  342.6 6.1 %fusion.15 = (bf16[2048,384]{1,0:T(8,128)(2,1)}, f32[2048]{0:T(1024)S(1)}) fusion(bf16[2048,384]{1,0:T(8,128)(2,1)S(1)} %pad_maximum_fusion.1.refs_3_, bf16[1024,2048]{1,0:T(8,128)(2,1)} %copy-done.4, bf16[1024,384]{1,0:T(8,128)(2,1)} %copy-done.18), kind=kOutput, calls=%fused_computation.57 | convolution fusion | flops 1613756416 | bytes 8134656 | tf_op jit(solution)/shard_map/dot_general | solution.py:690
  349.6 3.7 convolution_convert_fusion.2.refs_0_
  354.6 107.8 %shard_map.260 = (bf16[256,2048]{1,0:T(8,128)(2,1)S(1)}, bf16[2112,384]{1,0:T(8,128)(2,1)}, f32[128,2048]{1,0:T(8,128)S(1)}) custom-call(bf16[256,2048]{1,0:T(8,128)(2,1)S(1)} %convolution_convert_fusion.2.refs_0_, bf16[2112,384]{1,0:T(8,128)(2,1)} %pad_maximum_fusion.refs_1_, bf16[1024,384]{1,0:T(8,128)(2,1)S(1)} %copy-done.19, ...), custom_call_target="tpu_custom_call" | custom-call | flops 1 | bytes 1 | tf_op jit(solution)/shard_map/pallas_call | solution.py:486
  465.4 44.4 %shard_map.261 = bf16[17920,128]{1,0:T(8,128)(2,1)S(1)} custom-call(bf16[2240,128]{1,0:T(8,128)(2,1)S(1)} %pad_maximum_fusion.2.refs_0_), custom_call_target="tpu_custom_call" | custom-call | flops 1 | bytes 1 | tf_op jit(solution)/shard_map/pallas_call | solution.py:486
  509.8 1.6 convert_element_type.75
  511.4 2.3 slice.82
  514.9 6.4 %copy.39 = bf16[8,2048,128]{1,2,0:T(8,128)(2,1)} copy(bf16[8,2048,128]{2,1,0:T(8,128)(2,1)} %slice.82) | data formatting | bytes 8388608
  521.4 3.2 convert_bitcast_fusion
  524.6 4.0 fusion.13
  528.6 5.3 copy.38
  533.9 5.5 copy.37
  539.8 3.5 multiply_reduce_fusion.1
  545.1 1.5 slice_convert_fusion.2
  546.6 6.7 %convert_element_type.78 = f32[1024,2048]{1,0:T(8,128)} convert(bf16[1024,2048]{1,0:T(8,128)(2,1)} %get-tuple-element.71) | non-fusion elementwise | flops 2097152 | bytes 12582912 | tf_op jit(solution)/shard_map/convert_element_type | solution.py:843
  553.2 11.8 %slice_convert_fusion = (f32[2048,1024]{1,0:T(8,128)}, f32[2048,1024]{1,0:T(8,128)}) fusion(bf16[2048,2048]{1,0:T(8,128)(2,1)} %get-tuple-element.70), kind=kLoop, calls=%fused_computation.2 | loop fusion | flops 4194304 | bytes 25165824 | tf_op jit(solution)/shard_map/convert_element_type | solution.py:842
  (117 shorter events, 21.7 us)
Async XLA Ops:
  7.2 48.5 %copy-start.33 = (f32[64]{0:T(128)S(1)}, f32[64]{0:T(128)}, u32[]{:S(2)}) copy-start(f32[64]{0:T(128)} %param.26) | copy-start | bytes 772
  7.2 48.6 %copy-start.34 = (f32[64]{0:T(128)S(1)}, f32[64]{0:T(128)}, u32[]{:S(2)}) copy-start(f32[64]{0:T(128)} %param.27) | copy-start | bytes 772
  7.2 48.7 %copy-start.20 = (s32[1024]{0:T(1024)S(1)}, s32[1024]{0:T(1024)}, u32[]{:S(2)}) copy-start(s32[1024]{0:T(1024)} %param.16) | copy-start | bytes 12292
  7.2 130.3 %all-gather.2.cloned.1.call-start = ((), (), s32[]{:S(2)}) async-start(), calls=%async_computation | async-start | bytes 4718592 | tf_op jit(solution)/shard_map/all_gather | solution.py:750
  53.6 2.0 copy-start.4
  55.6 4.7 copy-start.30
  55.6 491.0 %all-reduce.4.cloned.1.call-start = ((), (), s32[]{:S(2)}) async-start(), calls=%async_computation.1 | async-start | bytes 25165824 | tf_op jit(solution)/shard_map/psum | solution.py:766
  58.5 2.6 copy-start.5
  64.4 1.0 copy-start
  67.6 67.8 %copy-start.23 = (bf16[128,2048]{1,0:T(8,128)(2,1)S(1)}, bf16[128,2048]{1,0:T(8,128)(2,1)}, u32[]{:S(2)}) copy-start(bf16[128,2048]{1,0:T(8,128)(2,1)} %param.15) | copy-start | bytes 1572868
  67.6 69.0 %copy-start.31 = (f32[2048]{0:T(1024)S(1)}, f32[2048]{0:T(1024)}, u32[]{:S(2)}) copy-start(f32[2048]{0:T(1024)} %param.25) | copy-start | bytes 24580
  79.2 56.4 %copy-start.9 = (bf16[1024,256]{1,0:T(8,128)(2,1)}, bf16[1024,256]{1,0:T(8,128)(2,1)S(1)}, u32[]{:S(2)}) copy-start(bf16[1024,256]{1,0:T(8,128)(2,1)S(1)} %get-tuple-element.34.refs_0_.ctx_ref) | copy-start | bytes 1572868
  79.2 1.4 copy-start.14
  185.0 14.2 %copy-start.7 = (bf16[1024,1024]{1,0:T(8,128)(2,1)S(1)}, bf16[1024,1024]{1,0:T(8,128)(2,1)}, u32[]{:S(2)}) copy-start(bf16[1024,1024]{1,0:T(8,128)(2,1)} %get-tuple-element.40.refs_1_) | copy-start | bytes 6291460
  185.0 14.2 %copy-start.27 = (bf16[1024,2048]{1,0:T(8,128)(2,1)S(1)}, bf16[1024,2048]{1,0:T(8,128)(2,1)}, u32[]{:S(2)}) copy-start(bf16[1024,2048]{1,0:T(8,128)(2,1)} %all-gather.2.cloned.1.call-done.refs_1_) | copy-start | bytes 12582916
  210.1 53.7 %copy-start.22 = (f32[128,2048]{1,0:T(8,128)S(1)}, f32[128,2048]{1,0:T(8,128)}, u32[]{:S(2)}) copy-start(f32[128,2048]{1,0:T(8,128)} %copy-done.21) | copy-start | bytes 3145732
  210.1 55.5 %copy-start.25 = (bf16[128,2048]{1,0:T(8,128)(2,1)S(1)}, bf16[128,2048]{1,0:T(8,128)(2,1)}, u32[]{:S(2)}) copy-start(bf16[128,2048]{1,0:T(8,128)(2,1)} %param.28) | copy-start | bytes 1572868
  263.8 3.6 copy-start.8
  267.4 52.3 %copy-start.15 = (bf16[256,2048]{1,0:T(8,128)(2,1)S(1)}, bf16[256,2048]{1,0:T(8,128)(2,1)}, u32[]{:S(2)}) copy-start(bf16[256,2048]{1,0:T(8,128)(2,1)} %refs_1_.1) | copy-start | bytes 3145732
  319.7 4.0 copy-start.16
  319.7 4.0 copy-start.1
  319.7 4.0 copy-start.3
  319.7 4.0 copy-start.10
  342.6 6.2 %copy-start.32 = (f32[2048]{0:T(1024)S(1)}, f32[2048]{0:T(1024)}, u32[]{:S(2)}) copy-start(f32[2048]{0:T(1024)} %param.24) | copy-start | bytes 24580
  342.6 7.0 %copy-start.11 = (bf16[1024,256]{1,0:T(8,128)(2,1)S(1)}, bf16[1024,256]{1,0:T(8,128)(2,1)}, u32[]{:S(2)}) copy-start(bf16[1024,256]{1,0:T(8,128)(2,1)} %copy-done.9) | copy-start | bytes 1572868
  349.5 3.7 copy-start.29
  349.6 5.0 copy-start.19
  463.3 46.5 %copy-start.13 = (bf16[256,2048]{1,0:T(8,128)(2,1)S(1)}, bf16[256,2048]{1,0:T(8,128)(2,1)}, u32[]{:S(2)}) copy-start(bf16[256,2048]{1,0:T(8,128)(2,1)} %copy-done.12) | copy-start | bytes 3145732
  533.9 5.5 copy-start.24
  533.9 5.8 %copy-start.17 = (f32[128,2048]{1,0:T(8,128)S(1)}, f32[128,2048]{1,0:T(8,128)}, u32[]{:S(2)}) copy-start(f32[128,2048]{1,0:T(8,128)} %copy-done.16) | copy-start | bytes 3145732
  533.9 5.8 %copy-start.26 = (bf16[128,2048]{1,0:T(8,128)(2,1)S(1)}, bf16[128,2048]{1,0:T(8,128)(2,1)}, u32[]{:S(2)}) copy-start(bf16[128,2048]{1,0:T(8,128)(2,1)} %param.28) | copy-start | bytes 1572868
  539.4 5.7 copy-start.28
  (5 other events, 4.9 us)
Sparse Core Ops, SparseCore 0:
  55.7 52.9 all-gather.1
  205.5 279.9 all-reduce.3

commit v3 on v2

--- a/solution.py
+++ b/solution.py
@@ -39,7 +39,7 @@
     def bits(self):
         return self.parts.bit_length() - 1
 
-    def meet(self, line, across):
+    def greet(self, line, across):
         barrier = pltpu.get_barrier_semaphore()
 
         def tell(device):
@@ -62,7 +62,15 @@
             for bit in range(self.bits()):
                 tell(self.partner(bit)[1])
             peers = peers + self.bits()
-        pl.semaphore_wait(barrier, peers)
+        return peers
+
+    def meet(self, peers):
+        pl.semaphore_wait(pltpu.get_barrier_semaphore(), peers)
+
+
+def weave(live):
+    while live:
+        live = [r for r in live if next(r, live) is not live]
 
 
 def remote(src, dst, send_sem, recv_sem, device):
@@ -71,7 +79,12 @@
     )
 
 
-class Gather:
+class Step:
+    def before(self, *refs):
+        pass
+
+
+class Gather(Step):
     line, across = True, False
 
     def __init__(self, x, members):
@@ -152,7 +165,7 @@
         lax.fori_loop(0, length, drain, 0)
 
 
-class GatherFfn:
+class GatherFfn(Step):
     line, across = True, False
 
     def __init__(self, x, grad_rows, w_gate, w_up, w_down, members):
@@ -164,12 +177,13 @@
         self.outputs = [
             (jax.ShapeDtypeStruct((total, width), BF16), VMEM),
             (jax.ShapeDtypeStruct((total, units), BF16), VMEM),
-            (jax.ShapeDtypeStruct((total, 2 * units), BF16), VMEM),
+            (jax.ShapeDtypeStruct((total, units), BF16), VMEM),
+            (jax.ShapeDtypeStruct((total, units), BF16), VMEM),
         ]
         self.scratch = [pltpu.VMEM(v.shape, v.dtype) for v in (grad_rows, w_gate, w_up, w_down)]
         self.scratch += [pltpu.SemaphoreType.DMA((5,)), sems, sems, sems, pltpu.SemaphoreType.DMA((members,))]
 
-    def run(self, here, x_ref, gr_ref, wg_ref, wu_ref, wd_ref, o_ref, hid_ref, ggu_ref,
+    def run(self, here, x_ref, gr_ref, wg_ref, wu_ref, wd_ref, o_ref, hid_ref, gg_ref, gu_ref,
             gr, wg, wu, wd, load_sem, left_sem, right_sem, side_sem, recv_sem):
         pos, core, length = here.pos, here.core, here.length
         rows, units, wide = x_ref.shape[0], self.units, 256
@@ -214,8 +228,8 @@
                 sigma = 1.0 / (1.0 + jnp.exp(-gate))
                 silu = gate * sigma
                 hid_ref[at, cols] = (silu * up).astype(BF16)
-                ggu_ref[at, cols] = (back * up * sigma * (1.0 + gate * (1.0 - sigma))).astype(BF16)
-                ggu_ref[at, pl.ds(pl.multiple_of(units + c * wide, wide), wide)] = (back * silu).astype(BF16)
+                gg_ref[at, cols] = (back * up * sigma * (1.0 + gate * (1.0 - sigma))).astype(BF16)
+                gu_ref[at, cols] = (back * silu).astype(BF16)
                 return carry
 
             lax.fori_loop(0, units // wide, body, 0)
@@ -274,168 +288,397 @@
         lax.fori_loop(0, length, drain, 0)
 
 
-class Scatter:
+class Scatter(Step):
     line, across = True, False
 
     def __init__(self, terms, members):
-        length = members // 2
         left, right, turned = terms[0]
         rows, width = left.shape[0] // members, right.shape[0 if turned else 1]
-        self.rows, self.width, self.turned = rows, width, [t for _, _, t in terms]
-        self.inputs = [(x, VMEM) for x, _, _ in terms] + [(w, ANY) for _, w, _ in terms]
+        self.rows, self.width, self.turned = rows, width, [t[2] for t in terms]
+        self.depth, self.start = right.shape[1 if turned else 0], [0] * len(terms)
+        lefts = [t[0] for t in terms]
+        if all(x is left for x in lefts) and len(terms) > 1:
+            lefts, self.start = [left], [i * self.depth for i in range(len(terms))]
+        self.inputs = [(x, VMEM) for x in lefts] + [(t[1], ANY) for t in terms]
         self.outputs = [(jax.ShapeDtypeStruct((rows, width), F32), VMEM)]
-        self.scratch = [pltpu.VMEM(w.shape, w.dtype) for _, w, _ in terms]
-        self.scratch += [pltpu.SemaphoreType.DMA((len(terms),)), pltpu.VMEM((members * rows, width), BF16)]
-        self.scratch += [pltpu.VMEM((length, rows, width), BF16)] * 5
-        self.scratch += [pltpu.SemaphoreType.DMA((length,))] * 6
+        self.scratch = [pltpu.VMEM(t[1].shape, t[1].dtype) for t in terms]
+        self.scratch += [pltpu.SemaphoreType.DMA((len(terms),))] + line_sum_scratch(members, rows, width)
 
     def run(self, here, *refs):
         n = len(self.turned)
-        lefts, rights, (o_ref,), helds = refs[:n], refs[n : 2 * n], refs[2 * n : 2 * n + 1], refs[2 * n + 1 : 3 * n + 1]
-        (load_sem, p_ref, side_buf, left_in, right_in, left_out, right_out,
-         side_send, side_recv, right_send, right_recv, left_send, left_recv) = refs[3 * n + 1 :]
-        pos, core, length, last = here.pos, here.core, here.length, here.last
-        rows, tile, wide = self.rows, 32, 256
+        m = len(self.inputs) - n
+        lefts, refs = (refs[:m] * n)[:n], refs[m:]
+        rights, o_ref, helds, load_sem, p_ref = refs[:n], refs[n], refs[n + 1 : 2 * n + 1], refs[2 * n + 1], refs[2 * n + 2]
+        rows, wide = self.rows, 256
         loads = [pltpu.make_async_copy(w, h, load_sem.at[i]) for i, (w, h) in enumerate(zip(rights, helds))]
         for load in loads:
             load.start()
 
-        def side_copy(p):
-            block = p_ref.at[pl.ds(pl.multiple_of((p * 2 + 1 - core) * rows, rows), rows)]
-            return remote(block, side_buf.at[p], side_send.at[p], side_recv.at[p], here.at(pos, 1 - core))
-
-        def line_copy(p, right):
-            if right:
-                return remote(right_out.at[p], right_in.at[p], right_send.at[p], right_recv.at[p], here.at(pos + 1, core))
-            return remote(left_out.at[p], left_in.at[p], left_send.at[p], left_recv.at[p], here.at(pos - 1, core))
-
         def multiply(p):
             at = pl.ds(pl.multiple_of(p * 2 * rows, 2 * rows), 2 * rows)
 
             def body(c, carry):
                 cols = pl.ds(pl.multiple_of(c * wide, wide), wide)
                 total = None
-                for left, held, turned in zip(lefts, helds, self.turned):
-                    part = dot_nt(left[at], held[cols]) if turned else dot_nn(left[at], held[:, cols])
+                for left, held, turned, start in zip(lefts, helds, self.turned, self.start):
+                    mine = left[at, start : start + self.depth]
+                    part = dot_nt(mine, held[cols]) if turned else dot_nn(mine, held[:, cols])
                     total = part if total is None else total + part
                 p_ref[at, cols] = total.astype(BF16)
                 return carry
 
             lax.fori_loop(0, self.width // wide, body, 0)
-            side_copy(p).start()
-
-        def add(p, incoming, out):
-            def body(r, carry):
-                s = pl.ds(pl.multiple_of(r * tile, tile), tile)
-                mine = pl.ds(pl.multiple_of((p * 2 + core) * rows + r * tile, tile), tile)
-                total = p_ref[mine].astype(F32) + side_buf[p, s].astype(F32)
-                for ref in incoming:
-                    total = total + ref[p, s].astype(F32)
-                if out is None:
-                    o_ref[s] = total
-                else:
-                    out[p, s] = total.astype(out.dtype)
-                return carry
-
-            lax.fori_loop(0, rows // tile, body, 0)
-
-        def move(p, right, first, source, target):
-            side_copy(p).wait_recv()
-
-            @pl.when(first)
-            def _():
-                add(p, [], target)
-
-            @pl.when(jnp.logical_not(first))
-            def _():
-                line_copy(p, right).wait_recv()
-                add(p, [source], target)
-
-            line_copy(p, right).start()
 
         for load in loads:
             load.wait()
-        for t in range(last):
-
-            def side(k, carry):
-                p = k * t + (1 - k) * (last - t)
-
-                @pl.when((1 - 2 * k) * (p - pos) > 0)
+        yield from line_sum(here, rows, multiply, o_ref, p_ref, *refs[2 * n + 3 :])
+
+
+def line_sum_scratch(members, rows, width):
+    length = members // 2
+    held = [pltpu.VMEM((members * rows, width), BF16), pltpu.VMEM((length, rows, width), BF16)]
+    held += [pltpu.VMEM((length, rows, width), BF16)] * 2
+    return held + [pltpu.SemaphoreType.DMA((length,))] * 6
+
+
+def line_sum(here, rows, multiply, o_ref, p_ref, side_buf, left_in, right_in,
+             side_send, side_recv, right_send, right_recv, left_send, left_recv):
+    pos, core, length, last, tile = here.pos, here.core, here.length, here.last, 32
+
+    def block(p, c):
+        return p_ref.at[pl.ds(pl.multiple_of((p * 2 + c) * rows, rows), rows)]
+
+    def side_copy(p):
+        return remote(block(p, 1 - core), side_buf.at[p], side_send.at[p], side_recv.at[p], here.at(pos, 1 - core))
+
+    def line_copy(p, right):
+        if right:
+            return remote(block(p, core), right_in.at[p], right_send.at[p], right_recv.at[p], here.at(pos + 1, core))
+        return remote(block(p, core), left_in.at[p], left_send.at[p], left_recv.at[p], here.at(pos - 1, core))
+
+    def make(p):
+        multiply(p)
+        side_copy(p).start()
+
+    def add(p, incoming, final):
+        def body(r, carry):
+            s = pl.ds(pl.multiple_of(r * tile, tile), tile)
+            mine = pl.ds(pl.multiple_of((p * 2 + core) * rows + r * tile, tile), tile)
+            total = p_ref[mine].astype(F32) + side_buf[p, s].astype(F32)
+            for ref in incoming:
+                total = total + ref[p, s].astype(F32)
+            if final:
+                o_ref[s] = total
+            else:
+                p_ref[mine] = total.astype(BF16)
+            return carry
+
+        lax.fori_loop(0, rows // tile, body, 0)
+
+    def move(p, right, first, source):
+        side_copy(p).wait_recv()
+
+        @pl.when(first)
+        def _():
+            add(p, [], False)
+
+        @pl.when(jnp.logical_not(first))
+        def _():
+            line_copy(p, right).wait_recv()
+            add(p, [source], False)
+
+        line_copy(p, right).start()
+
+    for t in range(last):
+
+        def side(k, carry):
+            p = k * t + (1 - k) * (last - t)
+
+            @pl.when((1 - 2 * k) * (p - pos) > 0)
+            def _():
+                make(p)
+
+            return carry
+
+        lax.fori_loop(0, 2, side, 0)
+        yield
+        right_p, left_p = last - t + pos, t - (last - pos)
+
+        @pl.when(t >= pos)
+        def _():
+            move(right_p, True, pos == 0, right_in)
+
+        @pl.when(left_p >= 0)
+        def _():
+            move(left_p, False, pos == last, left_in)
+
+    make(pos)
+    yield
+    side_copy(pos).wait_recv()
+
+    @pl.when(pos == 0)
+    def _():
+        line_copy(pos, False).wait_recv()
+        add(pos, [left_in], True)
+
+    @pl.when(pos == last)
+    def _():
+        line_copy(pos, True).wait_recv()
+        add(pos, [right_in], True)
+
+    @pl.when((pos > 0) & (pos < last))
+    def _():
+        line_copy(pos, False).wait_recv()
+        line_copy(pos, True).wait_recv()
+        add(pos, [left_in, right_in], True)
+
+    def drain(p, carry):
+        side_copy(p).wait_send()
+
+        @pl.when(p > pos)
+        def _():
+            line_copy(p, True).wait_send()
+
+        @pl.when(p < pos)
+        def _():
+            line_copy(p, False).wait_send()
+
+        return carry
+
+    lax.fori_loop(0, length, drain, 0)
+
+
+class Forward(Step):
+    line, across = True, False
+
+    def __init__(self, tokens, out_grad, attn_gain, ffn_gain, w_attn, w_output, cosine, sine, gain, positions, members):
+        rows, width = tokens.shape
+        length, size = members // 2, members * rows
+        self.heads = w_output.shape[0] // HD
+        inner, columns = w_output.shape[0], w_attn.shape[1]
+        sems = pltpu.SemaphoreType.DMA((length,))
+        self.grads = Gather(out_grad, members)
+        self.inputs = [(tokens, VMEM), (out_grad, ANY), (attn_gain[None], VMEM), (ffn_gain[None], VMEM), (w_attn, ANY)]
+        self.inputs += [(w_output, ANY)] + [(v, VMEM) for v in (cosine, sine, gain, positions.reshape(size, 1))]
+        self.outputs = [
+            (jax.ShapeDtypeStruct((size, width), BF16), ANY),
+            (jax.ShapeDtypeStruct((size, columns), F32), VMEM),
+            (jax.ShapeDtypeStruct((size, inner), BF16), VMEM),
+            (jax.ShapeDtypeStruct((size // BLOCK, 1, self.heads * BLOCK), F32), VMEM),
+            (jax.ShapeDtypeStruct((size, width), BF16), ANY),
+            (jax.ShapeDtypeStruct((rows, width), F32), VMEM),
+            (jax.ShapeDtypeStruct((rows, width), BF16), VMEM),
+        ]
+        self.scratch = [pltpu.VMEM((size, width), BF16), pltpu.VMEM(w_attn.shape, BF16), pltpu.VMEM(w_output.shape, BF16)]
+        self.scratch += [pltpu.VMEM((size, inner), BF16), pltpu.VMEM((size, HD), BF16), pltpu.VMEM((size, 2 * HD), BF16)]
+        self.scratch += [pltpu.VMEM((self.heads * BLOCK, 2 * HD), F32), pltpu.SemaphoreType.DMA((3,))]
+        self.scratch += [sems, sems, sems, pltpu.SemaphoreType.DMA((members,))]
+        self.scratch += self.grads.scratch + line_sum_scratch(members, rows, width)
+
+    def before(self, here, tok_ref, og_ref, again_ref, fgain_ref, wa_ref, wo_ref, cos_ref, sin_ref, gain_ref, pos_ref,
+               one_ref, proj_ref, ctx_ref, lse_ref, gr_ref, branch_ref, two_ref, all_ref, wa, wo, *rest):
+        load_sem = rest[4]
+        pltpu.make_async_copy(wa_ref, wa, load_sem.at[0]).start()
+        pltpu.make_async_copy(wo_ref, wo, load_sem.at[1]).start()
+        rows = tok_ref.shape[0]
+        me = (here.pos * 2 + here.core) * rows
+
+        def body(r, carry):
+            at = pl.ds(pl.multiple_of(r * 32, 32), 32)
+            x = tok_ref[at].astype(F32)
+            inv = lax.rsqrt(jnp.mean(x * x, -1, keepdims=True) + EPSILON)
+            all_ref[pl.ds(pl.multiple_of(me + r * 32, 32), 32)] = (x * inv * again_ref[...]).astype(BF16)
+            return carry
+
+        lax.fori_loop(0, rows // 32, body, 0)
+
+    def run(self, here, tok_ref, og_ref, again_ref, fgain_ref, wa_ref, wo_ref, cos_ref, sin_ref, gain_ref, pos_ref,
+            one_ref, proj_ref, ctx_ref, lse_ref, gr_ref, branch_ref, two_ref, all_ref, wa, wo,
+            q_ref, k_ref, v_ref, acc_ref, load_sem, left_sem, right_sem, side_sem, recv_sem, *rest):
+        pos, core, length = here.pos, here.core, here.length
+        rows, heads, inner = tok_ref.shape[0], self.heads, self.heads * HD
+        lane = lax.broadcasted_iota(jnp.int32, (1, HD), 1)
+
+        def block(p, c):
+            return all_ref.at[pl.ds(pl.multiple_of((p * 2 + c) * rows, rows), rows)]
+
+        def send(p, sem, to_p, to_c):
+            remote(block(p, core), block(p, core), sem.at[p], recv_sem.at[p * 2 + core], here.at(to_p, to_c)).start()
+
+        def arrived(p, c):
+            pltpu.make_async_copy(block(p, c), block(p, c), recv_sem.at[p * 2 + c]).wait()
+
+        def sent(sem, p):
+            pltpu.make_async_copy(block(p, core), block(p, core), sem.at[p]).wait()
+
+        def use(p):
+            at = pl.ds(pl.multiple_of(p * BLOCK, BLOCK), BLOCK)
+            x = dot_nn(all_ref[at], wa[...])
+            proj_ref[at] = x
+            cosine, sine = wide(cos_ref[at], inner + 2 * HD), wide(sin_ref[at], inner + 2 * HD)
+            unit, _ = normed(x)
+            spun = turn(unit * gain_ref[...], cosine, sine)
+            q_ref[at] = (spun[:, :inner].astype(BF16) * HD**-0.5).astype(BF16)
+            k_ref[at] = spun[:, inner : inner + HD].astype(BF16)
+            ones = jnp.broadcast_to(jnp.where(lane == 0, 1.0, 0.0), (BLOCK, HD)).astype(BF16)
+            v_ref[at] = jnp.concatenate([x[:, inner + HD :].astype(BF16), ones], 1)
+
+        def hop(step, carry):
+            right, left = pos + step, pos - step
+
+            @pl.when(right < length)
+            def _():
+                @pl.when(step > 0)
                 def _():
-                    multiply(p)
-
+                    arrived(right, core)
+
+                @pl.when(pos > 0)
+                def _():
+                    send(right, left_sem, pos - 1, core)
+
+                send(right, side_sem, pos, 1 - core)
+
+            @pl.when(left >= 0)
+            def _():
+                @pl.when(step > 0)
+                def _():
+                    arrived(left, core)
+
+                @pl.when(pos < here.last)
+                def _():
+                    send(left, right_sem, pos + 1, core)
+
+                @pl.when(step > 0)
+                def _():
+                    send(left, side_sem, pos, 1 - core)
+
+            def side(k, c):
+                p = pos + (1 - 2 * k) * step
+
+                @pl.when((p >= 0) & (p < length) & (step >= k))
+                def _():
+                    arrived(p, 1 - core)
+                    use(p)
+
+                return c
+
+            lax.fori_loop(0, 2, side, 0)
+            return carry
+
+        pltpu.make_async_copy(wa_ref, wa, load_sem.at[0]).wait()
+        lax.fori_loop(0, length, hop, 0)
+        keep = pltpu.make_async_copy(all_ref, one_ref, load_sem.at[2])
+        keep.start()
+        pltpu.make_async_copy(wo_ref, wo, load_sem.at[1]).wait()
+
+        def attend(i):
+            at = pl.ds(pl.multiple_of(i * BLOCK, BLOCK), BLOCK)
+            query = q_ref[at]
+            stacked = jnp.concatenate([query[:, h * HD : (h + 1) * HD] for h in range(heads)], 0)
+            acc_ref[...] = jnp.zeros_like(acc_ref)
+            index = i * BLOCK + lax.broadcasted_iota(jnp.int32, (BLOCK, 1), 0)
+            start = index - pos_ref[at]
+
+            def keys(j, c):
+                cols = pl.ds(pl.multiple_of(j * BLOCK, BLOCK), BLOCK)
+                scores = dot_nt(stacked, k_ref[cols])
+                place = j * BLOCK + lax.broadcasted_iota(jnp.int32, (1, BLOCK), 1)
+                seen = (place >= start) & (place <= index)
+                expo = [
+                    jnp.where(seen, jnp.exp(scores[h * BLOCK : (h + 1) * BLOCK]), 0.0).astype(BF16)
+                    for h in range(heads)
+                ]
+                acc_ref[...] += dot_nn(jnp.concatenate(expo, 0), v_ref[cols])
+                return c
+
+            lax.fori_loop(0, i + 1, keys, 0)
+            outs, logs = [], []
+            for h in range(heads):
+                acc = acc_ref[pl.ds(h * BLOCK, BLOCK)]
+                outs.append((acc[:, :HD] * (1.0 / acc[:, HD : HD + 1])).astype(BF16))
+                logs.append(jnp.log(acc.T[HD : HD + 1]))
+            ctx_ref[at] = jnp.concatenate(outs, 1)
+            lse_ref[i] = jnp.concatenate(logs, 1)
+
+        n = len(self.grads.scratch)
+        held = rest[n:]
+        p_ref, width = held[0], tok_ref.shape[1]
+
+        def multiply(p):
+            attend(p)
+            at = pl.ds(pl.multiple_of(p * BLOCK, BLOCK), BLOCK)
+
+            def body(c, carry):
+                cols = pl.ds(pl.multiple_of(c * 512, 512), 512)
+                p_ref[at, cols] = dot_nn(ctx_ref[at], wo[:, cols]).astype(BF16)
                 return carry
 
-            lax.fori_loop(0, 2, side, 0)
-            yield
-            right_p, left_p = last - t + pos, t - (last - pos)
-
-            @pl.when(t >= pos)
-            def _():
-                move(right_p, True, pos == 0, right_in, right_out)
-
-            @pl.when(left_p >= 0)
-            def _():
-                move(left_p, False, pos == last, left_in, left_out)
-
-        multiply(pos)
+            lax.fori_loop(0, width // 512, body, 0)
+
+        weave([self.grads.run(here, og_ref, gr_ref, *rest[:n]), line_sum(here, rows, multiply, branch_ref, *held)])
+
+        def body(r, carry):
+            at = pl.ds(pl.multiple_of(r * 32, 32), 32)
+            x = tok_ref[at].astype(F32) + branch_ref[at]
+            inv = lax.rsqrt(jnp.mean(x * x, -1, keepdims=True) + EPSILON)
+            two_ref[at] = (x * inv * fgain_ref[...]).astype(BF16)
+            return carry
+
+        lax.fori_loop(0, rows // 32, body, 0)
+
+        def drain(p, carry):
+            sent(side_sem, p)
+
+            @pl.when((p >= pos) & (pos > 0))
+            def _():
+                sent(left_sem, p)
+
+            @pl.when((p <= pos) & (pos < here.last))
+            def _():
+                sent(right_sem, p)
+
+            return carry
+
+        lax.fori_loop(0, length, drain, 0)
+        keep.wait()
         yield
-        side_copy(pos).wait_recv()
-
-        @pl.when(pos == 0)
-        def _():
-            line_copy(pos, False).wait_recv()
-            add(pos, [left_in], None)
-
-        @pl.when(pos == last)
-        def _():
-            line_copy(pos, True).wait_recv()
-            add(pos, [right_in], None)
-
-        @pl.when((pos > 0) & (pos < last))
-        def _():
-            line_copy(pos, False).wait_recv()
-            line_copy(pos, True).wait_recv()
-            add(pos, [left_in, right_in], None)
-
-        def drain(p, carry):
-            side_copy(p).wait_send()
-
-            @pl.when(p > pos)
-            def _():
-                line_copy(p, True).wait_send()
-
-            @pl.when(p < pos)
-            def _():
-                line_copy(p, False).wait_send()
-
-            return carry
-
-        lax.fori_loop(0, length, drain, 0)
-
-
-class Across:
+
+
+class Across(Step):
     line, across = False, True
 
-    def __init__(self, x, parts, backwards):
-        self.bits = parts.bit_length() - 1
-        self.order = list(range(self.bits))[:: -1 if backwards else 1]
+    def __init__(self, x, parts, colours, late=0):
+        self.bits, self.colours, self.late = parts.bit_length() - 1, colours, late
         rows, width = x.shape
         self.inputs = [(x, VMEM)]
         self.outputs = [(jax.ShapeDtypeStruct(x.shape, x.dtype), VMEM)]
         self.scratch = [pltpu.VMEM((rows, width), x.dtype)]
-        self.scratch += [pltpu.VMEM((rows >> (s + 1), width), x.dtype) for s in range(self.bits)]
-        self.scratch += [pltpu.SemaphoreType.DMA((2 * self.bits,))] * 2
+        for _ in colours:
+            part = rows // len(colours)
+            self.scratch += [pltpu.VMEM((part >> (s + 1), width), x.dtype) for s in range(self.bits)]
+            self.scratch += [pltpu.SemaphoreType.DMA((2 * self.bits,))] * 2
 
     def run(self, here, x_ref, o_ref, sum_ref, *rest):
+        for _ in range(self.late):
+            yield
+        n, rows = self.bits + 2, x_ref.shape[0] // len(self.colours)
+        live = [
+            self.one(here, backwards, i * rows, rows, x_ref, o_ref, sum_ref, *rest[i * n : (i + 1) * n])
+            for i, backwards in enumerate(self.colours)
+        ]
+        while live:
+            live = [r for r in live if next(r, live) is not live]
+            yield
+
+    def one(self, here, backwards, start, size, x_ref, o_ref, sum_ref, *rest):
         taken, (send_sem, recv_sem) = rest[: self.bits], rest[self.bits :]
-        rows = x_ref.shape[0]
-        start, size, copies, tile = 0, rows, [], 16
+        order = list(range(self.bits))[:: -1 if backwards else 1]
+        copies, tile = [], 16
 
         def part(ref, at, count):
             return ref.at[pl.ds(pl.multiple_of(at, count), count)]
 
-        for s, bit in enumerate(self.order):
+        for s, bit in enumerate(order):
             mine, device = here.partner(bit)
             half = size // 2
             keep, give = start + mine * half, start + (1 - mine) * half
@@ -455,7 +698,7 @@
 
             lax.fori_loop(0, half // tile, body, 0)
             start, size = keep, half
-        for s, bit in enumerate(self.order[::-1]):
+        for s, bit in enumerate(order[::-1]):
             mine, device = here.partner(bit)
             n = self.bits + s
             copy = remote(part(o_ref, start, size), part(o_ref, start, size), send_sem.at[n], recv_sem.at[n], device)
@@ -464,9 +707,54 @@
             yield
             copy.wait_recv()
             start, size = start - mine * size, size * 2
-        yield
         for copy in copies:
             copy.wait_send()
+
+
+class KeyValue(Step):
+    line, across = True, True
+
+    def __init__(self, x, width, members, parts):
+        self.width, self.extra, self.members = width, x.shape[0] - width, members
+        self.sum, self.all = Across(x, parts, (False,)), Gather(x, members)
+        self.inputs = [(x, VMEM)]
+        flat = jax.ShapeDtypeStruct((width, KV * HD), BF16)
+        self.outputs = [(flat, VMEM), (flat, VMEM), (jax.ShapeDtypeStruct((self.extra, 2 * HD), F32), VMEM)]
+        self.scratch = [pltpu.VMEM(x.shape, x.dtype), pltpu.VMEM((members * x.shape[0], 2 * HD), x.dtype)]
+        self.scratch += self.sum.scratch + self.all.scratch
+
+    def run(self, here, x_ref, key_ref, value_ref, small_ref, sum_ref, all_ref, *rest):
+        n = len(self.sum.scratch)
+        first = self.sum.run(here, x_ref, sum_ref, *rest[:n])
+        next(first)
+        yield
+        for _ in first:
+            pass
+        yield from self.all.run(here, sum_ref, all_ref, *rest[n:])
+        rows, share, tile = self.width + self.extra, self.members // KV, 128
+
+        def block(group, at, count):
+            total = 0.0
+            for k in range(share):
+                begin = pl.multiple_of((group * share + k) * rows + at, 16)
+                total = total + all_ref[pl.ds(begin, count)].astype(F32)
+            return total
+
+        for pair in range(KV // 2):
+            cols = slice(2 * HD * pair, 2 * HD * (pair + 1))
+
+            def body(r, carry):
+                at = pl.ds(pl.multiple_of(r * tile, tile), tile)
+                one, two = block(2 * pair, r * tile, tile), block(2 * pair + 1, r * tile, tile)
+                key_ref[at, cols] = jnp.concatenate([one[:, :HD], two[:, :HD]], 1).astype(BF16)
+                value_ref[at, cols] = jnp.concatenate([one[:, HD:], two[:, HD:]], 1).astype(BF16)
+                return carry
+
+            lax.fori_loop(0, self.width // tile, body, 0)
+        small = 0.0
+        for group in range(KV):
+            small = small + block(group, self.width, self.extra)
+        small_ref[...] = small
 
 
 def together(steps, members, parts, collective_id, vmem=48):
@@ -478,10 +766,11 @@
         made = [[refs.pop(0) for _ in range(c[1])] for c in counts]
         held = [[refs.pop(0) for _ in range(c[2])] for c in counts]
         here = Place(members, parts)
-        here.meet(any(s.line for s in steps), any(s.across for s in steps))
-        live = [s.run(here, *g, *m, *h) for s, g, m, h in zip(steps, given, made, held)]
-        while live:
-            live = [r for r in live if next(r, live) is not live]
+        peers = here.greet(any(s.line for s in steps), any(s.across for s in steps))
+        for s, g, m, h in zip(steps, given, made, held):
+            s.before(here, *g, *m, *h)
+        here.meet(peers)
+        weave([s.run(here, *g, *m, *h) for s, g, m, h in zip(steps, given, made, held)])
 
     return pl.pallas_call(
         kernel,
@@ -529,61 +818,6 @@
 
 def turn_back(x, cosine, sine):
     return x * cosine - half_turn(x) * sine
-
-def attend_kernel(heads, proj_ref, cos_ref, sin_ref, gain_ref, pos_ref, ctx_ref, lse_ref, k_ref, v_ref, acc_ref):
-    width = heads * HD
-    scale = HD ** -0.5
-    count = proj_ref.shape[0] // BLOCK
-    lane = lax.broadcasted_iota(jnp.int32, (1, HD), 1)
-    def outer(i, carry):
-        rows = pl.ds(pl.multiple_of(i * BLOCK, BLOCK), BLOCK)
-        x = proj_ref[rows]
-        cosine, sine = wide(cos_ref[rows], width + 2 * HD), wide(sin_ref[rows], width + 2 * HD)
-        unit, _ = normed(x)
-        spun = turn(unit * gain_ref[...], cosine, sine)
-        query = spun[:, :width].astype(BF16) * scale
-        query = query.astype(BF16)
-        stacked = jnp.concatenate([query[:, h * HD:(h + 1) * HD] for h in range(heads)], 0)
-        k_ref[rows] = spun[:, width:width + HD].astype(BF16)
-        value = x[:, width + HD:].astype(BF16)
-        ones = jnp.broadcast_to(jnp.where(lane == 0, 1.0, 0.0), (BLOCK, HD)).astype(BF16)
-        v_ref[rows] = jnp.concatenate([value, ones], 1)
-        acc_ref[...] = jnp.zeros_like(acc_ref)
-        index = i * BLOCK + lax.broadcasted_iota(jnp.int32, (BLOCK, 1), 0)
-        start = index - pos_ref[rows]
-        def inner(j, c):
-            cols = pl.ds(pl.multiple_of(j * BLOCK, BLOCK), BLOCK)
-            scores = dot_nt(stacked, k_ref[cols])
-            place = j * BLOCK + lax.broadcasted_iota(jnp.int32, (1, BLOCK), 1)
-            seen = (place >= start) & (place <= index)
-            expo = jnp.concatenate(
-                [jnp.where(seen, jnp.exp(scores[h * BLOCK:(h + 1) * BLOCK]), 0.0).astype(BF16) for h in range(heads)], 0)
-            acc_ref[...] += dot_nn(expo, v_ref[cols])
-            return c
-        lax.fori_loop(0, i + 1, inner, 0)
-        outs, logs = [], []
-        for h in range(heads):
-            acc = acc_ref[pl.ds(h * BLOCK, BLOCK)]
-            total = acc[:, HD:HD + 1]
-            outs.append((acc[:, :HD] * (1.0 / total)).astype(BF16))
-            logs.append(jnp.log(acc.T[HD:HD + 1]))
-        ctx_ref[rows] = jnp.concatenate(outs, 1)
-        lse_ref[i] = jnp.concatenate(logs, 1)
-        return carry
-    lax.fori_loop(0, count, outer, 0)
-
-def attend(proj, cosine, sine, gain, positions, heads):
-    size = proj.shape[0]
-    count = size // BLOCK
-    vm = pl.BlockSpec(memory_space=pltpu.VMEM)
-    return pl.pallas_call(
-        functools.partial(attend_kernel, heads),
-        out_shape=(jax.ShapeDtypeStruct((size, heads * HD), BF16), jax.ShapeDtypeStruct((count, 1, heads * BLOCK), F32)),
-        in_specs=[vm] * 5, out_specs=(vm, vm),
-        scratch_shapes=[pltpu.VMEM((size, HD), BF16), pltpu.VMEM((size, 2 * HD), BF16), pltpu.VMEM((heads * BLOCK, 2 * HD), F32)],
-        compiler_params=pltpu.CompilerParams(vmem_limit_bytes=40 << 20),
-        cost_estimate=pl.CostEstimate(flops=1, bytes_accessed=1, transcendentals=0),
-    )(proj, cosine, sine, gain, positions.reshape(size, 1))
 
 def stack_lanes(x, heads):
     return jnp.concatenate([x[h * HD:(h + 1) * HD] for h in range(heads)], 1)
@@ -738,36 +972,43 @@
     tokens_f = tokens.astype(F32)
     inv_one = lax.rsqrt(jnp.mean(tokens_f * tokens_f, -1, keepdims=True) + EPSILON)
     normed_one = tokens_f * inv_one
-    h_one = (normed_one * attn_gain).astype(BF16)
     key_cols = lax.dynamic_slice_in_dim(w_key, group * HD, HD, 1)
     value_cols = lax.dynamic_slice_in_dim(w_value, group * HD, HD, 1)
     w_attn = jnp.concatenate([w_query, key_cols, value_cols], 1)
     cosine, sine = rope_tables(positions)
     gain = jnp.concatenate([jnp.tile(query_gain, heads), key_gain, jnp.ones(HD, F32)])[None]
 
-    rows_one = together([Gather(h_one, members)], members, parts, 0)[0]
-    rows_one, out_grad_late = after(rows_one, out_grad)
-    grad_rows = lax.all_gather(out_grad_late, "mp", axis=0, tiled=True)
-    projected = matmul(rows_one, w_attn)
-    context, lse = attend(projected, cosine, sine, gain, positions, heads)
-    attn_branch = together([Scatter([(context, w_output, False)], members)], members, parts, 1)[0]
+    rows_one, projected, context, lse, grad_rows, attn_branch, h_two = together(
+        [
+            Forward(
+                tokens, out_grad, attn_gain, ffn_gain, w_attn, w_output, cosine, sine, gain, positions, members
+            )
+        ],
+        members,
+        parts,
+        0,
+        58,
+    )
+    rows_two, hidden, grad_gate, grad_up = together(
+        [GatherFfn(h_two, grad_rows, w_gate, w_up, w_down, members)], members, parts, 5, 58
+    )
     residual_mid = tokens_f + attn_branch
     inv_two = lax.rsqrt(jnp.mean(residual_mid * residual_mid, -1, keepdims=True) + EPSILON)
     normed_two = residual_mid * inv_two
-    h_two = (normed_two * ffn_gain).astype(BF16)
-    rows_two, hidden, grad_gate_up = together(
-        [GatherFfn(h_two, grad_rows, w_gate, w_up, w_down, members)], members, parts, 5, 58
+    ffn_parts = (
+        matmul_left_t(rows_two, grad_gate).astype(BF16),
+        matmul_left_t(rows_two, grad_up).astype(BF16),
     )
-    ffn_parts = (
-        matmul_left_t(rows_two, grad_gate_up).astype(BF16),
-        matmul_left_t(hidden, grad_rows).astype(BF16),
-    )
-    ffn_parts, grad_gate_up, hidden = lax.optimization_barrier((ffn_parts, grad_gate_up, hidden))
-    grad_w_ffn, grad_w_down = lax.psum(ffn_parts, "dp")
-
-    grad_gate, grad_up = grad_gate_up[:, :ffn_width], grad_gate_up[:, ffn_width:]
+    ffn_parts, grad_gate, grad_up, hidden = lax.optimization_barrier((ffn_parts, grad_gate, grad_up, hidden))
+    grad_w_gate, grad_w_up = lax.psum(ffn_parts, "dp")
+    down_part = matmul_left_t(hidden, grad_rows).astype(BF16)
+
     grad_h_two = together(
-        [Scatter([(grad_gate, w_gate, True), (grad_up, w_up, True)], members)], members, parts, 6, 58
+        [Scatter([(grad_gate, w_gate, True), (grad_up, w_up, True)], members)],
+        members,
+        parts,
+        6,
+        58,
     )[0]
     grad_ffn_gain = jnp.sum(grad_h_two * normed_two, 0)
     grad_mid = out_grad.astype(F32) + norm_back(grad_h_two, normed_two, inv_two, ffn_gain)
@@ -794,31 +1035,25 @@
             jnp.sum(tokens_f * tokens_f)[None],
         ]
     )
-    columns = w_attn.shape[1]
     unit = 16 * parts
-    extra = -(-small.shape[0] // (unit * columns)) * unit
-    small_rows = jnp.pad(small, (0, extra * columns - small.shape[0])).reshape(extra, columns)
-    attn_part = jnp.concatenate([grad_w_attn, small_rows], 0).astype(BF16)
-    grad_w_output, attn_sum, grad_h_one = together(
+    extra = -(-small.shape[0] // (unit * 2 * HD)) * unit
+    small_rows = jnp.pad(small, (0, extra * 2 * HD - small.shape[0])).reshape(extra, 2 * HD)
+    kv_part = jnp.concatenate([grad_w_attn[:, query_width:], small_rows], 0).astype(BF16)
+    query_part = grad_w_attn[:, :query_width].astype(BF16)
+    grad_w_key, grad_w_value, small_sum, grad_h_one, grad_w_output, grad_w_query, grad_w_down = together(
         [
-            Across(output_part, parts, False),
-            Across(attn_part, parts, True),
+            KeyValue(kv_part, width, members, parts),
             Scatter([(grad_proj, w_attn, True)], members),
+            Across(output_part, parts, (False,), 2),
+            Across(query_part, parts, (True,), 2),
+            Across(down_part, parts, (False, True), 2),
         ],
         members,
         parts,
         3,
+        58,
     )
-    payload = jnp.concatenate(
-        [attn_sum[:width, query_width:], attn_sum[width:].reshape(-1, 2 * HD)], 0
-    )
-    every = together([Gather(payload, members)], members, parts, 4)[0]
-    every = every.reshape(members, payload.shape[0], 2 * HD)
-    kv = every[:, :width].astype(F32).reshape(KV, share, width, 2 * HD).sum(1)
-    kv = jnp.transpose(kv, (1, 0, 2))
-    grad_w_key = kv[:, :, :HD].reshape(width, KV * HD)
-    grad_w_value = kv[:, :, HD:].reshape(width, KV * HD)
-    small_sum = every[:, width:].astype(F32).sum(0).reshape(-1)
+    small_sum = small_sum.reshape(-1)
     entry_count = tokens.size * parts * members
     at = 2 * width
     residual_rms = jnp.sqrt(small_sum[at + 2 * HD : at + 2 * HD + 1] / entry_count)
@@ -834,12 +1069,12 @@
     return (
         output,
         grad_tokens,
-        attn_sum[:width, :query_width].astype(F32),
-        grad_w_key,
-        grad_w_value,
+        grad_w_query.astype(F32),
+        grad_w_key.astype(F32),
+        grad_w_value.astype(F32),
         grad_w_output.astype(F32),
-        grad_w_ffn[:, :ffn_width].astype(F32),
-        grad_w_ffn[:, ffn_width:].astype(F32),
+        grad_w_gate.astype(F32),
+        grad_w_up.astype(F32),
         grad_w_down.astype(F32),
         small_sum[:width],
         small_sum[width:at],

time: 580 us -> 544 us (0.938)
  the two profiles are of different devices: /device:TPU:0 before, /device:TPU:10 now
where the time goes in v3:
time: 544 us; the launch traced here: 537 us
  Pallas kernels  437 us (80%)
  other arithmetic  38 us (7%)
  matrix products  32.8 us (6%)
  between operations  16.8 us (3%)
  local copies, waits for them, and re-layouts  12.4 us (2%)
    pallas_call x5, Pallas kernels, together(): pl.pallas_call(kernel, out_shape=[o for s in steps for o, _ in s.outputs]...  419 us
    dot_general x5, matrix products, matmul_left_t(): lax.dot_general(left, right, (((0,), (0,)), ((), ())), preferred_element_...  29.1 us
    pallas_call x1, Pallas kernels, attend_back(): pl.pallas_call(functools.partial(attend_back_kernel, heads), out_shape=(j...  17.7 us
  transfers between devices with their start and end apart: 1, of which 0 were waited for; matrix products, arithmetic and copies ran while one was open for 8% of the time, Pallas kernels for 55%

profile of v3, /device:TPU:10, one launch (start us, length us, event | category | flops | bytes accessed | tf_op | source)
XLA Modules:
  0.0 536.8 jit_solution(8368885060883274348)
XLA Ops:
  7.3 0.8 convert_element_type.62
  8.6 1.0 copy.29.refs_6_.cos_ref
  9.7 1.0 copy.30.refs_7_.sin_ref
  12.7 1.7 copy.31.refs_9_
  14.4 1.6 constant_dynamic-slice_fusion
  16.0 1.5 pad_maximum_fusion.refs_4_.refs_2_
  17.5 99.1 %shard_map.253 = (bf16[1024,2048]{1,0:T(8,128)(2,1)}, f32[1024,384]{1,0:T(8,128)}, bf16[1024,256]{1,0:T(8,128)(2,1)}, f32[4,1,1024]{2,1,0:T(1,128)}, bf16[1024,2...) custom-call(bf16[128,2048]{1,0:T(8,128)(2,1)} %refs_0_.1, bf16[128,2048]{1,0:T(8,128)(2,1)} %refs_1_.1, ...), custom_call_target="tpu_custom_call" | custom-call | flops 1 | bytes 1 | tf_op jit(solution)/shard_map/pallas_call | solution.py:775
  116.6 41.9 %shard_map.254 = (bf16[1024,2048]{1,0:T(8,128)(2,1)}, bf16[1024,1024]{1,0:T(8,128)(2,1)}, bf16[1024,1024]{1,0:T(8,128)(2,1)}, bf16[1024,1024]{1,0:T(8,128)(2,1)}) custom-call(bf16[128,2048]{1,0:T(8,128)(2,1)} %get-tuple-element.43.refs_0_, bf16[1024,2048]{1,0:T(8,128)(2,1)} %get-tuple-element.44.refs_1_, bf16[2048,1024]{1,0:T(8,128)(2,1)} %refs_2_.4, ...), custom_call_target="tpu_custom_call" | custom-call | flops 1 | bytes 1 | tf_op jit(solution)/shard_map/pallas_call | solution.py:775
  158.5 9.6 %convolution_convert_fusion.1 = bf16[2048,1024]{1,0:T(8,128)(2,1)} fusion(bf16[1024,2048]{1,0:T(8,128)(2,1)} %get-tuple-element.45, bf16[1024,1024]{1,0:T(8,128)(2,1)} %get-tuple-element.50.refs_1_), kind=kOutput, calls=%fused_computation.1 | convolution fusion | flops 4297064448 | bytes 10485760 | tf_op jit(solution)/shard_map/dot_general | solution.py:924
  168.1 6.2 %convolution_convert_fusion.2 = bf16[2048,1024]{1,0:T(8,128)(2,1)} fusion(bf16[1024,2048]{1,0:T(8,128)(2,1)S(1)} %copy-done.34, bf16[1024,1024]{1,0:T(8,128)(2,1)S(1)} %copy-done.23), kind=kOutput, calls=%fused_computation.2 | convolution fusion | flops 4297064448 | bytes 10485760 | tf_op jit(solution)/shard_map/dot_general | solution.py:924
  174.3 60.6 %shard_map.255 = f32[128,2048]{1,0:T(8,128)} custom-call(bf16[1024,1024]{1,0:T(8,128)(2,1)} %get-tuple-element.49.refs_0_, bf16[1024,1024]{1,0:T(8,128)(2,1)} %get-tuple-element.50.refs_1_, bf16[2048,1024]{1,0:T(8,128)(2,1)} %refs_2_.4, bf16[2048,1024]{1,0:T(8,128)(2,1)} %refs_3_.3), custom_call_target="tpu_custom_call" | custom-call | flops 1 | bytes 1 | tf_op jit(solution)/shard_map/pallas_call | solution.py:775
  235.3 2.6 multiply_reduce_fusion.3
  238.4 51.7 %shard_map.256 = (bf16[1024,2048]{1,0:T(8,128)(2,1)}, f32[128,2048]{1,0:T(8,128)S(1)}) custom-call(bf16[128,2048]{1,0:T(8,128)(2,1)S(1)} %fusion.10.refs_0_, bf16[1024,1024]{1,0:T(8,128)(2,1)S(1)} %copy-done.2, bf16[1024,2048]{1,0:T(8,128)(2,1)} %refs_2_.5), custom_call_target="tpu_custom_call" | custom-call | flops 1 | bytes 1 | tf_op jit(solution)/shard_map/pallas_call | solution.py:775
  290.2 3.7 convolution_convert_fusion.4.grad_ref
  294.0 17.7 %shard_map.257 = (bf16[1024,384]{1,0:T(8,128)(2,1)S(1)}, f32[1,384]{1,0:T(1,128)S(1)}) custom-call(f32[1024,384]{1,0:T(8,128)S(1)} %copy-done.3, f32[1024,128]{1,0:T(8,128)S(1)} %copy-done, f32[1024,128]{1,0:T(8,128)S(1)} %copy-done.1, f32[1,384]{1,0:T(1,128)S(1)} %copy-done.8, s32[4,1,256]{2,1,0:T(1,128)S(1)} %bitcast.33, bf16[1024,256]{1,0:T(8,128)(2,1)S(1)} %copy-done.5, ...), custom_call_target="tpu_custom_call" | custom-call | flops 1 | bytes 1 | tf_op jit(solution)/shard_map/pallas_call | solution.py:908
  311.7 2.5 fusion.11
  314.2 1.1 copy-done.24
  315.3 0.8 slice.47
  316.3 0.7 concatenate.16
  317.0 2.0 pad_maximum_fusion.1.refs_0_
  319.1 4.7 convolution_convert_fusion.3.refs_3_
  323.7 6.2 %convolution_convert_fusion.refs_5_ = bf16[1024,2048]{1,0:T(8,128)(2,1)} fusion(bf16[1024,1024]{1,0:T(8,128)(2,1)S(1)} %copy-done.2, bf16[1024,2048]{1,0:T(8,128)(2,1)S(1)} %copy-done.20), kind=kOutput, calls=%fused_computation | convolution fusion | flops 4297064448 | bytes 10485760 | tf_op jit(solution)/shard_map/dot_general | solution.py:924
  329.9 1.0 slice.49.refs_4_
  331.0 165.8 %shard_map.258 = (bf16[2048,512]{1,0:T(8,128)(2,1)}, bf16[2048,512]{1,0:T(8,128)(2,1)}, f32[64,128]{1,0:T(8,128)}, f32[128,2048]{1,0:T(8,128)}, bf16[256,2048]{1...) custom-call(bf16[2112,128]{1,0:T(8,128)(2,1)} %pad_maximum_fusion.1.refs_0_, ...), custom_call_target="tpu_custom_call" | custom-call | flops 1 | bytes 1 | tf_op jit(solution)/shard_map/pallas_call | solution.py:775
  496.8 6.8 %convert_element_type.79 = f32[1024,2048]{1,0:T(8,128)} convert(bf16[1024,2048]{1,0:T(8,128)(2,1)} %get-tuple-element.67) | non-fusion elementwise | flops 2097152 | bytes 12582912 | tf_op jit(solution)/shard_map/convert_element_type | solution.py:1078
  503.6 2.6 convert_element_type.74
  506.2 2.6 convert_element_type.75
  508.9 1.5 convert_element_type.73
  510.3 1.6 convert_element_type.76
  513.5 1.9 fusion.8
  517.2 6.8 %convert_element_type.77 = f32[2048,1024]{1,0:T(8,128)} convert(bf16[2048,1024]{1,0:T(8,128)(2,1)} %get-tuple-element.74) | non-fusion elementwise | flops 2097152 | bytes 12582912 | tf_op jit(solution)/shard_map/convert_element_type | solution.py:1076
  523.9 4.4 convert_element_type.78
  (100 shorter events, 6.3 us)
Async XLA Ops:
  7.2 8.8 %copy-start.26 = (bf16[2048,256]{1,0:T(8,128)(2,1)S(1)}, bf16[2048,256]{1,0:T(8,128)(2,1)}, u32[]{:S(2)}) copy-start(bf16[2048,256]{1,0:T(8,128)(2,1)} %param.17) | copy-start | bytes 3145732
  7.2 510.0 %all-reduce.4.cloned.1.call-start = ((), (), s32[]{:S(2)}) async-start(), calls=%async_computation | async-start | bytes 16777216 | tf_op jit(solution)/shard_map/psum | solution.py:1003
  158.5 9.6 %copy-start.23 = (bf16[1024,1024]{1,0:T(8,128)(2,1)S(1)}, bf16[1024,1024]{1,0:T(8,128)(2,1)}, u32[]{:S(2)}) copy-start(bf16[1024,1024]{1,0:T(8,128)(2,1)} %get-tuple-element.49.refs_0_) | copy-start | bytes 6291460
  158.5 9.6 %copy-start.34 = (bf16[1024,2048]{1,0:T(8,128)(2,1)S(1)}, bf16[1024,2048]{1,0:T(8,128)(2,1)}, u32[]{:S(2)}) copy-start(bf16[1024,2048]{1,0:T(8,128)(2,1)} %get-tuple-element.45) | copy-start | bytes 12582916
  174.3 60.7 %copy-start.9 = (bf16[128,2048]{1,0:T(8,128)(2,1)S(1)}, bf16[128,2048]{1,0:T(8,128)(2,1)}, u32[]{:S(2)}) copy-start(bf16[128,2048]{1,0:T(8,128)(2,1)} %refs_0_.1) | copy-start | bytes 1572868
  174.3 60.7 %copy-start.11 = (f32[128,2048]{1,0:T(8,128)S(1)}, f32[128,2048]{1,0:T(8,128)}, u32[]{:S(2)}) copy-start(f32[128,2048]{1,0:T(8,128)} %get-tuple-element.42) | copy-start | bytes 3145732
  174.3 60.9 %copy-start.30 = (f32[2048]{0:T(1024)S(1)}, f32[2048]{0:T(1024)}, u32[]{:S(2)}) copy-start(f32[2048]{0:T(1024)} %param.25) | copy-start | bytes 24580
  235.0 2.9 copy-start.13
  235.0 2.9 copy-start.16
  235.0 3.4 copy-start.2
  238.4 51.7 %copy-start.29 = (bf16[256,2048]{1,0:T(8,128)(2,1)S(1)}, bf16[256,2048]{1,0:T(8,128)(2,1)}, u32[]{:S(2)}) copy-start(bf16[256,2048]{1,0:T(8,128)(2,1)} %refs_5_.1) | copy-start | bytes 3145732
  290.1 3.8 copy-start
  290.1 3.8 copy-start.1
  290.1 3.8 copy-start.3
  290.1 3.8 copy-start.5
  290.1 3.8 copy-start.6
  290.1 3.8 copy-start.7
  290.1 3.8 copy-start.8
  290.2 21.5 %copy-start.15 = (bf16[2048,384]{1,0:T(8,128)(2,1)S(1)}, bf16[2048,384]{1,0:T(8,128)(2,1)}, u32[]{:S(2)}) copy-start(bf16[2048,384]{1,0:T(8,128)(2,1)} %pad_maximum_fusion.refs_4_.refs_2_) | copy-start | bytes 4718596
  290.2 21.5 %copy-start.33 = (bf16[1024,2048]{1,0:T(8,128)(2,1)S(1)}, bf16[1024,2048]{1,0:T(8,128)(2,1)}, u32[]{:S(2)}) copy-start(bf16[1024,2048]{1,0:T(8,128)(2,1)} %get-tuple-element.53) | copy-start | bytes 12582916
  311.7 4.6 copy-start.31
  317.0 6.7 %copy-start.20 = (bf16[1024,2048]{1,0:T(8,128)(2,1)S(1)}, bf16[1024,2048]{1,0:T(8,128)(2,1)}, u32[]{:S(2)}) copy-start(bf16[1024,2048]{1,0:T(8,128)(2,1)} %get-tuple-element.44.refs_1_) | copy-start | bytes 12582916
  323.7 6.2 %copy-start.25 = (bf16[2048,384]{1,0:T(8,128)(2,1)S(1)}, bf16[2048,384]{1,0:T(8,128)(2,1)}, u32[]{:S(2)}) copy-start(bf16[2048,384]{1,0:T(8,128)(2,1)} %copy-done.24) | copy-start | bytes 4718596
  496.8 6.8 %copy-start.22 = (bf16[2048,512]{1,0:T(8,128)(2,1)S(1)}, bf16[2048,512]{1,0:T(8,128)(2,1)}, u32[]{:S(2)}) copy-start(bf16[2048,512]{1,0:T(8,128)(2,1)} %get-tuple-element.62) | copy-start | bytes 6291460
  506.2 4.1 copy-start.27
  508.8 3.1 copy-start.32
  508.8 4.3 copy-start.10
  508.8 4.3 copy-start.19
  508.8 4.6 copy-start.12
  508.8 4.6 copy-start.14
  508.8 4.6 copy-start.17
  517.2 6.8 %copy-start.18 = (bf16[2048,1024]{1,0:T(8,128)(2,1)S(1)}, bf16[2048,1024]{1,0:T(8,128)(2,1)}, u32[]{:S(2)}) copy-start(bf16[2048,1024]{1,0:T(8,128)(2,1)} %get-tuple-element.75) | copy-start | bytes 12582916
  (4 other events, 8.9 us)
Sparse Core Ops, SparseCore 0:
  174.4 185.7 all-reduce.3

commit v4 on v3

--- a/solution.py
+++ b/solution.py
@@ -2,6 +2,7 @@
 
 import jax
 import jax.numpy as jnp
+import numpy as np
 from jax import lax
 from jax.experimental import pallas as pl
 from jax.experimental.pallas import tpu as pltpu
@@ -451,15 +452,18 @@
 class Forward(Step):
     line, across = True, False
 
-    def __init__(self, tokens, out_grad, attn_gain, ffn_gain, w_attn, w_output, cosine, sine, gain, positions, members):
+    def __init__(self, tokens, out_grad, attn_gain, ffn_gain, query_gain, key_gain, w_query, w_key, w_value, w_output,
+                 positions, members):
         rows, width = tokens.shape
-        length, size = members // 2, members * rows
-        self.heads = w_output.shape[0] // HD
-        inner, columns = w_output.shape[0], w_attn.shape[1]
+        length, size, inner = members // 2, members * rows, w_query.shape[1]
+        self.heads, self.share, columns = inner // HD, members // KV, inner + 2 * HD
         sems = pltpu.SemaphoreType.DMA((length,))
         self.grads = Gather(out_grad, members)
-        self.inputs = [(tokens, VMEM), (out_grad, ANY), (attn_gain[None], VMEM), (ffn_gain[None], VMEM), (w_attn, ANY)]
-        self.inputs += [(w_output, ANY)] + [(v, VMEM) for v in (cosine, sine, gain, positions.reshape(size, 1))]
+        freq = ROPE_BASE ** (-np.arange(HD // 2, dtype=np.float32) / (HD // 2))
+        freq = jnp.asarray(np.tile(freq, 4)[None], F32)
+        self.inputs = [(tokens, VMEM), (out_grad, ANY), (attn_gain[None], VMEM), (ffn_gain[None], VMEM)]
+        self.inputs += [(query_gain[None], VMEM), (key_gain[None], VMEM), (w_query, ANY), (w_key, ANY), (w_value, ANY)]
+        self.inputs += [(w_output, ANY), (positions.reshape(size // 128, 128), VMEM), (freq, VMEM)]
         self.outputs = [
             (jax.ShapeDtypeStruct((size, width), BF16), ANY),
             (jax.ShapeDtypeStruct((size, columns), F32), VMEM),
@@ -468,18 +472,28 @@
             (jax.ShapeDtypeStruct((size, width), BF16), ANY),
             (jax.ShapeDtypeStruct((rows, width), F32), VMEM),
             (jax.ShapeDtypeStruct((rows, width), BF16), VMEM),
+            (jax.ShapeDtypeStruct((size, 2 * HD), F32), VMEM),
+            (jax.ShapeDtypeStruct((size, 2 * HD), F32), VMEM),
         ]
-        self.scratch = [pltpu.VMEM((size, width), BF16), pltpu.VMEM(w_attn.shape, BF16), pltpu.VMEM(w_output.shape, BF16)]
+        self.scratch = [pltpu.VMEM((size, width), BF16), pltpu.VMEM(w_query.shape, BF16), pltpu.VMEM((width, 2 * HD), BF16)]
+        self.scratch += [pltpu.VMEM((width, 2 * HD), BF16), pltpu.VMEM((width, 2 * HD), BF16), pltpu.VMEM(w_output.shape, BF16)]
+        self.scratch += [pltpu.VMEM((size, 2 * HD), jnp.int32)]
         self.scratch += [pltpu.VMEM((size, inner), BF16), pltpu.VMEM((size, HD), BF16), pltpu.VMEM((size, 2 * HD), BF16)]
-        self.scratch += [pltpu.VMEM((self.heads * BLOCK, 2 * HD), F32), pltpu.SemaphoreType.DMA((3,))]
+        self.scratch += [pltpu.VMEM((self.heads * BLOCK, 2 * HD), F32), pltpu.SemaphoreType.DMA((5,))]
         self.scratch += [sems, sems, sems, pltpu.SemaphoreType.DMA((members,))]
         self.scratch += self.grads.scratch + line_sum_scratch(members, rows, width)
 
-    def before(self, here, tok_ref, og_ref, again_ref, fgain_ref, wa_ref, wo_ref, cos_ref, sin_ref, gain_ref, pos_ref,
-               one_ref, proj_ref, ctx_ref, lse_ref, gr_ref, branch_ref, two_ref, all_ref, wa, wo, *rest):
-        load_sem = rest[4]
-        pltpu.make_async_copy(wa_ref, wa, load_sem.at[0]).start()
-        pltpu.make_async_copy(wo_ref, wo, load_sem.at[1]).start()
+    def loads(self, here, wq_ref, wk_ref, wv_ref, wo_ref, wq, wk, wv, wo, load_sem):
+        group = (here.pos * 2 + here.core) // self.share
+        cols = pl.ds(pl.multiple_of(group // 2 * 2 * HD, 2 * HD), 2 * HD)
+        pairs = [(wq_ref, wq), (wk_ref.at[:, cols], wk), (wv_ref.at[:, cols], wv), (wo_ref, wo)]
+        return lax.rem(group, 2), [pltpu.make_async_copy(a, b, load_sem.at[i]) for i, (a, b) in enumerate(pairs)]
+
+    def before(self, here, tok_ref, og_ref, again_ref, fgain_ref, qgain_ref, kgain_ref, wq_ref, wk_ref, wv_ref, wo_ref,
+               pos_ref, freq_ref, one_ref, proj_ref, ctx_ref, lse_ref, gr_ref, branch_ref, two_ref, cos_ref, sin_ref,
+               all_ref, wq, wk, wv, wkv, wo, *rest):
+        for load in self.loads(here, wq_ref, wk_ref, wv_ref, wo_ref, wq, wk, wv, wo, rest[5])[1]:
+            load.start()
         rows = tok_ref.shape[0]
         me = (here.pos * 2 + here.core) * rows
 
@@ -492,11 +506,13 @@
 
         lax.fori_loop(0, rows // 32, body, 0)
 
-    def run(self, here, tok_ref, og_ref, again_ref, fgain_ref, wa_ref, wo_ref, cos_ref, sin_ref, gain_ref, pos_ref,
-            one_ref, proj_ref, ctx_ref, lse_ref, gr_ref, branch_ref, two_ref, all_ref, wa, wo,
+    def run(self, here, tok_ref, og_ref, again_ref, fgain_ref, qgain_ref, kgain_ref, wq_ref, wk_ref, wv_ref, wo_ref,
+            pos_ref, freq_ref, one_ref, proj_ref, ctx_ref, lse_ref, gr_ref, branch_ref, two_ref, cos_ref, sin_ref,
+            all_ref, wq, wk, wv, wkv, wo, place_ref,
             q_ref, k_ref, v_ref, acc_ref, load_sem, left_sem, right_sem, side_sem, recv_sem, *rest):
         pos, core, length = here.pos, here.core, here.length
-        rows, heads, inner = tok_ref.shape[0], self.heads, self.heads * HD
+        rows, width = tok_ref.shape
+        heads, inner, size = self.heads, self.heads * HD, proj_ref.shape[0]
         lane = lax.broadcasted_iota(jnp.int32, (1, HD), 1)
 
         def block(p, c):
@@ -511,19 +527,47 @@
         def sent(sem, p):
             pltpu.make_async_copy(block(p, core), block(p, core), sem.at[p]).wait()
 
+        def prepare():
+            odd, loads = self.loads(here, wq_ref, wk_ref, wv_ref, wo_ref, wq, wk, wv, wo, load_sem)
+            for load in loads:
+                load.wait()
+            low = lax.broadcasted_iota(jnp.int32, (1, 2 * HD), 1) < HD
+
+            def pick(r, carry):
+                at = pl.ds(pl.multiple_of(r * 256, 256), 256)
+                key, value = wk[at].astype(F32), wv[at].astype(F32)
+                key = jnp.where(odd == 1, pltpu.roll(key, HD, 1), key)
+                value = jnp.where(odd == 1, value, pltpu.roll(value, HD, 1))
+                wkv[at] = jnp.where(low, key, value).astype(BF16)
+                return carry
+
+            lax.fori_loop(0, width // 256, pick, 0)
+
+            def table(r, carry):
+                at = pl.ds(pl.multiple_of(r * 128, 128), 128)
+                place = jnp.broadcast_to(pos_ref[pl.ds(r, 1)].astype(F32), (128, 128)).T
+                place_ref[at] = place.astype(jnp.int32)
+                angle = place * freq_ref[...]
+                cos_ref[at] = jnp.cos(angle)
+                sin_ref[at] = jnp.sin(angle)
+                return carry
+
+            lax.fori_loop(0, size // 128, table, 0)
+
         def use(p):
             at = pl.ds(pl.multiple_of(p * BLOCK, BLOCK), BLOCK)
-            x = dot_nn(all_ref[at], wa[...])
+            x = jnp.concatenate([dot_nn(all_ref[at], wq[...]), dot_nn(all_ref[at], wkv[...])], 1)
             proj_ref[at] = x
+            gain = jnp.concatenate([qgain_ref[...]] * heads + [kgain_ref[...], jnp.ones((1, HD), F32)], 1)
             cosine, sine = wide(cos_ref[at], inner + 2 * HD), wide(sin_ref[at], inner + 2 * HD)
             unit, _ = normed(x)
-            spun = turn(unit * gain_ref[...], cosine, sine)
+            spun = turn(unit * gain, cosine, sine)
             q_ref[at] = (spun[:, :inner].astype(BF16) * HD**-0.5).astype(BF16)
             k_ref[at] = spun[:, inner : inner + HD].astype(BF16)
             ones = jnp.broadcast_to(jnp.where(lane == 0, 1.0, 0.0), (BLOCK, HD)).astype(BF16)
             v_ref[at] = jnp.concatenate([x[:, inner + HD :].astype(BF16), ones], 1)
 
-        def hop(step, carry):
+        def pass_on(step):
             right, left = pos + step, pos - step
 
             @pl.when(right < length)
@@ -552,6 +596,7 @@
                 def _():
                     send(left, side_sem, pos, 1 - core)
 
+        def use_both(step):
             def side(k, c):
                 p = pos + (1 - 2 * k) * step
 
@@ -563,13 +608,24 @@
                 return c
 
             lax.fori_loop(0, 2, side, 0)
+
+        pass_on(0)
+        prepare()
+
+        def hop(step, carry):
+            use_both(step)
+            pass_on(step + 1)
             return carry
 
-        pltpu.make_async_copy(wa_ref, wa, load_sem.at[0]).wait()
-        lax.fori_loop(0, length, hop, 0)
-        keep = pltpu.make_async_copy(all_ref, one_ref, load_sem.at[2])
+        lax.fori_loop(0, here.last, hop, 0)
+        n = len(self.grads.scratch)
+        held = rest[n:]
+        p_ref = held[0]
+        grads = self.grads.run(here, og_ref, gr_ref, *rest[:n])
+        next(grads)
+        use_both(here.last)
+        keep = pltpu.make_async_copy(all_ref, one_ref, load_sem.at[4])
         keep.start()
-        pltpu.make_async_copy(wo_ref, wo, load_sem.at[1]).wait()
 
         def attend(i):
             at = pl.ds(pl.multiple_of(i * BLOCK, BLOCK), BLOCK)
@@ -577,7 +633,7 @@
             stacked = jnp.concatenate([query[:, h * HD : (h + 1) * HD] for h in range(heads)], 0)
             acc_ref[...] = jnp.zeros_like(acc_ref)
             index = i * BLOCK + lax.broadcasted_iota(jnp.int32, (BLOCK, 1), 0)
-            start = index - pos_ref[at]
+            start = index - place_ref[at, :1]
 
             def keys(j, c):
                 cols = pl.ds(pl.multiple_of(j * BLOCK, BLOCK), BLOCK)
@@ -600,10 +656,6 @@
             ctx_ref[at] = jnp.concatenate(outs, 1)
             lse_ref[i] = jnp.concatenate(logs, 1)
 
-        n = len(self.grads.scratch)
-        held = rest[n:]
-        p_ref, width = held[0], tok_ref.shape[1]
-
         def multiply(p):
             attend(p)
             at = pl.ds(pl.multiple_of(p * BLOCK, BLOCK), BLOCK)
@@ -615,7 +667,7 @@
 
             lax.fori_loop(0, width // 512, body, 0)
 
-        weave([self.grads.run(here, og_ref, gr_ref, *rest[:n]), line_sum(here, rows, multiply, branch_ref, *held)])
+        weave([line_sum(here, rows, multiply, branch_ref, *held), grads])
 
         def body(r, carry):
             at = pl.ds(pl.multiple_of(r * 32, 32), 32)
@@ -822,12 +874,12 @@
 def stack_lanes(x, heads):
     return jnp.concatenate([x[h * HD:(h + 1) * HD] for h in range(heads)], 1)
 
-def attend_back_kernel(heads, proj_ref, cos_ref, sin_ref, gain_ref, pos_ref, ctx_ref, grad_ref, lse_ref,
+def attend_back_kernel(heads, proj_ref, cos_ref, sin_ref, qgain_ref, kgain_ref, pos_ref, ctx_ref, grad_ref, lse_ref,
                        out_ref, sums_ref, k_ref, kt_ref, v_ref, dk_ref, dv_ref, dq_ref):
     width = heads * HD
     scale = HD ** -0.5
     count = proj_ref.shape[0] // BLOCK
-    gain = gain_ref[...]
+    gain = jnp.concatenate([qgain_ref[...]] * heads + [kgain_ref[...], jnp.ones((1, HD), F32)], 1)
     def prepare(i, carry):
         rows = pl.ds(pl.multiple_of(i * BLOCK, BLOCK), BLOCK)
         x = proj_ref[rows, width:]
@@ -901,19 +953,19 @@
         return carry
     lax.fori_loop(0, count, finish, 0)
 
-def attend_back(proj, cosine, sine, gain, positions, context, grad_context, lse, heads):
+def attend_back(proj, cosine, sine, query_gain, key_gain, positions, context, grad_context, lse, heads):
     size = proj.shape[0]
     count = size // BLOCK
     vm = pl.BlockSpec(memory_space=pltpu.VMEM)
     return pl.pallas_call(
         functools.partial(attend_back_kernel, heads),
         out_shape=(jax.ShapeDtypeStruct(proj.shape, BF16), jax.ShapeDtypeStruct((1, proj.shape[1]), F32)),
-        in_specs=[vm] * 8, out_specs=(vm, vm),
+        in_specs=[vm] * 9, out_specs=(vm, vm),
         scratch_shapes=[pltpu.VMEM((size, HD), BF16), pltpu.VMEM((count, HD, BLOCK), BF16), pltpu.VMEM((size, HD), BF16),
                         pltpu.VMEM((size, HD), F32), pltpu.VMEM((size, HD), F32), pltpu.VMEM((HD, heads * BLOCK), F32)],
         compiler_params=pltpu.CompilerParams(vmem_limit_bytes=40 << 20),
         cost_estimate=pl.CostEstimate(flops=1, bytes_accessed=1, transcendentals=0),
-    )(proj, cosine, sine, gain, positions.reshape(count, 1, BLOCK), context, grad_context, lse)
+    )(proj, cosine, sine, query_gain[None], key_gain[None], positions.reshape(count, 1, BLOCK), context, grad_context, lse)
 
 
 def matmul(left, right):
@@ -926,13 +978,6 @@
 
 def matmul_right_t(left, right):
     return lax.dot_general(left, right, (((1,), (1,)), ((), ())), preferred_element_type=F32)
-
-
-def rope_tables(position_row):
-    half = HD // 2
-    freq = ROPE_BASE ** (-jnp.arange(half, dtype=F32) / half)
-    angle = position_row.astype(F32)[:, None] * freq[None, :]
-    return jnp.tile(jnp.cos(angle), (1, 4)), jnp.tile(jnp.sin(angle), (1, 4))
 
 
 def norm_back(grad_normed, unit, inverse, gain):
@@ -969,19 +1014,21 @@
     share = members // KV
     group = lax.axis_index("mp") // share
 
-    tokens_f = tokens.astype(F32)
-    inv_one = lax.rsqrt(jnp.mean(tokens_f * tokens_f, -1, keepdims=True) + EPSILON)
-    normed_one = tokens_f * inv_one
-    key_cols = lax.dynamic_slice_in_dim(w_key, group * HD, HD, 1)
-    value_cols = lax.dynamic_slice_in_dim(w_value, group * HD, HD, 1)
-    w_attn = jnp.concatenate([w_query, key_cols, value_cols], 1)
-    cosine, sine = rope_tables(positions)
-    gain = jnp.concatenate([jnp.tile(query_gain, heads), key_gain, jnp.ones(HD, F32)])[None]
-
-    rows_one, projected, context, lse, grad_rows, attn_branch, h_two = together(
+    rows_one, projected, context, lse, grad_rows, attn_branch, h_two, cosine, sine = together(
         [
             Forward(
-                tokens, out_grad, attn_gain, ffn_gain, w_attn, w_output, cosine, sine, gain, positions, members
+                tokens,
+                out_grad,
+                attn_gain,
+                ffn_gain,
+                query_gain,
+                key_gain,
+                w_query,
+                w_key,
+                w_value,
+                w_output,
+                positions,
+                members,
             )
         ],
         members,
@@ -992,16 +1039,23 @@
     rows_two, hidden, grad_gate, grad_up = together(
         [GatherFfn(h_two, grad_rows, w_gate, w_up, w_down, members)], members, parts, 5, 58
     )
+    rows_two, tokens_late, w_key, w_value = after(rows_two, tokens, w_key, w_value)
+    tokens_f = tokens_late.astype(F32)
+    inv_one = lax.rsqrt(jnp.mean(tokens_f * tokens_f, -1, keepdims=True) + EPSILON)
+    normed_one = tokens_f * inv_one
+    key_cols = lax.dynamic_slice_in_dim(w_key, group * HD, HD, 1)
+    value_cols = lax.dynamic_slice_in_dim(w_value, group * HD, HD, 1)
+    w_attn = jnp.concatenate([w_query, key_cols, value_cols], 1)
     residual_mid = tokens_f + attn_branch
     inv_two = lax.rsqrt(jnp.mean(residual_mid * residual_mid, -1, keepdims=True) + EPSILON)
     normed_two = residual_mid * inv_two
     ffn_parts = (
+        matmul_left_t(hidden, grad_rows).astype(BF16),
         matmul_left_t(rows_two, grad_gate).astype(BF16),
         matmul_left_t(rows_two, grad_up).astype(BF16),
     )
     ffn_parts, grad_gate, grad_up, hidden = lax.optimization_barrier((ffn_parts, grad_gate, grad_up, hidden))
-    grad_w_gate, grad_w_up = lax.psum(ffn_parts, "dp")
-    down_part = matmul_left_t(hidden, grad_rows).astype(BF16)
+    grad_w_down, grad_w_gate, grad_w_up = lax.psum(ffn_parts, "dp")
 
     grad_h_two = together(
         [Scatter([(grad_gate, w_gate, True), (grad_up, w_up, True)], members)],
@@ -1020,7 +1074,7 @@
     )
     grad_context = matmul_right_t(grad_attn_rows, w_output).astype(BF16)
     grad_proj, gain_sums = attend_back(
-        projected, cosine, sine, gain, positions, context, grad_context, lse, heads
+        projected, cosine, sine, query_gain, key_gain, positions, context, grad_context, lse, heads
     )
     output_part = matmul_left_t(context, grad_attn_rows).astype(BF16)
     grad_w_attn = matmul_left_t(rows_one, grad_proj)
@@ -1040,13 +1094,12 @@
     small_rows = jnp.pad(small, (0, extra * 2 * HD - small.shape[0])).reshape(extra, 2 * HD)
     kv_part = jnp.concatenate([grad_w_attn[:, query_width:], small_rows], 0).astype(BF16)
     query_part = grad_w_attn[:, :query_width].astype(BF16)
-    grad_w_key, grad_w_value, small_sum, grad_h_one, grad_w_output, grad_w_query, grad_w_down = together(
+    grad_w_key, grad_w_value, small_sum, grad_h_one, grad_w_output, grad_w_query = together(
         [
             KeyValue(kv_part, width, members, parts),
             Scatter([(grad_proj, w_attn, True)], members),
             Across(output_part, parts, (False,), 2),
             Across(query_part, parts, (True,), 2),
-            Across(down_part, parts, (False, True), 2),
         ],
         members,
         parts,

time: 544 us -> 496 us (0.912)
  Pallas kernels: 437 us -> 395 us
  local copies, waits for them, and re-layouts: 12.4 us -> 5.76 us
    pallas_call x5, Pallas kernels: 419 us -> 377 us  [together(): pl.pallas_call(kernel, out_shape=[o for s in steps for o, _ in s.outputs]...]
where the time goes in v4:
time: 496 us; the launch traced here: 487 us
  Pallas kernels  395 us (80%)
  matrix products  36.3 us (7%)
  other arithmetic  33 us (7%)
  between operations  16.7 us (3%)
  local copies, waits for them, and re-layouts  5.76 us (1%)
    pallas_call x5, Pallas kernels, together(): pl.pallas_call(kernel, out_shape=[o for s in steps for o, _ in s.outputs]...  377 us
    dot_general x5, matrix products, matmul_left_t(): lax.dot_general(left, right, (((0,), (0,)), ((), ())), preferred_element_...  32.7 us
    pallas_call x1, Pallas kernels, attend_back(): pl.pallas_call(functools.partial(attend_back_kernel, heads), out_shape=(j...  17.7 us
  transfers between devices with their start and end apart: 1, of which 0 were waited for; matrix products, arithmetic and copies ran while one was open for 8% of the time, Pallas kernels for 55%

profile of v4, /device:TPU:10, one launch (start us, length us, event | category | flops | bytes accessed | tf_op | source)
XLA Modules:
  0.0 486.9 jit_solution(12598832372139143046)
XLA Ops:
  7.2 89.8 %shard_map.262 = (bf16[1024,2048]{1,0:T(8,128)(2,1)}, f32[1024,384]{1,0:T(8,128)}, bf16[1024,256]{1,0:T(8,128)(2,1)}, f32[4,1,1024]{2,1,0:T(1,128)}, bf16[1024,2...) custom-call(bf16[128,2048]{1,0:T(8,128)(2,1)} %refs_0_.1, ...), custom_call_target="tpu_custom_call" | custom-call | flops 1 | bytes 1 | tf_op jit(solution)/shard_map/pallas_call | solution.py:827
  97.0 38.9 %shard_map.263 = (bf16[1024,2048]{1,0:T(8,128)(2,1)}, bf16[1024,1024]{1,0:T(8,128)(2,1)}, bf16[1024,1024]{1,0:T(8,128)(2,1)}, bf16[1024,1024]{1,0:T(8,128)(2,1)}) custom-call(bf16[128,2048]{1,0:T(8,128)(2,1)} %get-tuple-element.48.refs_0_, bf16[1024,2048]{1,0:T(8,128)(2,1)} %get-tuple-element.49.refs_1_, bf16[2048,1024]{1,0:T(8,128)(2,1)} %refs_2_.4, ...), custom_call_target="tpu_custom_call" | custom-call | flops 1 | bytes 1 | tf_op jit(solution)/shard_map/pallas_call | solution.py:827
  136.0 9.6 %convolution_convert_fusion = bf16[2048,1024]{1,0:T(8,128)(2,1)} fusion(bf16[1024,2048]{1,0:T(8,128)(2,1)} %get-tuple-element.54, bf16[1024,1024]{1,0:T(8,128)(2,1)} %get-tuple-element.58.refs_1_), kind=kOutput, calls=%fused_computation | convolution fusion | flops 4297064448 | bytes 10485760 | tf_op jit(solution)/shard_map/dot_general | solution.py:976
  145.6 6.2 %convolution_convert_fusion.1 = bf16[2048,1024]{1,0:T(8,128)(2,1)} fusion(bf16[1024,2048]{1,0:T(8,128)(2,1)S(1)} %copy-done.30, bf16[1024,1024]{1,0:T(8,128)(2,1)S(1)} %copy-done.23), kind=kOutput, calls=%fused_computation.1 | convolution fusion | flops 4297064448 | bytes 10485760 | tf_op jit(solution)/shard_map/dot_general | solution.py:976
  151.8 6.2 %convolution_convert_fusion.2 = bf16[1024,2048]{1,0:T(8,128)(2,1)} fusion(bf16[1024,1024]{1,0:T(8,128)(2,1)S(1)} %copy-done, bf16[1024,2048]{1,0:T(8,128)(2,1)S(1)} %copy-done.21), kind=kOutput, calls=%fused_computation.2 | convolution fusion | flops 4297064448 | bytes 10485760 | tf_op jit(solution)/shard_map/dot_general | solution.py:976
  158.1 60.1 %shard_map.264 = f32[128,2048]{1,0:T(8,128)} custom-call(bf16[1024,1024]{1,0:T(8,128)(2,1)} %get-tuple-element.57.refs_0_, bf16[1024,1024]{1,0:T(8,128)(2,1)} %get-tuple-element.58.refs_1_, bf16[2048,1024]{1,0:T(8,128)(2,1)} %refs_2_.4, bf16[2048,1024]{1,0:T(8,128)(2,1)} %refs_3_.3), custom_call_target="tpu_custom_call" | custom-call | flops 1 | bytes 1 | tf_op jit(solution)/shard_map/pallas_call | solution.py:827
  218.3 0.2 multiply_reduce_fusion.5
  218.5 2.9 multiply_reduce_fusion.3
  221.4 0.5 fusion.10.refs_0_
  221.9 52.7 %shard_map.265 = (bf16[1024,2048]{1,0:T(8,128)(2,1)}, f32[128,2048]{1,0:T(8,128)S(1)}) custom-call(bf16[128,2048]{1,0:T(8,128)(2,1)S(1)} %fusion.10.refs_0_, bf16[1024,1024]{1,0:T(8,128)(2,1)S(1)} %copy-done, bf16[1024,2048]{1,0:T(8,128)(2,1)} %refs_2_.5), custom_call_target="tpu_custom_call" | custom-call | flops 1 | bytes 1 | tf_op jit(solution)/shard_map/pallas_call | solution.py:827
  274.7 3.6 convolution_convert_fusion.4.grad_ref
  278.4 17.7 %shard_map.266 = (bf16[1024,384]{1,0:T(8,128)(2,1)S(1)}, f32[1,384]{1,0:T(1,128)S(1)}) custom-call(f32[1024,384]{1,0:T(8,128)S(1)} %copy-done.1, f32[1024,128]{1,0:T(8,128)S(1)} %copy-done.4, f32[1024,128]{1,0:T(8,128)S(1)} %copy-done.5, f32[1,64]{1,0:T(1,128)S(1)} %bitcast.35, f32[1,64]{1,0:T(1,128)S(1)} %bitcast.37, s32[4,1,256]{2,1,0:T(1,128)S(1)} %bitcast.33, ...), custom_call_target="tpu_custom_call" | custom-call | flops 1 | bytes 1 | tf_op jit(solution)/shard_map/pallas_call | solution.py:960
  296.2 2.0 constant_dynamic-slice_fusion
  298.2 6.2 %multiply_reduce_fusion = (f32[2048]{0:T(1024)S(1)}, bf16[2048,384]{1,0:T(8,128)(2,1)}, bf16[2048,384]{1,0:T(8,128)(2,1)S(1)}) fusion(bf16[2048,64]{1,0:T(8,128)(2,1)S(1)} %get-tuple-element.100, bf16[2048,64]{1,0:T(8,128)(2,1)S(1)} %get-tuple-element.101, bf16[2048,256]{1,0:T(8,128)(2,1)} %refs_6_.1, bf16[1024,2048]{1,0:T(8,128)(2,1)} %get-tuple-element.61, ...), kind=kOutput, calls=%fused_computation.3 | convolution fusion | flops 1618475008 | bytes 9707520 | tf_op jit(solution)/shard_map/dot_general | solution.py:976
  304.4 1.0 slice.49.refs_4_
  305.6 0.7 concatenate.12
  306.3 0.8 pad_maximum_fusion.1.refs_0_
  307.2 4.4 convolution_convert_fusion.3.refs_3_
  311.6 135.9 %shard_map.267 = (bf16[2048,512]{1,0:T(8,128)(2,1)}, bf16[2048,512]{1,0:T(8,128)(2,1)}, f32[64,128]{1,0:T(8,128)}, f32[128,2048]{1,0:T(8,128)}, bf16[256,2048]{1,0:T(8,128)(2,1)}, /*index=5*/bf16[2048,256]{1,0:T(8,128)(2,1)}) custom-call(bf16[2112,128]{1,0:T(8,128)(2,1)} %pad_maximum_fusion.1.refs_0_, bf16[1024,384]{1,0:T(8,128)(2,1)} %copy-done.2, ...), custom_call_target="tpu_custom_call" | custom-call | flops 1 | bytes 1 | tf_op jit(solution)/shard_map/pallas_call | solution.py:827
  447.5 4.3 convert_element_type.70
  451.8 2.6 convert_element_type.71
  454.5 1.5 convert_element_type.69
  456.0 1.6 convert_element_type.72
  457.5 0.5 slice.52
  458.8 0.3 fusion.4
  459.1 1.9 fusion.8
  461.0 0.6 pad_maximum_fusion.2
  461.6 0.6 fusion.11
  462.2 0.6 slice_bitcast_fusion
  462.8 6.8 %convert_element_type.73 = f32[2048,1024]{1,0:T(8,128)} convert(bf16[2048,1024]{1,0:T(8,128)(2,1)} %get-tuple-element.86) | non-fusion elementwise | flops 2097152 | bytes 12582912 | tf_op jit(solution)/shard_map/convert_element_type | solution.py:1129
  469.6 4.4 convert_element_type.74
  474.0 4.4 convert_element_type.75
  (77 shorter events, 0.4 us)
Async XLA Ops:
  7.2 455.6 %all-reduce.4.cloned.1.call-start = ((), (), s32[]{:S(2)}) async-start(), calls=%async_computation | async-start | bytes 25165824 | tf_op jit(solution)/shard_map/psum | solution.py:1058
  136.0 9.6 %copy-start.23 = (bf16[1024,1024]{1,0:T(8,128)(2,1)S(1)}, bf16[1024,1024]{1,0:T(8,128)(2,1)}, u32[]{:S(2)}) copy-start(bf16[1024,1024]{1,0:T(8,128)(2,1)} %get-tuple-element.57.refs_0_) | copy-start | bytes 6291460
  136.0 9.6 %copy-start.30 = (bf16[1024,2048]{1,0:T(8,128)(2,1)S(1)}, bf16[1024,2048]{1,0:T(8,128)(2,1)}, u32[]{:S(2)}) copy-start(bf16[1024,2048]{1,0:T(8,128)(2,1)} %get-tuple-element.54) | copy-start | bytes 12582916
  145.6 6.3 %copy-start = (bf16[1024,1024]{1,0:T(8,128)(2,1)S(1)}, bf16[1024,1024]{1,0:T(8,128)(2,1)}, u32[]{:S(2)}) copy-start(bf16[1024,1024]{1,0:T(8,128)(2,1)} %get-tuple-element.59.refs_1_) | copy-start | bytes 6291460
  145.6 6.3 %copy-start.21 = (bf16[1024,2048]{1,0:T(8,128)(2,1)S(1)}, bf16[1024,2048]{1,0:T(8,128)(2,1)}, u32[]{:S(2)}) copy-start(bf16[1024,2048]{1,0:T(8,128)(2,1)} %get-tuple-element.49.refs_1_) | copy-start | bytes 12582916
  158.1 60.2 %copy-start.10 = (bf16[128,2048]{1,0:T(8,128)(2,1)S(1)}, bf16[128,2048]{1,0:T(8,128)(2,1)}, u32[]{:S(2)}) copy-start(bf16[128,2048]{1,0:T(8,128)(2,1)} %refs_0_.1) | copy-start | bytes 1572868
  158.1 60.2 %copy-start.12 = (f32[128,2048]{1,0:T(8,128)S(1)}, f32[128,2048]{1,0:T(8,128)}, u32[]{:S(2)}) copy-start(f32[128,2048]{1,0:T(8,128)} %get-tuple-element.52) | copy-start | bytes 3145732
  158.1 60.4 %copy-start.27 = (f32[2048]{0:T(1024)S(1)}, f32[2048]{0:T(1024)}, u32[]{:S(2)}) copy-start(f32[2048]{0:T(1024)} %param.26) | copy-start | bytes 24580
  218.2 3.2 copy-start.14
  218.2 3.2 copy-start.16
  221.9 52.7 %copy-start.24 = (bf16[256,2048]{1,0:T(8,128)(2,1)S(1)}, bf16[256,2048]{1,0:T(8,128)(2,1)}, u32[]{:S(2)}) copy-start(bf16[256,2048]{1,0:T(8,128)(2,1)} %refs_9_.1) | copy-start | bytes 3145732
  274.6 3.7 copy-start.1
  274.6 3.7 copy-start.3
  274.7 3.7 copy-start.4
  274.7 3.7 copy-start.5
  274.7 3.7 copy-start.6
  274.7 3.7 copy-start.7
  274.7 3.7 copy-start.8
  274.7 3.7 copy-start.9
  296.1 8.2 %copy-start.2 = (bf16[1024,384]{1,0:T(8,128)(2,1)}, bf16[1024,384]{1,0:T(8,128)(2,1)S(1)}, u32[]{:S(2)}) copy-start(bf16[1024,384]{1,0:T(8,128)(2,1)S(1)} %get-tuple-element.68.refs_1_) | copy-start | bytes 2359300
  298.1 7.4 %copy-start.28 = (f32[2048]{0:T(1024)S(1)}, f32[2048]{0:T(1024)}, u32[]{:S(2)}) copy-start(f32[2048]{0:T(1024)} %param.25) | copy-start | bytes 24580
  447.5 4.4 copy-start.22
  451.8 2.7 copy-start.26
  451.8 4.1 copy-start.25
  454.5 3.1 copy-start.29
  454.5 4.3 copy-start.11
  454.5 4.3 copy-start.20
  454.5 4.6 copy-start.13
  454.5 4.6 copy-start.15
  454.5 4.6 copy-start.17
  462.8 6.8 %copy-start.19 = (bf16[2048,1024]{1,0:T(8,128)(2,1)S(1)}, bf16[2048,1024]{1,0:T(8,128)(2,1)}, u32[]{:S(2)}) copy-start(bf16[2048,1024]{1,0:T(8,128)(2,1)} %get-tuple-element.87) | copy-start | bytes 12582916
  469.6 4.4 copy-start.18
Sparse Core Ops, SparseCore 0:
  158.2 289.4 all-reduce.3

commit v5 on v4

--- a/solution.py
+++ b/solution.py
@@ -174,7 +174,7 @@
         total = members * rows
         sems = pltpu.SemaphoreType.DMA((length,))
         self.units = units
-        self.inputs = [(v, ANY) for v in (x, grad_rows, w_gate, w_up, w_down)]
+        self.inputs = [(v, ANY) for v in (x, grad_rows)] + [(v, ANY) for v in (w_gate, w_up, w_down)]
         self.outputs = [
             (jax.ShapeDtypeStruct((total, width), BF16), VMEM),
             (jax.ShapeDtypeStruct((total, units), BF16), VMEM),
@@ -809,7 +809,16 @@
         small_ref[...] = small
 
 
-def together(steps, members, parts, collective_id, vmem=48):
+def held_bytes(shape, dtype):
+    *lead, rows, columns = (1,) + tuple(shape)
+    return int(np.prod(lead)) * -(-rows // 8) * 8 * -(-columns // 128) * 128 * jnp.dtype(dtype).itemsize
+
+
+def together(steps, members, parts, collective_id, whole=False, spare=6):
+    need = 0
+    for s in steps:
+        need += sum(held_bytes(x.shape, x.dtype) for x, m in s.inputs + s.outputs if m is VMEM)
+        need += sum(held_bytes(h.shape, h.dtype) for h in s.scratch if h is not pltpu.SemaphoreType.DMA and h.memory_space == pltpu.VMEM)
     counts = [(len(s.inputs), len(s.outputs), len(s.scratch)) for s in steps]
 
     def kernel(*refs):
@@ -831,7 +840,7 @@
         out_specs=[m for s in steps for _, m in s.outputs],
         scratch_shapes=[h for s in steps for h in s.scratch],
         compiler_params=pltpu.CompilerParams(
-            collective_id=collective_id, has_side_effects=True, vmem_limit_bytes=vmem << 20
+            collective_id=collective_id, has_side_effects=True, vmem_limit_bytes=58 << 20 if whole else need + (spare << 20)
         ),
         cost_estimate=pl.CostEstimate(flops=1, bytes_accessed=1, transcendentals=0),
     )(*[x for s in steps for x, _ in s.inputs])
@@ -842,6 +851,9 @@
 
 def dot_nt(a, b):
     return lax.dot_general(a, b, (((1,), (1,)), ((), ())), preferred_element_type=F32)
+
+def dot_tn(a, b):
+    return lax.dot_general(a, b, (((0,), (0,)), ((), ())), preferred_element_type=F32)
 
 def group_mean(x):
     width = x.shape[1]
@@ -1034,10 +1046,10 @@
         members,
         parts,
         0,
-        58,
+        True,
     )
     rows_two, hidden, grad_gate, grad_up = together(
-        [GatherFfn(h_two, grad_rows, w_gate, w_up, w_down, members)], members, parts, 5, 58
+        [GatherFfn(h_two, grad_rows, w_gate, w_up, w_down, members)], members, parts, 5, False, 14
     )
     rows_two, tokens_late, w_key, w_value = after(rows_two, tokens, w_key, w_value)
     tokens_f = tokens_late.astype(F32)
@@ -1062,7 +1074,7 @@
         members,
         parts,
         6,
-        58,
+        True,
     )[0]
     grad_ffn_gain = jnp.sum(grad_h_two * normed_two, 0)
     grad_mid = out_grad.astype(F32) + norm_back(grad_h_two, normed_two, inv_two, ffn_gain)
@@ -1104,7 +1116,6 @@
         members,
         parts,
         3,
-        58,
     )
     small_sum = small_sum.reshape(-1)
     entry_count = tokens.size * parts * members

time: 496 us -> 483 us (0.974)
  matrix products: 36.3 us -> 28.3 us
  Pallas kernels: 395 us -> 388 us
    pallas_call x5, Pallas kernels: 377 us -> 370 us  [together(): pl.pallas_call(kernel, out_shape=[o for s in steps for o, _ in s.outputs]...]
    dot_general x5, matrix products: 32.7 us -> 27 us  [matmul_left_t(): lax.dot_general(left, right, (((0,), (0,)), ((), ())), preferred_element_...]
  transfers between devices with their start and end apart: 1 -> 1, of which waited for: 0 -> 0; matrix products, arithmetic and copies ran while one was open for 8% -> 7% of each run, Pallas kernels for 55% -> 56%
where the time goes in v5:
time: 483 us; the launch traced here: 474 us
  Pallas kernels  388 us (80%)
  other arithmetic  32.7 us (7%)
  matrix products  28.3 us (6%)
  between operations  16.7 us (3%)
  local copies, waits for them, and re-layouts  8.59 us (2%)
    pallas_call x5, Pallas kernels, together(): pl.pallas_call(kernel, out_shape=[o for s in steps for o, _ in s.outputs]...  370 us
    dot_general x5, matrix products, matmul_left_t(): lax.dot_general(left, right, (((0,), (0,)), ((), ())), preferred_element_...  27 us
    pallas_call x1, Pallas kernels, attend_back(): pl.pallas_call(functools.partial(attend_back_kernel, heads), out_shape=(j...  17.7 us
  transfers between devices with their start and end apart: 1, of which 0 were waited for; matrix products, arithmetic and copies ran while one was open for 7% of the time, Pallas kernels for 56%

profile of v5, /device:TPU:10, one launch (start us, length us, event | category | flops | bytes accessed | tf_op | source)
XLA Modules:
  0.0 474.2 jit_solution(4728678621847678446)
XLA Ops:
  7.2 89.7 %shard_map.262 = (bf16[1024,2048]{1,0:T(8,128)(2,1)}, f32[1024,384]{1,0:T(8,128)}, bf16[1024,256]{1,0:T(8,128)(2,1)}, f32[4,1,1024]{2,1,0:T(1,128)}, bf16[1024,2...) custom-call(bf16[128,2048]{1,0:T(8,128)(2,1)} %refs_0_.1, ...), custom_call_target="tpu_custom_call" | custom-call | flops 1 | bytes 1 | tf_op jit(solution)/shard_map/pallas_call | solution.py:836
  96.9 1.0 copy-done.9
  98.0 34.8 %shard_map.263 = (bf16[1024,2048]{1,0:T(8,128)(2,1)S(1)}, bf16[1024,1024]{1,0:T(8,128)(2,1)S(1)}, bf16[1024,1024]{1,0:T(8,128)(2,1)S(1)}, bf16[1024,1024]{1,0:T(8,128)(2,1)S(1)}) custom-call(bf16[128,2048]{1,0:T(8,128)(2,1)S(1)} %copy-done.9, bf16[1024,2048]{1,0:T(8,128)(2,1)} %get-tuple-element.49.refs_1_, bf16[2048,1024]{1,0:T(8,128)(2,1)} %refs_2_.4, ...), custom_call_target="tpu_custom_call" | custom-call | flops 1 | bytes 1 | tf_op jit(solution)/shard_map/pallas_call | solution.py:836
  132.8 6.1 %convolution_convert_fusion = bf16[2048,1024]{1,0:T(8,128)(2,1)} fusion(bf16[1024,2048]{1,0:T(8,128)(2,1)S(1)} %get-tuple-element.54, bf16[1024,1024]{1,0:T(8,128)(2,1)S(1)} %get-tuple-element.58.refs_1_), kind=kOutput, calls=%fused_computation | convolution fusion | flops 4297064448 | bytes 10485760 | tf_op jit(solution)/shard_map/dot_general | solution.py:988
  139.0 6.1 %convolution_convert_fusion.1 = bf16[2048,1024]{1,0:T(8,128)(2,1)} fusion(bf16[1024,2048]{1,0:T(8,128)(2,1)S(1)} %get-tuple-element.54, bf16[1024,1024]{1,0:T(8,128)(2,1)S(1)} %get-tuple-element.57.refs_0_), kind=kOutput, calls=%fused_computation.1 | convolution fusion | flops 4297064448 | bytes 10485760 | tf_op jit(solution)/shard_map/dot_general | solution.py:988
  145.1 6.2 %convolution_convert_fusion.2 = bf16[1024,2048]{1,0:T(8,128)(2,1)} fusion(bf16[1024,1024]{1,0:T(8,128)(2,1)S(1)} %get-tuple-element.59.refs_1_, bf16[1024,2048]{1,0:T(8,128)(2,1)S(1)} %copy-done.24), kind=kOutput, calls=%fused_computation.2 | convolution fusion | flops 4297064448 | bytes 10485760 | tf_op jit(solution)/shard_map/dot_general | solution.py:988
  151.4 60.1 %shard_map.264 = f32[128,2048]{1,0:T(8,128)} custom-call(bf16[1024,1024]{1,0:T(8,128)(2,1)} %copy-done.1, bf16[1024,1024]{1,0:T(8,128)(2,1)} %copy-done.2, bf16[2048,1024]{1,0:T(8,128)(2,1)} %refs_2_.4, bf16[2048,1024]{1,0:T(8,128)(2,1)} %refs_3_.3), custom_call_target="tpu_custom_call" | custom-call | flops 1 | bytes 1 | tf_op jit(solution)/shard_map/pallas_call | solution.py:836
  211.8 2.9 multiply_reduce_fusion.3
  214.7 1.7 fusion.10.refs_0_
  216.4 52.5 %shard_map.265 = (bf16[1024,2048]{1,0:T(8,128)(2,1)S(1)}, f32[128,2048]{1,0:T(8,128)S(1)}) custom-call(bf16[128,2048]{1,0:T(8,128)(2,1)S(1)} %fusion.10.refs_0_, bf16[1024,1024]{1,0:T(8,128)(2,1)S(1)} %get-tuple-element.59.refs_1_, bf16[1024,2048]{1,0:T(8,128)(2,1)S(1)} %copy-done), custom_call_target="tpu_custom_call" | custom-call | flops 1 | bytes 1 | tf_op jit(solution)/shard_map/pallas_call | solution.py:836
  269.0 1.3 convolution_convert_fusion.4.grad_ref
  270.4 1.2 copy-done.14
  272.7 17.7 %shard_map.266 = (bf16[1024,384]{1,0:T(8,128)(2,1)S(1)}, f32[1,384]{1,0:T(1,128)S(1)}) custom-call(f32[1024,384]{1,0:T(8,128)S(1)} %copy-done.3, f32[1024,128]{1,0:T(8,128)S(1)} %copy-done.7, f32[1024,128]{1,0:T(8,128)S(1)} %copy-done.8, f32[1,64]{1,0:T(1,128)S(1)} %bitcast.37, f32[1,64]{1,0:T(1,128)S(1)} %bitcast.39, s32[4,1,256]{2,1,0:T(1,128)S(1)} %bitcast.33, ...), custom_call_target="tpu_custom_call" | custom-call | flops 1 | bytes 1 | tf_op jit(solution)/shard_map/pallas_call | solution.py:972
  290.5 1.6 constant_dynamic-slice_fusion
  292.1 4.8 %multiply_reduce_fusion = (f32[2048]{0:T(1024)S(1)}, bf16[2048,384]{1,0:T(8,128)(2,1)S(1)}, bf16[2048,384]{1,0:T(8,128)(2,1)S(1)}) fusion(bf16[2048,64]{1,0:T(8,128)(2,1)S(1)} %get-tuple-element.100, bf16[2048,64]{1,0:T(8,128)(2,1)S(1)} %get-tuple-element.101, bf16[2048,256]{1,0:T(8,128)(2,1)S(1)} %copy-done.26, bf16[1024,2048]{1,0:T(8,128)(2,1)} %get-tuple-element.61, ...), kind=kOutput, calls=%fused_computation.3 | convolution fusion | flops 1618475008 | bytes 9707520 | tf_op jit(solution)/shard_map/dot_general | solution.py:988
  296.9 0.8 slice.47
  298.0 0.7 concatenate.12
  298.7 1.1 pad_maximum_fusion.1.refs_0_
  299.9 3.7 convolution_convert_fusion.3.refs_3_
  303.6 133.1 %shard_map.267 = (bf16[2048,512]{1,0:T(8,128)(2,1)S(1)}, bf16[2048,512]{1,0:T(8,128)(2,1)S(1)}, f32[64,128]{1,0:T(8,128)S(1)}, f32[128,2048]{1,0:T(8,128)S(1)}, ...) custom-call(bf16[2112,128]{1,0:T(8,128)(2,1)S(1)} %pad_maximum_fusion.1.refs_0_, ...), custom_call_target="tpu_custom_call" | custom-call | flops 1 | bytes 1 | tf_op jit(solution)/shard_map/pallas_call | solution.py:836
  436.6 2.6 convert_element_type.70
  439.3 2.6 convert_element_type.71
  441.9 1.5 convert_element_type.69
  443.4 1.6 convert_element_type.72
  444.9 0.5 slice.52
  446.5 1.9 fusion.8
  448.4 0.6 pad_maximum_fusion.2
  448.9 0.6 fusion.11
  449.5 0.6 slice_bitcast_fusion
  450.1 6.8 %convert_element_type.73 = f32[2048,1024]{1,0:T(8,128)} convert(bf16[2048,1024]{1,0:T(8,128)(2,1)} %get-tuple-element.86) | non-fusion elementwise | flops 2097152 | bytes 12582912 | tf_op jit(solution)/shard_map/convert_element_type | solution.py:1140
  456.9 4.4 convert_element_type.74
  461.4 4.4 convert_element_type.75
  (73 shorter events, 2.1 us)
Async XLA Ops:
  7.2 442.9 %all-reduce.4.cloned.1.call-start = ((), (), s32[]{:S(2)}) async-start(), calls=%async_computation | async-start | bytes 25165824 | tf_op jit(solution)/shard_map/psum | solution.py:1070
  96.9 1.0 copy-start.9
  132.8 6.2 %copy-start.2 = (bf16[1024,1024]{1,0:T(8,128)(2,1)}, bf16[1024,1024]{1,0:T(8,128)(2,1)S(1)}, u32[]{:S(2)}) copy-start(bf16[1024,1024]{1,0:T(8,128)(2,1)S(1)} %get-tuple-element.58.refs_1_) | copy-start | bytes 6291460
  132.8 6.1 %copy-start.1 = (bf16[1024,1024]{1,0:T(8,128)(2,1)}, bf16[1024,1024]{1,0:T(8,128)(2,1)S(1)}, u32[]{:S(2)}) copy-start(bf16[1024,1024]{1,0:T(8,128)(2,1)S(1)} %get-tuple-element.57.refs_0_) | copy-start | bytes 6291460
  139.0 6.1 %copy-start.24 = (bf16[1024,2048]{1,0:T(8,128)(2,1)S(1)}, bf16[1024,2048]{1,0:T(8,128)(2,1)}, u32[]{:S(2)}) copy-start(bf16[1024,2048]{1,0:T(8,128)(2,1)} %get-tuple-element.49.refs_1_) | copy-start | bytes 12582916
  151.3 60.2 %copy-start.15 = (bf16[128,2048]{1,0:T(8,128)(2,1)S(1)}, bf16[128,2048]{1,0:T(8,128)(2,1)}, u32[]{:S(2)}) copy-start(bf16[128,2048]{1,0:T(8,128)(2,1)} %refs_0_.1) | copy-start | bytes 1572868
  151.3 60.2 %copy-start.17 = (f32[128,2048]{1,0:T(8,128)S(1)}, f32[128,2048]{1,0:T(8,128)}, u32[]{:S(2)}) copy-start(f32[128,2048]{1,0:T(8,128)} %get-tuple-element.52) | copy-start | bytes 3145732
  151.3 60.4 %copy-start.27 = (f32[2048]{0:T(1024)S(1)}, f32[2048]{0:T(1024)}, u32[]{:S(2)}) copy-start(f32[2048]{0:T(1024)} %param.26) | copy-start | bytes 24580
  151.4 63.4 %copy-start.20 = (bf16[128,2048]{1,0:T(8,128)(2,1)S(1)}, bf16[128,2048]{1,0:T(8,128)(2,1)}, u32[]{:S(2)}) copy-start(bf16[128,2048]{1,0:T(8,128)(2,1)} %refs_1_.1) | copy-start | bytes 1572868
  211.5 4.9 %copy-start = (bf16[1024,2048]{1,0:T(8,128)(2,1)S(1)}, bf16[1024,2048]{1,0:T(8,128)(2,1)}, u32[]{:S(2)}) copy-start(bf16[1024,2048]{1,0:T(8,128)(2,1)} %refs_2_.5) | copy-start | bytes 12582916
  216.4 52.5 %copy-start.25 = (bf16[256,2048]{1,0:T(8,128)(2,1)S(1)}, bf16[256,2048]{1,0:T(8,128)(2,1)}, u32[]{:S(2)}) copy-start(bf16[256,2048]{1,0:T(8,128)(2,1)} %refs_9_.1) | copy-start | bytes 3145732
  268.9 1.4 copy-start.4
  268.9 2.7 copy-start.14
  269.0 2.6 copy-start.3
  269.0 3.1 copy-start.6
  269.0 3.5 copy-start.7
  269.0 3.7 copy-start.8
  269.0 3.7 copy-start.10
  269.0 3.7 copy-start.11
  269.0 3.7 copy-start.12
  269.0 3.7 copy-start.13
  270.3 21.8 %copy-start.26 = (bf16[2048,256]{1,0:T(8,128)(2,1)S(1)}, bf16[2048,256]{1,0:T(8,128)(2,1)}, u32[]{:S(2)}) copy-start(bf16[2048,256]{1,0:T(8,128)(2,1)} %refs_6_.1) | copy-start | bytes 3145732
  292.1 5.9 %copy-start.28 = (f32[2048]{0:T(1024)S(1)}, f32[2048]{0:T(1024)}, u32[]{:S(2)}) copy-start(f32[2048]{0:T(1024)} %param.25) | copy-start | bytes 24580
  441.9 4.3 copy-start.16
  441.9 4.6 copy-start.5
  441.9 4.6 copy-start.18
  441.9 4.6 copy-start.19
  441.9 4.6 copy-start.21
  450.1 6.8 %copy-start.23 = (bf16[2048,1024]{1,0:T(8,128)(2,1)S(1)}, bf16[2048,1024]{1,0:T(8,128)(2,1)}, u32[]{:S(2)}) copy-start(bf16[2048,1024]{1,0:T(8,128)(2,1)} %get-tuple-element.87) | copy-start | bytes 12582916
  456.9 4.4 copy-start.22
Sparse Core Ops, SparseCore 0:
  151.4 289.3 all-reduce.3

commit v6 on v5

--- a/solution.py
+++ b/solution.py
@@ -95,59 +95,76 @@
         self.outputs = [(jax.ShapeDtypeStruct((members * x.shape[0],) + x.shape[1:], x.dtype), ANY)]
         self.scratch = [pltpu.SemaphoreType.DMA, sems, sems, sems, pltpu.SemaphoreType.DMA((members,))]
 
-    def run(self, here, x_ref, o_ref, own_sem, left_sem, right_sem, side_sem, recv_sem):
-        pos, core, length = here.pos, here.core, here.length
+    def run(self, here, *refs):
+        self.begin(here, *refs)
+        for step in range(1, here.length):
+            yield
+            self.hop(here, step, *refs)
+        yield
+        self.end(here, *refs)
+
+    def parts(self, here, x_ref, o_ref, own_sem, left_sem, right_sem, side_sem, recv_sem):
         rows = x_ref.shape[0]
 
         def block(p, c):
             return o_ref.at[pl.ds(pl.multiple_of((p * 2 + c) * rows, rows), rows)]
 
         def send(src, p, sem, to_p, to_c):
-            remote(src, block(p, core), sem.at[p], recv_sem.at[p * 2 + core], here.at(to_p, to_c)).start()
+            remote(src, block(p, here.core), sem.at[p], recv_sem.at[p * 2 + here.core], here.at(to_p, to_c)).start()
 
         def arrived(p, c):
             pltpu.make_async_copy(x_ref, block(p, c), recv_sem.at[p * 2 + c]).wait()
 
+        own = pltpu.make_async_copy(x_ref, block(here.pos, here.core), own_sem)
+        return block, send, arrived, own, left_sem, right_sem, side_sem
+
+    def begin(self, here, x_ref, *refs):
+        pos, core = here.pos, here.core
+        block, send, arrived, own, left_sem, right_sem, side_sem = self.parts(here, x_ref, *refs)
+
+        @pl.when(pos > 0)
+        def _():
+            send(x_ref, pos, left_sem, pos - 1, core)
+
+        @pl.when(pos < here.last)
+        def _():
+            send(x_ref, pos, right_sem, pos + 1, core)
+
+        send(x_ref, pos, side_sem, pos, 1 - core)
+        own.start()
+
+    def hop(self, here, step, x_ref, *refs):
+        pos, core = here.pos, here.core
+        block, send, arrived, own, left_sem, right_sem, side_sem = self.parts(here, x_ref, *refs)
+        right, left = pos + step, pos - step
+
+        @pl.when(right < here.length)
+        def _():
+            arrived(right, core)
+
+            @pl.when(pos > 0)
+            def _():
+                send(block(right, core), right, left_sem, pos - 1, core)
+
+            send(block(right, core), right, side_sem, pos, 1 - core)
+
+        @pl.when(left >= 0)
+        def _():
+            arrived(left, core)
+
+            @pl.when(pos < here.last)
+            def _():
+                send(block(left, core), left, right_sem, pos + 1, core)
+
+            send(block(left, core), left, side_sem, pos, 1 - core)
+
+    def end(self, here, x_ref, *refs):
+        pos, core = here.pos, here.core
+        block, send, arrived, own, left_sem, right_sem, side_sem = self.parts(here, x_ref, *refs)
+        own.wait()
+
         def sent(sem, p):
             pltpu.make_async_copy(x_ref, block(pos, core), sem.at[p]).wait()
-
-        @pl.when(pos > 0)
-        def _():
-            send(x_ref, pos, left_sem, pos - 1, core)
-
-        @pl.when(pos < here.last)
-        def _():
-            send(x_ref, pos, right_sem, pos + 1, core)
-
-        send(x_ref, pos, side_sem, pos, 1 - core)
-        own = pltpu.make_async_copy(x_ref, block(pos, core), own_sem)
-        own.start()
-        for step in range(1, length):
-            yield
-            right, left = pos + step, pos - step
-
-            @pl.when(right < length)
-            def _():
-                arrived(right, core)
-
-                @pl.when(pos > 0)
-                def _():
-                    send(block(right, core), right, left_sem, pos - 1, core)
-
-                send(block(right, core), right, side_sem, pos, 1 - core)
-
-            @pl.when(left >= 0)
-            def _():
-                arrived(left, core)
-
-                @pl.when(pos < here.last)
-                def _():
-                    send(block(left, core), left, right_sem, pos + 1, core)
-
-                send(block(left, core), left, side_sem, pos, 1 - core)
-
-        yield
-        own.wait()
 
         def drain(p, carry):
             arrived(p, 1 - core)
@@ -163,7 +180,7 @@
 
             return carry
 
-        lax.fori_loop(0, length, drain, 0)
+        lax.fori_loop(0, here.length, drain, 0)
 
 
 class GatherFfn(Step):
@@ -306,6 +323,16 @@
         self.scratch += [pltpu.SemaphoreType.DMA((len(terms),))] + line_sum_scratch(members, rows, width)
 
     def run(self, here, *refs):
+        total = self.begin(here, *refs)
+        for t in range(here.last):
+            total.fill(t)
+            yield
+            total.slot(t)
+        total.fill(here.last)
+        yield
+        total.end()
+
+    def begin(self, here, *refs):
         n = len(self.turned)
         m = len(self.inputs) - n
         lefts, refs = (refs[:m] * n)[:n], refs[m:]
@@ -332,7 +359,7 @@
 
         for load in loads:
             load.wait()
-        yield from line_sum(here, rows, multiply, o_ref, p_ref, *refs[2 * n + 3 :])
+        return LineSum(here, rows, multiply, o_ref, p_ref, *refs[2 * n + 3 :])
 
 
 def line_sum_scratch(members, rows, width):
@@ -342,111 +369,163 @@
     return held + [pltpu.SemaphoreType.DMA((length,))] * 6
 
 
-def line_sum(here, rows, multiply, o_ref, p_ref, side_buf, left_in, right_in,
-             side_send, side_recv, right_send, right_recv, left_send, left_recv):
-    pos, core, length, last, tile = here.pos, here.core, here.length, here.last, 32
-
-    def block(p, c):
-        return p_ref.at[pl.ds(pl.multiple_of((p * 2 + c) * rows, rows), rows)]
-
-    def side_copy(p):
-        return remote(block(p, 1 - core), side_buf.at[p], side_send.at[p], side_recv.at[p], here.at(pos, 1 - core))
-
-    def line_copy(p, right):
-        if right:
-            return remote(block(p, core), right_in.at[p], right_send.at[p], right_recv.at[p], here.at(pos + 1, core))
-        return remote(block(p, core), left_in.at[p], left_send.at[p], left_recv.at[p], here.at(pos - 1, core))
-
-    def make(p):
-        multiply(p)
-        side_copy(p).start()
-
-    def add(p, incoming, final):
+class LineSum:
+    def __init__(self, here, rows, multiply, o_ref, p_ref, side_buf, left_in, right_in,
+                 side_send, side_recv, right_send, right_recv, left_send, left_recv):
+        self.here, self.rows, self.multiply, self.o_ref, self.p_ref = here, rows, multiply, o_ref, p_ref
+        self.side_buf, self.left_in, self.right_in = side_buf, left_in, right_in
+        self.side, self.right, self.left = (side_send, side_recv), (right_send, right_recv), (left_send, left_recv)
+
+    def block(self, p, c):
+        return self.p_ref.at[pl.ds(pl.multiple_of((p * 2 + c) * self.rows, self.rows), self.rows)]
+
+    def side_copy(self, p):
+        here = self.here
+        sems = [s.at[p] for s in self.side]
+        return remote(self.block(p, 1 - here.core), self.side_buf.at[p], *sems, here.at(here.pos, 1 - here.core))
+
+    def line_copy(self, p, right):
+        here = self.here
+        buf, sems = (self.right_in, self.right) if right else (self.left_in, self.left)
+        to = here.at(here.pos + 1 if right else here.pos - 1, here.core)
+        return remote(self.block(p, here.core), buf.at[p], *[s.at[p] for s in sems], to)
+
+    def add(self, p, incoming, final):
+        tile, rows = 16, self.rows
+
         def body(r, carry):
             s = pl.ds(pl.multiple_of(r * tile, tile), tile)
-            mine = pl.ds(pl.multiple_of((p * 2 + core) * rows + r * tile, tile), tile)
-            total = p_ref[mine].astype(F32) + side_buf[p, s].astype(F32)
+            mine = pl.ds(pl.multiple_of((p * 2 + self.here.core) * rows + r * tile, tile), tile)
+            total = self.p_ref[mine].astype(F32) + self.side_buf[p, s].astype(F32)
             for ref in incoming:
                 total = total + ref[p, s].astype(F32)
             if final:
-                o_ref[s] = total
+                self.o_ref[s] = total
             else:
-                p_ref[mine] = total.astype(BF16)
+                self.p_ref[mine] = total.astype(BF16)
             return carry
 
         lax.fori_loop(0, rows // tile, body, 0)
 
-    def move(p, right, first, source):
-        side_copy(p).wait_recv()
+    def fill(self, t):
+        pos, last = self.here.pos, self.here.last
+
+        def side(k, carry):
+            own = t == last
+            p = jnp.where(own, pos, k * t + (1 - k) * (last - t))
+
+            @pl.when(jnp.where(own, 1 - k, (1 - 2 * k) * (p - pos)) > 0)
+            def _():
+                self.multiply(p)
+                self.side_copy(p).start()
+
+            return carry
+
+        lax.fori_loop(0, 2, side, 0)
+
+    def move(self, p, right, first, source):
+        self.side_copy(p).wait_recv()
 
         @pl.when(first)
         def _():
-            add(p, [], False)
+            self.add(p, [], False)
 
         @pl.when(jnp.logical_not(first))
         def _():
-            line_copy(p, right).wait_recv()
-            add(p, [source], False)
-
-        line_copy(p, right).start()
-
-    for t in range(last):
-
-        def side(k, carry):
-            p = k * t + (1 - k) * (last - t)
-
-            @pl.when((1 - 2 * k) * (p - pos) > 0)
-            def _():
-                make(p)
+            self.line_copy(p, right).wait_recv()
+            self.add(p, [source], False)
+
+        self.line_copy(p, right).start()
+
+    def slot(self, t):
+        pos, last = self.here.pos, self.here.last
+        right_p, left_p = last - t + pos, t - (last - pos)
+
+        @pl.when(t >= pos)
+        def _():
+            self.move(right_p, True, pos == 0, self.right_in)
+
+        @pl.when(left_p >= 0)
+        def _():
+            self.move(left_p, False, pos == last, self.left_in)
+
+    def end(self):
+        pos, last = self.here.pos, self.here.last
+        self.side_copy(pos).wait_recv()
+
+        @pl.when(pos == 0)
+        def _():
+            self.line_copy(pos, False).wait_recv()
+            self.add(pos, [self.left_in], True)
+
+        @pl.when(pos == last)
+        def _():
+            self.line_copy(pos, True).wait_recv()
+            self.add(pos, [self.right_in], True)
+
+        @pl.when((pos > 0) & (pos < last))
+        def _():
+            self.line_copy(pos, False).wait_recv()
+            self.line_copy(pos, True).wait_recv()
+            self.add(pos, [self.left_in, self.right_in], True)
+
+        def drain(p, carry):
+            self.side_copy(p).wait_send()
+
+            @pl.when(p > pos)
+            def _():
+                self.line_copy(p, True).wait_send()
+
+            @pl.when(p < pos)
+            def _():
+                self.line_copy(p, False).wait_send()
 
             return carry
 
-        lax.fori_loop(0, 2, side, 0)
+        lax.fori_loop(0, self.here.length, drain, 0)
+
+
+def rounds(here, total, hop=None):
+    def body(t, carry):
+        total.fill(t)
+
+        @pl.when(t < here.last)
+        def _():
+            if hop is not None:
+                hop(t + 1)
+            total.slot(t)
+
+        return carry
+
+    lax.fori_loop(0, here.length, body, 0)
+
+
+class ScatterAlone(Scatter):
+    def __init__(self, terms, members, gathered=None):
+        Scatter.__init__(self, terms, members)
+        self.other = None if gathered is None else Gather(gathered, members)
+        self.sizes = [len(v) for v in (self.inputs, self.outputs, self.scratch)]
+        if gathered is not None:
+            self.inputs = self.inputs + self.other.inputs
+            self.outputs = self.outputs + self.other.outputs
+            self.scratch = self.scratch + self.other.scratch
+
+    def run(self, here, *refs):
+        ends, mine, rest = [len(v) for v in (self.inputs, self.outputs, self.scratch)], [], []
+        for size, end in zip(self.sizes, ends):
+            mine += refs[:size]
+            rest += refs[size:end]
+            refs = refs[end:]
+        if self.other is not None:
+            self.other.begin(here, *rest)
+        all_inputs, self.inputs = self.inputs, self.inputs[: self.sizes[0]]
+        total = self.begin(here, *mine)
+        self.inputs = all_inputs
+        rounds(here, total, None if self.other is None else lambda step: self.other.hop(here, step, *rest))
+        total.end()
+        if self.other is not None:
+            self.other.end(here, *rest)
         yield
-        right_p, left_p = last - t + pos, t - (last - pos)
-
-        @pl.when(t >= pos)
-        def _():
-            move(right_p, True, pos == 0, right_in)
-
-        @pl.when(left_p >= 0)
-        def _():
-            move(left_p, False, pos == last, left_in)
-
-    make(pos)
-    yield
-    side_copy(pos).wait_recv()
-
-    @pl.when(pos == 0)
-    def _():
-        line_copy(pos, False).wait_recv()
-        add(pos, [left_in], True)
-
-    @pl.when(pos == last)
-    def _():
-        line_copy(pos, True).wait_recv()
-        add(pos, [right_in], True)
-
-    @pl.when((pos > 0) & (pos < last))
-    def _():
-        line_copy(pos, False).wait_recv()
-        line_copy(pos, True).wait_recv()
-        add(pos, [left_in, right_in], True)
-
-    def drain(p, carry):
-        side_copy(p).wait_send()
-
-        @pl.when(p > pos)
-        def _():
-            line_copy(p, True).wait_send()
-
-        @pl.when(p < pos)
-        def _():
-            line_copy(p, False).wait_send()
-
-        return carry
-
-    lax.fori_loop(0, length, drain, 0)
 
 
 class Forward(Step):
@@ -621,8 +700,8 @@
         n = len(self.grads.scratch)
         held = rest[n:]
         p_ref = held[0]
-        grads = self.grads.run(here, og_ref, gr_ref, *rest[:n])
-        next(grads)
+        grads = (og_ref, gr_ref) + tuple(rest[:n])
+        self.grads.begin(here, *grads)
         use_both(here.last)
         keep = pltpu.make_async_copy(all_ref, one_ref, load_sem.at[4])
         keep.start()
@@ -667,7 +746,9 @@
 
             lax.fori_loop(0, width // 512, body, 0)
 
-        weave([line_sum(here, rows, multiply, branch_ref, *held), grads])
+        total = LineSum(here, rows, multiply, branch_ref, *held)
+        rounds(here, total, lambda step: self.grads.hop(here, step, *grads))
+        total.end()
 
         def body(r, carry):
             at = pl.ds(pl.multiple_of(r * 32, 32), 32)
@@ -692,6 +773,7 @@
             return carry
 
         lax.fori_loop(0, length, drain, 0)
+        self.grads.end(here, *grads)
         keep.wait()
         yield
 
@@ -1070,7 +1152,7 @@
     grad_w_down, grad_w_gate, grad_w_up = lax.psum(ffn_parts, "dp")
 
     grad_h_two = together(
-        [Scatter([(grad_gate, w_gate, True), (grad_up, w_up, True)], members)],
+        [ScatterAlone([(grad_gate, w_gate, True), (grad_up, w_up, True)], members)],
         members,
         parts,
         6,
@@ -1078,8 +1160,8 @@
     )[0]
     grad_ffn_gain = jnp.sum(grad_h_two * normed_two, 0)
     grad_mid = out_grad.astype(F32) + norm_back(grad_h_two, normed_two, inv_two, ffn_gain)
-    grad_attn_rows, ffn_branch = together(
-        [Gather(grad_mid.astype(BF16), members), Scatter([(hidden, w_down, False)], members)],
+    ffn_branch, grad_attn_rows = together(
+        [ScatterAlone([(hidden, w_down, False)], members, grad_mid.astype(BF16))],
         members,
         parts,
         2,

time: 483 us -> 476 us (0.986); the launches traced: 474 us -> 474 us
  no operation moved by 1% of the time
where the time goes in v6:
time: 476 us; the launch traced here: 474 us
  Pallas kernels  388 us (82%)
  other arithmetic  32.6 us (7%)
  matrix products  28.2 us (6%)
  between operations  16.2 us (3%)
  local copies, waits for them, and re-layouts  8.57 us (2%)
    pallas_call x5, Pallas kernels, together(): pl.pallas_call(kernel, out_shape=[o for s in steps for o, _ in s.outputs]...  370 us
    dot_general x5, matrix products, matmul_left_t(): lax.dot_general(left, right, (((0,), (0,)), ((), ())), preferred_element_...  26.9 us
    pallas_call x1, Pallas kernels, attend_back(): pl.pallas_call(functools.partial(attend_back_kernel, heads), out_shape=(j...  17.7 us
  transfers between devices with their start and end apart: 1, of which 0 were waited for; matrix products, arithmetic and copies ran while one was open for 7% of the time, Pallas kernels for 56%

profile of v6, /device:TPU:10, one launch (start us, length us, event | category | flops | bytes accessed | tf_op | source)
XLA Modules:
  0.0 473.7 jit_solution(16765448722314226877)
XLA Ops:
  7.2 89.8 %shard_map.262 = (bf16[1024,2048]{1,0:T(8,128)(2,1)}, f32[1024,384]{1,0:T(8,128)}, bf16[1024,256]{1,0:T(8,128)(2,1)}, f32[4,1,1024]{2,1,0:T(1,128)}, bf16[1024,2...) custom-call(bf16[128,2048]{1,0:T(8,128)(2,1)} %refs_0_.1, ...), custom_call_target="tpu_custom_call" | custom-call | flops 1 | bytes 1 | tf_op jit(solution)/shard_map/pallas_call | solution.py:918
  97.0 1.0 copy-done.9
  98.1 34.8 %shard_map.263 = (bf16[1024,2048]{1,0:T(8,128)(2,1)S(1)}, bf16[1024,1024]{1,0:T(8,128)(2,1)S(1)}, bf16[1024,1024]{1,0:T(8,128)(2,1)S(1)}, bf16[1024,1024]{1,0:T(8,128)(2,1)S(1)}) custom-call(bf16[128,2048]{1,0:T(8,128)(2,1)S(1)} %copy-done.9, bf16[1024,2048]{1,0:T(8,128)(2,1)} %get-tuple-element.49.refs_1_, bf16[2048,1024]{1,0:T(8,128)(2,1)} %refs_2_.3, ...), custom_call_target="tpu_custom_call" | custom-call | flops 1 | bytes 1 | tf_op jit(solution)/shard_map/pallas_call | solution.py:918
  132.9 6.1 %convolution_convert_fusion = bf16[2048,1024]{1,0:T(8,128)(2,1)} fusion(bf16[1024,2048]{1,0:T(8,128)(2,1)S(1)} %get-tuple-element.54, bf16[1024,1024]{1,0:T(8,128)(2,1)S(1)} %get-tuple-element.59.refs_1_), kind=kOutput, calls=%fused_computation | convolution fusion | flops 4297064448 | bytes 10485760 | tf_op jit(solution)/shard_map/dot_general | solution.py:1070
  139.1 6.1 %convolution_convert_fusion.1 = bf16[2048,1024]{1,0:T(8,128)(2,1)} fusion(bf16[1024,2048]{1,0:T(8,128)(2,1)S(1)} %get-tuple-element.54, bf16[1024,1024]{1,0:T(8,128)(2,1)S(1)} %get-tuple-element.58.refs_0_), kind=kOutput, calls=%fused_computation.1 | convolution fusion | flops 4297064448 | bytes 10485760 | tf_op jit(solution)/shard_map/dot_general | solution.py:1070
  145.2 6.2 %convolution_convert_fusion.2 = bf16[1024,2048]{1,0:T(8,128)(2,1)} fusion(bf16[1024,1024]{1,0:T(8,128)(2,1)S(1)} %get-tuple-element.57.refs_0_, bf16[1024,2048]{1,0:T(8,128)(2,1)S(1)} %copy-done.24), kind=kOutput, calls=%fused_computation.2 | convolution fusion | flops 4297064448 | bytes 10485760 | tf_op jit(solution)/shard_map/dot_general | solution.py:1070
  151.5 60.3 %shard_map.264 = f32[128,2048]{1,0:T(8,128)} custom-call(bf16[1024,1024]{1,0:T(8,128)(2,1)} %copy-done.1, bf16[1024,1024]{1,0:T(8,128)(2,1)} %copy-done.2, bf16[2048,1024]{1,0:T(8,128)(2,1)} %refs_2_.3, bf16[2048,1024]{1,0:T(8,128)(2,1)} %refs_3_.3), custom_call_target="tpu_custom_call" | custom-call | flops 1 | bytes 1 | tf_op jit(solution)/shard_map/pallas_call | solution.py:918
  212.0 2.9 multiply_reduce_fusion.3
  214.9 1.7 fusion.10.refs_2_
  216.6 52.8 %shard_map.265 = (f32[128,2048]{1,0:T(8,128)S(1)}, bf16[1024,2048]{1,0:T(8,128)(2,1)S(1)}) custom-call(bf16[1024,1024]{1,0:T(8,128)(2,1)S(1)} %get-tuple-element.57.refs_0_, bf16[1024,2048]{1,0:T(8,128)(2,1)S(1)} %copy-done, bf16[128,2048]{1,0:T(8,128)(2,1)S(1)} %fusion.10.refs_2_), custom_call_target="tpu_custom_call" | custom-call | flops 1 | bytes 1 | tf_op jit(solution)/shard_map/pallas_call | solution.py:918
  269.5 1.3 convolution_convert_fusion.4.grad_ref
  270.8 1.2 copy-done.14
  273.2 17.7 %shard_map.266 = (bf16[1024,384]{1,0:T(8,128)(2,1)S(1)}, f32[1,384]{1,0:T(1,128)S(1)}) custom-call(f32[1024,384]{1,0:T(8,128)S(1)} %copy-done.3, f32[1024,128]{1,0:T(8,128)S(1)} %copy-done.7, f32[1024,128]{1,0:T(8,128)S(1)} %copy-done.8, f32[1,64]{1,0:T(1,128)S(1)} %bitcast.37, f32[1,64]{1,0:T(1,128)S(1)} %bitcast.39, s32[4,1,256]{2,1,0:T(1,128)S(1)} %bitcast.33, ...), custom_call_target="tpu_custom_call" | custom-call | flops 1 | bytes 1 | tf_op jit(solution)/shard_map/pallas_call | solution.py:1054
  290.9 1.6 constant_dynamic-slice_fusion
  292.6 4.8 %multiply_reduce_fusion = (f32[2048]{0:T(1024)S(1)}, bf16[2048,384]{1,0:T(8,128)(2,1)S(1)}, bf16[2048,384]{1,0:T(8,128)(2,1)S(1)}) fusion(bf16[2048,64]{1,0:T(8,128)(2,1)S(1)} %get-tuple-element.100, bf16[2048,64]{1,0:T(8,128)(2,1)S(1)} %get-tuple-element.101, bf16[2048,256]{1,0:T(8,128)(2,1)S(1)} %copy-done.26, bf16[1024,2048]{1,0:T(8,128)(2,1)} %get-tuple-element.61, ...), kind=kOutput, calls=%fused_computation.3 | convolution fusion | flops 1618475008 | bytes 9707520 | tf_op jit(solution)/shard_map/dot_general | solution.py:1070
  297.4 0.8 slice.47
  298.4 0.7 concatenate.12
  299.2 1.1 pad_maximum_fusion.1.refs_0_
  300.3 3.7 convolution_convert_fusion.3.refs_3_
  304.0 132.5 %shard_map.267 = (bf16[2048,512]{1,0:T(8,128)(2,1)S(1)}, bf16[2048,512]{1,0:T(8,128)(2,1)S(1)}, f32[64,128]{1,0:T(8,128)S(1)}, f32[128,2048]{1,0:T(8,128)S(1)}, ...) custom-call(bf16[2112,128]{1,0:T(8,128)(2,1)S(1)} %pad_maximum_fusion.1.refs_0_, ...), custom_call_target="tpu_custom_call" | custom-call | flops 1 | bytes 1 | tf_op jit(solution)/shard_map/pallas_call | solution.py:918
  436.5 2.6 convert_element_type.70
  439.1 2.6 convert_element_type.71
  441.7 1.5 convert_element_type.69
  443.2 1.6 convert_element_type.72
  444.8 0.5 slice.52
  446.4 1.9 fusion.8
  448.2 0.6 pad_maximum_fusion.2
  448.8 0.6 fusion.11
  449.4 0.6 slice_bitcast_fusion
  450.0 6.8 %convert_element_type.73 = f32[2048,1024]{1,0:T(8,128)} convert(bf16[2048,1024]{1,0:T(8,128)(2,1)} %get-tuple-element.86) | non-fusion elementwise | flops 2097152 | bytes 12582912 | tf_op jit(solution)/shard_map/convert_element_type | solution.py:1222
  456.8 4.4 convert_element_type.74
  461.2 4.4 convert_element_type.75
  (73 shorter events, 2.1 us)
Async XLA Ops:
  7.2 442.8 %all-reduce.4.cloned.1.call-start = ((), (), s32[]{:S(2)}) async-start(), calls=%async_computation | async-start | bytes 25165824 | tf_op jit(solution)/shard_map/psum | solution.py:1152
  97.0 1.0 copy-start.9
  132.9 6.2 %copy-start.2 = (bf16[1024,1024]{1,0:T(8,128)(2,1)}, bf16[1024,1024]{1,0:T(8,128)(2,1)S(1)}, u32[]{:S(2)}) copy-start(bf16[1024,1024]{1,0:T(8,128)(2,1)S(1)} %get-tuple-element.59.refs_1_) | copy-start | bytes 6291460
  132.9 6.1 %copy-start.1 = (bf16[1024,1024]{1,0:T(8,128)(2,1)}, bf16[1024,1024]{1,0:T(8,128)(2,1)S(1)}, u32[]{:S(2)}) copy-start(bf16[1024,1024]{1,0:T(8,128)(2,1)S(1)} %get-tuple-element.58.refs_0_) | copy-start | bytes 6291460
  139.1 6.1 %copy-start.24 = (bf16[1024,2048]{1,0:T(8,128)(2,1)S(1)}, bf16[1024,2048]{1,0:T(8,128)(2,1)}, u32[]{:S(2)}) copy-start(bf16[1024,2048]{1,0:T(8,128)(2,1)} %get-tuple-element.49.refs_1_) | copy-start | bytes 12582916
  151.4 60.3 %copy-start.15 = (bf16[128,2048]{1,0:T(8,128)(2,1)S(1)}, bf16[128,2048]{1,0:T(8,128)(2,1)}, u32[]{:S(2)}) copy-start(bf16[128,2048]{1,0:T(8,128)(2,1)} %refs_0_.1) | copy-start | bytes 1572868
  151.4 60.3 %copy-start.17 = (f32[128,2048]{1,0:T(8,128)S(1)}, f32[128,2048]{1,0:T(8,128)}, u32[]{:S(2)}) copy-start(f32[128,2048]{1,0:T(8,128)} %get-tuple-element.52) | copy-start | bytes 3145732
  151.4 60.6 %copy-start.27 = (f32[2048]{0:T(1024)S(1)}, f32[2048]{0:T(1024)}, u32[]{:S(2)}) copy-start(f32[2048]{0:T(1024)} %param.26) | copy-start | bytes 24580
  151.4 63.4 %copy-start.20 = (bf16[128,2048]{1,0:T(8,128)(2,1)S(1)}, bf16[128,2048]{1,0:T(8,128)(2,1)}, u32[]{:S(2)}) copy-start(bf16[128,2048]{1,0:T(8,128)(2,1)} %refs_1_.2) | copy-start | bytes 1572868
  211.7 4.8 %copy-start = (bf16[1024,2048]{1,0:T(8,128)(2,1)S(1)}, bf16[1024,2048]{1,0:T(8,128)(2,1)}, u32[]{:S(2)}) copy-start(bf16[1024,2048]{1,0:T(8,128)(2,1)} %refs_1_.3) | copy-start | bytes 12582916
  216.6 52.8 %copy-start.25 = (bf16[256,2048]{1,0:T(8,128)(2,1)S(1)}, bf16[256,2048]{1,0:T(8,128)(2,1)}, u32[]{:S(2)}) copy-start(bf16[256,2048]{1,0:T(8,128)(2,1)} %refs_9_.1) | copy-start | bytes 3145732
  269.4 1.4 copy-start.4
  269.4 2.7 copy-start.14
  269.4 2.6 copy-start.3
  269.4 3.1 copy-start.6
  269.4 3.6 copy-start.7
  269.4 3.7 copy-start.8
  269.4 3.7 copy-start.10
  269.5 3.7 copy-start.11
  269.5 3.7 copy-start.12
  269.5 3.7 copy-start.13
  270.8 21.7 %copy-start.26 = (bf16[2048,256]{1,0:T(8,128)(2,1)S(1)}, bf16[2048,256]{1,0:T(8,128)(2,1)}, u32[]{:S(2)}) copy-start(bf16[2048,256]{1,0:T(8,128)(2,1)} %refs_6_.1) | copy-start | bytes 3145732
  292.5 5.9 %copy-start.28 = (f32[2048]{0:T(1024)S(1)}, f32[2048]{0:T(1024)}, u32[]{:S(2)}) copy-start(f32[2048]{0:T(1024)} %param.25) | copy-start | bytes 24580
  441.7 4.3 copy-start.16
  441.7 4.6 copy-start.5
  441.7 4.6 copy-start.18
  441.7 4.6 copy-start.19
  441.7 4.6 copy-start.21
  450.0 6.8 %copy-start.23 = (bf16[2048,1024]{1,0:T(8,128)(2,1)S(1)}, bf16[2048,1024]{1,0:T(8,128)(2,1)}, u32[]{:S(2)}) copy-start(bf16[2048,1024]{1,0:T(8,128)(2,1)} %get-tuple-element.87) | copy-start | bytes 12582916
  456.8 4.4 copy-start.22
Sparse Core Ops, SparseCore 0:
  151.5 289.4 all-reduce.3

commit v7 on v6

--- a/solution.py
+++ b/solution.py
@@ -1192,8 +1192,8 @@
         [
             KeyValue(kv_part, width, members, parts),
             Scatter([(grad_proj, w_attn, True)], members),
-            Across(output_part, parts, (False,), 2),
-            Across(query_part, parts, (True,), 2),
+            Across(output_part, parts, (False,)),
+            Across(query_part, parts, (True,)),
         ],
         members,
         parts,

time: 476 us -> 466 us (0.979)
  Pallas kernels: 388 us -> 369 us
  waiting for transfers between devices: 0.02 us -> 9.39 us
    pallas_call x5, Pallas kernels: 370 us -> 352 us  [together(): pl.pallas_call(kernel, out_shape=[o for s in steps for o, _ in s.outputs]...]
    psum x1, waiting for transfers between devices: 0.01 us -> 9.37 us  [per_device(): grad_w_down, grad_w_gate, grad_w_up = lax.psum(ffn_parts, 'dp')]
  transfers between devices with their start and end apart: 1 -> 1, of which waited for: 0 -> 1; matrix products, arithmetic and copies ran while one was open for 7% -> 7% of each run, Pallas kernels for 56% -> 53%
where the time goes in v7:
time: 466 us; the launch traced here: 465 us
  Pallas kernels  369 us (79%)
  other arithmetic  32.6 us (7%)
  matrix products  28.2 us (6%)
  between operations  16.2 us (3%)
  waiting for transfers between devices  9.39 us (2%)
  local copies, waits for them, and re-layouts  8.57 us (2%)
    pallas_call x5, Pallas kernels, together(): pl.pallas_call(kernel, out_shape=[o for s in steps for o, _ in s.outputs]...  352 us
    dot_general x5, matrix products, matmul_left_t(): lax.dot_general(left, right, (((0,), (0,)), ((), ())), preferred_element_...  26.9 us
    pallas_call x1, Pallas kernels, attend_back(): pl.pallas_call(functools.partial(attend_back_kernel, heads), out_shape=(j...  17.7 us
    psum x1, waiting for transfers between devices, per_device(): grad_w_down, grad_w_gate, grad_w_up = lax.psum(ffn_parts, 'dp')  9.37 us
  transfers between devices with their start and end apart: 1, of which 1 were waited for; matrix products, arithmetic and copies ran while one was open for 7% of the time, Pallas kernels for 53%

profile of v7, /device:TPU:10, one launch (start us, length us, event | category | flops | bytes accessed | tf_op | source)
XLA Modules:
  0.0 464.5 jit_solution(5455011892101005257)
XLA Ops:
  7.2 89.8 %shard_map.262 = (bf16[1024,2048]{1,0:T(8,128)(2,1)}, f32[1024,384]{1,0:T(8,128)}, bf16[1024,256]{1,0:T(8,128)(2,1)}, f32[4,1,1024]{2,1,0:T(1,128)}, bf16[1024,2...) custom-call(bf16[128,2048]{1,0:T(8,128)(2,1)} %refs_0_.1, ...), custom_call_target="tpu_custom_call" | custom-call | flops 1 | bytes 1 | tf_op jit(solution)/shard_map/pallas_call | solution.py:918
  97.0 1.0 copy-done.9
  98.1 34.8 %shard_map.263 = (bf16[1024,2048]{1,0:T(8,128)(2,1)S(1)}, bf16[1024,1024]{1,0:T(8,128)(2,1)S(1)}, bf16[1024,1024]{1,0:T(8,128)(2,1)S(1)}, bf16[1024,1024]{1,0:T(8,128)(2,1)S(1)}) custom-call(bf16[128,2048]{1,0:T(8,128)(2,1)S(1)} %copy-done.9, bf16[1024,2048]{1,0:T(8,128)(2,1)} %get-tuple-element.49.refs_1_, bf16[2048,1024]{1,0:T(8,128)(2,1)} %refs_2_.3, ...), custom_call_target="tpu_custom_call" | custom-call | flops 1 | bytes 1 | tf_op jit(solution)/shard_map/pallas_call | solution.py:918
  132.9 6.1 %convolution_convert_fusion = bf16[2048,1024]{1,0:T(8,128)(2,1)} fusion(bf16[1024,2048]{1,0:T(8,128)(2,1)S(1)} %get-tuple-element.54, bf16[1024,1024]{1,0:T(8,128)(2,1)S(1)} %get-tuple-element.59.refs_1_), kind=kOutput, calls=%fused_computation | convolution fusion | flops 4297064448 | bytes 10485760 | tf_op jit(solution)/shard_map/dot_general | solution.py:1070
  139.1 6.1 %convolution_convert_fusion.1 = bf16[2048,1024]{1,0:T(8,128)(2,1)} fusion(bf16[1024,2048]{1,0:T(8,128)(2,1)S(1)} %get-tuple-element.54, bf16[1024,1024]{1,0:T(8,128)(2,1)S(1)} %get-tuple-element.58.refs_0_), kind=kOutput, calls=%fused_computation.1 | convolution fusion | flops 4297064448 | bytes 10485760 | tf_op jit(solution)/shard_map/dot_general | solution.py:1070
  145.2 6.2 %convolution_convert_fusion.2 = bf16[1024,2048]{1,0:T(8,128)(2,1)} fusion(bf16[1024,1024]{1,0:T(8,128)(2,1)S(1)} %get-tuple-element.57.refs_0_, bf16[1024,2048]{1,0:T(8,128)(2,1)S(1)} %copy-done.24), kind=kOutput, calls=%fused_computation.2 | convolution fusion | flops 4297064448 | bytes 10485760 | tf_op jit(solution)/shard_map/dot_general | solution.py:1070
  151.5 60.3 %shard_map.264 = f32[128,2048]{1,0:T(8,128)} custom-call(bf16[1024,1024]{1,0:T(8,128)(2,1)} %copy-done.1, bf16[1024,1024]{1,0:T(8,128)(2,1)} %copy-done.2, bf16[2048,1024]{1,0:T(8,128)(2,1)} %refs_2_.3, bf16[2048,1024]{1,0:T(8,128)(2,1)} %refs_3_.3), custom_call_target="tpu_custom_call" | custom-call | flops 1 | bytes 1 | tf_op jit(solution)/shard_map/pallas_call | solution.py:918
  212.0 2.9 multiply_reduce_fusion.3
  214.9 1.7 fusion.10.refs_2_
  216.6 52.8 %shard_map.265 = (f32[128,2048]{1,0:T(8,128)S(1)}, bf16[1024,2048]{1,0:T(8,128)(2,1)S(1)}) custom-call(bf16[1024,1024]{1,0:T(8,128)(2,1)S(1)} %get-tuple-element.57.refs_0_, bf16[1024,2048]{1,0:T(8,128)(2,1)S(1)} %copy-done, bf16[128,2048]{1,0:T(8,128)(2,1)S(1)} %fusion.10.refs_2_), custom_call_target="tpu_custom_call" | custom-call | flops 1 | bytes 1 | tf_op jit(solution)/shard_map/pallas_call | solution.py:918
  269.5 1.3 convolution_convert_fusion.4.grad_ref
  270.8 1.2 copy-done.14
  273.2 17.7 %shard_map.266 = (bf16[1024,384]{1,0:T(8,128)(2,1)S(1)}, f32[1,384]{1,0:T(1,128)S(1)}) custom-call(f32[1024,384]{1,0:T(8,128)S(1)} %copy-done.3, f32[1024,128]{1,0:T(8,128)S(1)} %copy-done.7, f32[1024,128]{1,0:T(8,128)S(1)} %copy-done.8, f32[1,64]{1,0:T(1,128)S(1)} %bitcast.37, f32[1,64]{1,0:T(1,128)S(1)} %bitcast.39, s32[4,1,256]{2,1,0:T(1,128)S(1)} %bitcast.33, ...), custom_call_target="tpu_custom_call" | custom-call | flops 1 | bytes 1 | tf_op jit(solution)/shard_map/pallas_call | solution.py:1054
  290.9 1.6 constant_dynamic-slice_fusion
  292.6 4.8 %multiply_reduce_fusion = (f32[2048]{0:T(1024)S(1)}, bf16[2048,384]{1,0:T(8,128)(2,1)S(1)}, bf16[2048,384]{1,0:T(8,128)(2,1)S(1)}) fusion(bf16[2048,64]{1,0:T(8,128)(2,1)S(1)} %get-tuple-element.100, bf16[2048,64]{1,0:T(8,128)(2,1)S(1)} %get-tuple-element.101, bf16[2048,256]{1,0:T(8,128)(2,1)S(1)} %copy-done.26, bf16[1024,2048]{1,0:T(8,128)(2,1)} %get-tuple-element.61, ...), kind=kOutput, calls=%fused_computation.3 | convolution fusion | flops 1618475008 | bytes 9707520 | tf_op jit(solution)/shard_map/dot_general | solution.py:1070
  297.4 0.8 slice.47
  298.4 0.7 concatenate.12
  299.2 1.1 pad_maximum_fusion.1.refs_0_
  300.3 3.7 convolution_convert_fusion.3.refs_3_
  304.0 114.1 %shard_map.267 = (bf16[2048,512]{1,0:T(8,128)(2,1)S(1)}, bf16[2048,512]{1,0:T(8,128)(2,1)S(1)}, f32[64,128]{1,0:T(8,128)S(1)}, f32[128,2048]{1,0:T(8,128)S(1)}, ...) custom-call(bf16[2112,128]{1,0:T(8,128)(2,1)S(1)} %pad_maximum_fusion.1.refs_0_, ...), custom_call_target="tpu_custom_call" | custom-call | flops 1 | bytes 1 | tf_op jit(solution)/shard_map/pallas_call | solution.py:918
  418.0 2.6 convert_element_type.70
  420.6 2.6 convert_element_type.71
  423.3 1.5 convert_element_type.69
  424.8 1.6 convert_element_type.72
  427.9 1.9 fusion.8
  429.7 0.6 pad_maximum_fusion.2
  430.3 0.6 fusion.11
  430.9 0.6 slice_bitcast_fusion
  431.5 9.4 %all-reduce.4.cloned.1.call-done = (bf16[2048,1024]{1,0:T(8,128)(2,1)}, bf16[2048,1024]{1,0:T(8,128)(2,1)}, bf16[1024,2048]{1,0:T(8,128)(2,1)}) async-done(((bf16[2048,1024]{1,0:T(8,128)(2,1)}, bf16[2048,1024]{1,0:T(8,128)(2,1)}, bf16[1024,2048]{1,0:T(8,128)(2,1)}), (bf16[2048,1024]{1,0:T(8,128)(2,1)}, bf16[2048,1024]{1,0:T(8,128)(2,1)}, bf16[1024,2048]{1,0:T(8,128)(2,1)})) %all-reduce.4.cloned.1.call-update) | async-done | bytes 12582928 | tf_op jit(solution)/shard_map/psum | solution.py:1152
  440.9 6.8 %convert_element_type.73 = f32[2048,1024]{1,0:T(8,128)} convert(bf16[2048,1024]{1,0:T(8,128)(2,1)} %get-tuple-element.86) | non-fusion elementwise | flops 2097152 | bytes 12582912 | tf_op jit(solution)/shard_map/convert_element_type | solution.py:1222
  447.7 4.4 convert_element_type.74
  452.1 4.4 convert_element_type.75
  (73 shorter events, 2.6 us)
Async XLA Ops:
  7.2 433.7 %all-reduce.4.cloned.1.call-start = ((), (), s32[]{:S(2)}) async-start(), calls=%async_computation | async-start | bytes 25165824 | tf_op jit(solution)/shard_map/psum | solution.py:1152
  97.0 1.0 copy-start.9
  132.9 6.2 %copy-start.2 = (bf16[1024,1024]{1,0:T(8,128)(2,1)}, bf16[1024,1024]{1,0:T(8,128)(2,1)S(1)}, u32[]{:S(2)}) copy-start(bf16[1024,1024]{1,0:T(8,128)(2,1)S(1)} %get-tuple-element.59.refs_1_) | copy-start | bytes 6291460
  132.9 6.1 %copy-start.1 = (bf16[1024,1024]{1,0:T(8,128)(2,1)}, bf16[1024,1024]{1,0:T(8,128)(2,1)S(1)}, u32[]{:S(2)}) copy-start(bf16[1024,1024]{1,0:T(8,128)(2,1)S(1)} %get-tuple-element.58.refs_0_) | copy-start | bytes 6291460
  139.1 6.1 %copy-start.24 = (bf16[1024,2048]{1,0:T(8,128)(2,1)S(1)}, bf16[1024,2048]{1,0:T(8,128)(2,1)}, u32[]{:S(2)}) copy-start(bf16[1024,2048]{1,0:T(8,128)(2,1)} %get-tuple-element.49.refs_1_) | copy-start | bytes 12582916
  151.4 60.3 %copy-start.15 = (bf16[128,2048]{1,0:T(8,128)(2,1)S(1)}, bf16[128,2048]{1,0:T(8,128)(2,1)}, u32[]{:S(2)}) copy-start(bf16[128,2048]{1,0:T(8,128)(2,1)} %refs_0_.1) | copy-start | bytes 1572868
  151.4 60.3 %copy-start.17 = (f32[128,2048]{1,0:T(8,128)S(1)}, f32[128,2048]{1,0:T(8,128)}, u32[]{:S(2)}) copy-start(f32[128,2048]{1,0:T(8,128)} %get-tuple-element.52) | copy-start | bytes 3145732
  151.4 60.6 %copy-start.27 = (f32[2048]{0:T(1024)S(1)}, f32[2048]{0:T(1024)}, u32[]{:S(2)}) copy-start(f32[2048]{0:T(1024)} %param.26) | copy-start | bytes 24580
  151.4 63.4 %copy-start.20 = (bf16[128,2048]{1,0:T(8,128)(2,1)S(1)}, bf16[128,2048]{1,0:T(8,128)(2,1)}, u32[]{:S(2)}) copy-start(bf16[128,2048]{1,0:T(8,128)(2,1)} %refs_1_.2) | copy-start | bytes 1572868
  211.7 4.8 %copy-start = (bf16[1024,2048]{1,0:T(8,128)(2,1)S(1)}, bf16[1024,2048]{1,0:T(8,128)(2,1)}, u32[]{:S(2)}) copy-start(bf16[1024,2048]{1,0:T(8,128)(2,1)} %refs_1_.3) | copy-start | bytes 12582916
  216.6 52.8 %copy-start.25 = (bf16[256,2048]{1,0:T(8,128)(2,1)S(1)}, bf16[256,2048]{1,0:T(8,128)(2,1)}, u32[]{:S(2)}) copy-start(bf16[256,2048]{1,0:T(8,128)(2,1)} %refs_9_.1) | copy-start | bytes 3145732
  269.4 1.4 copy-start.4
  269.4 2.7 copy-start.14
  269.4 2.6 copy-start.3
  269.4 3.1 copy-start.6
  269.4 3.6 copy-start.7
  269.4 3.7 copy-start.8
  269.4 3.7 copy-start.10
  269.5 3.7 copy-start.11
  269.5 3.7 copy-start.12
  269.5 3.7 copy-start.13
  270.8 21.7 %copy-start.26 = (bf16[2048,256]{1,0:T(8,128)(2,1)S(1)}, bf16[2048,256]{1,0:T(8,128)(2,1)}, u32[]{:S(2)}) copy-start(bf16[2048,256]{1,0:T(8,128)(2,1)} %refs_6_.1) | copy-start | bytes 3145732
  292.5 5.9 %copy-start.28 = (f32[2048]{0:T(1024)S(1)}, f32[2048]{0:T(1024)}, u32[]{:S(2)}) copy-start(f32[2048]{0:T(1024)} %param.25) | copy-start | bytes 24580
  423.2 4.3 copy-start.16
  423.2 4.6 copy-start.5
  423.3 4.6 copy-start.18
  423.3 4.6 copy-start.19
  423.3 4.6 copy-start.21
  440.9 6.8 %copy-start.23 = (bf16[2048,1024]{1,0:T(8,128)(2,1)S(1)}, bf16[2048,1024]{1,0:T(8,128)(2,1)}, u32[]{:S(2)}) copy-start(bf16[2048,1024]{1,0:T(8,128)(2,1)} %get-tuple-element.87) | copy-start | bytes 12582916
  447.7 4.4 copy-start.22
Sparse Core Ops, SparseCore 0:
  151.5 289.2 all-reduce.3

commit v8 on v7

--- a/solution.py
+++ b/solution.py
@@ -1031,7 +1031,9 @@
         e = dqn * gain[:, :width]
         out_ref[rows, :width] = (inv * (e - unit * group_mean(e * unit))).astype(BF16)
         return carry
-    lax.fori_loop(0, count, outer, 0)
+    for first in range(2):
+        lax.fori_loop(first * count // 2, (first + 1) * count // 2, outer, 0)
+        yield
     def finish(i, carry):
         rows = pl.ds(pl.multiple_of(i * BLOCK, BLOCK), BLOCK)
         x = proj_ref[rows, width:]
@@ -1046,20 +1048,23 @@
         out_ref[rows, width:] = jnp.where(lane < HD, dkp, dk).astype(BF16)
         return carry
     lax.fori_loop(0, count, finish, 0)
-
-def attend_back(proj, cosine, sine, query_gain, key_gain, positions, context, grad_context, lse, heads):
-    size = proj.shape[0]
-    count = size // BLOCK
-    vm = pl.BlockSpec(memory_space=pltpu.VMEM)
-    return pl.pallas_call(
-        functools.partial(attend_back_kernel, heads),
-        out_shape=(jax.ShapeDtypeStruct(proj.shape, BF16), jax.ShapeDtypeStruct((1, proj.shape[1]), F32)),
-        in_specs=[vm] * 9, out_specs=(vm, vm),
-        scratch_shapes=[pltpu.VMEM((size, HD), BF16), pltpu.VMEM((count, HD, BLOCK), BF16), pltpu.VMEM((size, HD), BF16),
-                        pltpu.VMEM((size, HD), F32), pltpu.VMEM((size, HD), F32), pltpu.VMEM((HD, heads * BLOCK), F32)],
-        compiler_params=pltpu.CompilerParams(vmem_limit_bytes=40 << 20),
-        cost_estimate=pl.CostEstimate(flops=1, bytes_accessed=1, transcendentals=0),
-    )(proj, cosine, sine, query_gain[None], key_gain[None], positions.reshape(count, 1, BLOCK), context, grad_context, lse)
+    yield
+
+class AttendBack(Step):
+    line, across = False, False
+
+    def __init__(self, proj, cosine, sine, query_gain, key_gain, positions, context, grad_context, lse, heads):
+        size = proj.shape[0]
+        count = size // BLOCK
+        self.heads = heads
+        args = (proj, cosine, sine, query_gain[None], key_gain[None], positions.reshape(count, 1, BLOCK), context, grad_context, lse)
+        self.inputs = [(x, VMEM) for x in args]
+        self.outputs = [(jax.ShapeDtypeStruct(proj.shape, BF16), VMEM), (jax.ShapeDtypeStruct((1, proj.shape[1]), F32), VMEM)]
+        self.scratch = [pltpu.VMEM((size, HD), BF16), pltpu.VMEM((count, HD, BLOCK), BF16), pltpu.VMEM((size, HD), BF16)]
+        self.scratch += [pltpu.VMEM((size, HD), F32), pltpu.VMEM((size, HD), F32), pltpu.VMEM((HD, heads * BLOCK), F32)]
+
+    def run(self, here, *refs):
+        yield from attend_back_kernel(self.heads, *refs)
 
 
 def matmul(left, right):
@@ -1167,10 +1172,18 @@
         2,
     )
     grad_context = matmul_right_t(grad_attn_rows, w_output).astype(BF16)
-    grad_proj, gain_sums = attend_back(
-        projected, cosine, sine, query_gain, key_gain, positions, context, grad_context, lse, heads
+    output_part = matmul_left_t(context, grad_attn_rows).astype(BF16)
+    grad_proj, gain_sums, grad_w_output = together(
+        [
+            AttendBack(
+                projected, cosine, sine, query_gain, key_gain, positions, context, grad_context, lse, heads
+            ),
+            Across(output_part, parts, (False, True) if output_part.shape[0] % (32 * parts) == 0 else (False,)),
+        ],
+        members,
+        parts,
+        7,
     )
-    output_part = matmul_left_t(context, grad_attn_rows).astype(BF16)
     grad_w_attn = matmul_left_t(rows_one, grad_proj)
     grad_attn_gain = jnp.sum(w_attn.astype(F32) * grad_w_attn, 1) / attn_gain
 
@@ -1188,12 +1201,11 @@
     small_rows = jnp.pad(small, (0, extra * 2 * HD - small.shape[0])).reshape(extra, 2 * HD)
     kv_part = jnp.concatenate([grad_w_attn[:, query_width:], small_rows], 0).astype(BF16)
     query_part = grad_w_attn[:, :query_width].astype(BF16)
-    grad_w_key, grad_w_value, small_sum, grad_h_one, grad_w_output, grad_w_query = together(
+    grad_w_key, grad_w_value, small_sum, grad_h_one, grad_w_query = together(
         [
             KeyValue(kv_part, width, members, parts),
             Scatter([(grad_proj, w_attn, True)], members),
-            Across(output_part, parts, (False,)),
-            Across(query_part, parts, (True,)),
+            Across(query_part, parts, (False, True)),
         ],
         members,
         parts,

time: 466 us -> 461 us (0.989)
  waiting for transfers between devices: 9.39 us -> 0.02 us
  Pallas kernels: 369 us -> 378 us
    pallas_call x5 -> x6, Pallas kernels: 352 us -> 378 us  [together(): pl.pallas_call(kernel, out_shape=[o for s in steps for o, _ in s.outputs]...]
    pallas_call x1 -> x0, Pallas kernels: 17.7 us -> none  [attend_back(): pl.pallas_call(functools.partial(attend_back_kernel, heads), out_shape=(j...]
    psum x1, waiting for transfers between devices: 9.37 us -> 0.01 us  [per_device(): grad_w_down, grad_w_gate, grad_w_up = lax.psum(ffn_parts, 'dp')]
  transfers between devices with their start and end apart: 1 -> 1, of which waited for: 1 -> 0; matrix products, arithmetic and copies ran while one was open for 7% -> 6% of each run, Pallas kernels for 53% -> 55%
where the time goes in v8:
time: 461 us
  Pallas kernels  378 us (82%)
  other arithmetic  32.6 us (7%)
  matrix products  25.8 us (6%)
  between operations  16.2 us (4%)
  local copies, waits for them, and re-layouts  7.92 us (2%)
    pallas_call x6, Pallas kernels, together(): pl.pallas_call(kernel, out_shape=[o for s in steps for o, _ in s.outputs]...  378 us
    dot_general x5, matrix products, matmul_left_t(): lax.dot_general(left, right, (((0,), (0,)), ((), ())), preferred_element_...  24.5 us
  transfers between devices with their start and end apart: 1, of which 0 were waited for; matrix products, arithmetic and copies ran while one was open for 6% of the time, Pallas kernels for 55%

profile of v8, /device:TPU:10, one launch (start us, length us, event | category | flops | bytes accessed | tf_op | source)
XLA Modules:
  0.0 461.0 jit_solution(10807436019284027319)
XLA Ops:
  7.2 89.8 %shard_map.262 = (bf16[1024,2048]{1,0:T(8,128)(2,1)}, f32[1024,384]{1,0:T(8,128)}, bf16[1024,256]{1,0:T(8,128)(2,1)}, f32[4,1,1024]{2,1,0:T(1,128)}, bf16[1024,2...) custom-call(bf16[128,2048]{1,0:T(8,128)(2,1)} %refs_0_.1, ...), custom_call_target="tpu_custom_call" | custom-call | flops 1 | bytes 1 | tf_op jit(solution)/shard_map/pallas_call | solution.py:918
  97.0 1.0 copy-done.11
  98.1 34.8 %shard_map.263 = (bf16[1024,2048]{1,0:T(8,128)(2,1)S(1)}, bf16[1024,1024]{1,0:T(8,128)(2,1)S(1)}, bf16[1024,1024]{1,0:T(8,128)(2,1)S(1)}, bf16[1024,1024]{1,0:T(8,128)(2,1)S(1)}) custom-call(bf16[128,2048]{1,0:T(8,128)(2,1)S(1)} %copy-done.11, bf16[1024,2048]{1,0:T(8,128)(2,1)} %get-tuple-element.49.refs_1_, bf16[2048,1024]{1,0:T(8,128)(2,1)} %refs_2_.3, ...), custom_call_target="tpu_custom_call" | custom-call | flops 1 | bytes 1 | tf_op jit(solution)/shard_map/pallas_call | solution.py:918
  132.9 6.1 %convolution_convert_fusion = bf16[2048,1024]{1,0:T(8,128)(2,1)} fusion(bf16[1024,2048]{1,0:T(8,128)(2,1)S(1)} %get-tuple-element.54, bf16[1024,1024]{1,0:T(8,128)(2,1)S(1)} %get-tuple-element.59.refs_1_), kind=kOutput, calls=%fused_computation | convolution fusion | flops 4297064448 | bytes 10485760 | tf_op jit(solution)/shard_map/dot_general | solution.py:1075
  139.1 6.1 %convolution_convert_fusion.1 = bf16[2048,1024]{1,0:T(8,128)(2,1)} fusion(bf16[1024,2048]{1,0:T(8,128)(2,1)S(1)} %get-tuple-element.54, bf16[1024,1024]{1,0:T(8,128)(2,1)S(1)} %get-tuple-element.58.refs_0_), kind=kOutput, calls=%fused_computation.1 | convolution fusion | flops 4297064448 | bytes 10485760 | tf_op jit(solution)/shard_map/dot_general | solution.py:1075
  145.2 6.2 %convolution_convert_fusion.2 = bf16[1024,2048]{1,0:T(8,128)(2,1)} fusion(bf16[1024,1024]{1,0:T(8,128)(2,1)S(1)} %get-tuple-element.57.refs_0_, bf16[1024,2048]{1,0:T(8,128)(2,1)S(1)} %copy-done.25), kind=kOutput, calls=%fused_computation.2 | convolution fusion | flops 4297064448 | bytes 10485760 | tf_op jit(solution)/shard_map/dot_general | solution.py:1075
  151.5 60.3 %shard_map.264 = f32[128,2048]{1,0:T(8,128)} custom-call(bf16[1024,1024]{1,0:T(8,128)(2,1)} %copy-done.1, bf16[1024,1024]{1,0:T(8,128)(2,1)} %copy-done.2, bf16[2048,1024]{1,0:T(8,128)(2,1)} %refs_2_.3, bf16[2048,1024]{1,0:T(8,128)(2,1)} %refs_3_.3), custom_call_target="tpu_custom_call" | custom-call | flops 1 | bytes 1 | tf_op jit(solution)/shard_map/pallas_call | solution.py:918
  212.0 2.9 multiply_reduce_fusion.3
  214.9 1.7 fusion.10.refs_2_
  216.6 52.8 %shard_map.265 = (f32[128,2048]{1,0:T(8,128)S(1)}, bf16[1024,2048]{1,0:T(8,128)(2,1)S(1)}) custom-call(bf16[1024,1024]{1,0:T(8,128)(2,1)S(1)} %get-tuple-element.57.refs_0_, bf16[1024,2048]{1,0:T(8,128)(2,1)S(1)} %copy-done, bf16[128,2048]{1,0:T(8,128)(2,1)S(1)} %fusion.10.refs_2_), custom_call_target="tpu_custom_call" | custom-call | flops 1 | bytes 1 | tf_op jit(solution)/shard_map/pallas_call | solution.py:918
  269.4 1.3 convolution_convert_fusion.3.refs_9_
  271.0 1.3 convolution_convert_fusion.4.refs_7_
  272.8 44.3 %shard_map.266 = (bf16[1024,384]{1,0:T(8,128)(2,1)S(1)}, f32[1,384]{1,0:T(1,128)S(1)}, bf16[256,2048]{1,0:T(8,128)(2,1)S(1)}) custom-call(f32[1024,384]{1,0:T(8,128)S(1)} %copy-done.3, f32[1024,128]{1,0:T(8,128)S(1)} %copy-done.9, f32[1024,128]{1,0:T(8,128)S(1)} %copy-done.10, f32[1,64]{1,0:T(1,128)S(1)} %bitcast.37, f32[1,64]{1,0:T(1,128)S(1)} %bitcast.39, ...), custom_call_target="tpu_custom_call" | custom-call | flops 1 | bytes 1 | tf_op jit(solution)/shard_map/pallas_call | solution.py:918
  317.1 1.0 copy-done.4
  318.1 1.6 constant_dynamic-slice_fusion
  319.7 4.8 %multiply_reduce_fusion = (f32[2048]{0:T(1024)S(1)}, bf16[2048,384]{1,0:T(8,128)(2,1)S(1)}, bf16[2048,384]{1,0:T(8,128)(2,1)S(1)}) fusion(bf16[2048,64]{1,0:T(8,128)(2,1)S(1)} %get-tuple-element.100, bf16[2048,64]{1,0:T(8,128)(2,1)S(1)} %get-tuple-element.101, bf16[2048,256]{1,0:T(8,128)(2,1)S(1)} %copy-done.27, bf16[1024,2048]{1,0:T(8,128)(2,1)} %get-tuple-element.61, ...), kind=kOutput, calls=%fused_computation.3 | convolution fusion | flops 1618475008 | bytes 9707520 | tf_op jit(solution)/shard_map/dot_general | solution.py:1075
  324.5 0.8 slice.47
  325.6 0.7 concatenate.12
  326.3 1.1 pad_maximum_fusion.1.refs_0_
  327.4 96.3 %shard_map.267 = (bf16[2048,512]{1,0:T(8,128)(2,1)S(1)}, bf16[2048,512]{1,0:T(8,128)(2,1)S(1)}, f32[64,128]{1,0:T(8,128)S(1)}, f32[128,2048]{1,0:T(8,128)S(1)}, bf16[2048,256]{1,0:T(8,128)(2,1)S(1)}) custom-call(bf16[2112,128]{1,0:T(8,128)(2,1)S(1)} %pad_maximum_fusion.1.refs_0_, bf16[1024,384]{1,0:T(8,128)(2,1)S(1)} %get-tuple-element.68.refs_1_, ...), custom_call_target="tpu_custom_call" | custom-call | flops 1 | bytes 1 | tf_op jit(solution)/shard_map/pallas_call | solution.py:918
  423.7 2.6 convert_element_type.70
  426.3 2.6 convert_element_type.71
  429.0 1.5 convert_element_type.69
  430.4 0.5 slice.52
  431.7 1.6 convert_element_type.72
  433.6 1.9 fusion.8
  435.5 0.6 pad_maximum_fusion.2
  436.1 0.6 fusion.11
  436.7 0.6 slice_bitcast_fusion
  437.3 6.8 %convert_element_type.73 = f32[2048,1024]{1,0:T(8,128)} convert(bf16[2048,1024]{1,0:T(8,128)(2,1)} %get-tuple-element.86) | non-fusion elementwise | flops 2097152 | bytes 12582912 | tf_op jit(solution)/shard_map/convert_element_type | solution.py:1234
  444.1 4.4 convert_element_type.74
  448.5 4.4 convert_element_type.75
  (75 shorter events, 1.7 us)
Async XLA Ops:
  7.2 430.1 %all-reduce.4.cloned.1.call-start = ((), (), s32[]{:S(2)}) async-start(), calls=%async_computation | async-start | bytes 25165824 | tf_op jit(solution)/shard_map/psum | solution.py:1157
  97.0 1.0 copy-start.11
  132.9 6.2 %copy-start.2 = (bf16[1024,1024]{1,0:T(8,128)(2,1)}, bf16[1024,1024]{1,0:T(8,128)(2,1)S(1)}, u32[]{:S(2)}) copy-start(bf16[1024,1024]{1,0:T(8,128)(2,1)S(1)} %get-tuple-element.59.refs_1_) | copy-start | bytes 6291460
  132.9 6.1 %copy-start.1 = (bf16[1024,1024]{1,0:T(8,128)(2,1)}, bf16[1024,1024]{1,0:T(8,128)(2,1)S(1)}, u32[]{:S(2)}) copy-start(bf16[1024,1024]{1,0:T(8,128)(2,1)S(1)} %get-tuple-element.58.refs_0_) | copy-start | bytes 6291460
  139.1 6.1 %copy-start.25 = (bf16[1024,2048]{1,0:T(8,128)(2,1)S(1)}, bf16[1024,2048]{1,0:T(8,128)(2,1)}, u32[]{:S(2)}) copy-start(bf16[1024,2048]{1,0:T(8,128)(2,1)} %get-tuple-element.49.refs_1_) | copy-start | bytes 12582916
  151.4 60.3 %copy-start.16 = (bf16[128,2048]{1,0:T(8,128)(2,1)S(1)}, bf16[128,2048]{1,0:T(8,128)(2,1)}, u32[]{:S(2)}) copy-start(bf16[128,2048]{1,0:T(8,128)(2,1)} %refs_0_.1) | copy-start | bytes 1572868
  151.4 60.3 %copy-start.18 = (f32[128,2048]{1,0:T(8,128)S(1)}, f32[128,2048]{1,0:T(8,128)}, u32[]{:S(2)}) copy-start(f32[128,2048]{1,0:T(8,128)} %get-tuple-element.52) | copy-start | bytes 3145732
  151.4 60.5 %copy-start.28 = (f32[2048]{0:T(1024)S(1)}, f32[2048]{0:T(1024)}, u32[]{:S(2)}) copy-start(f32[2048]{0:T(1024)} %param.26) | copy-start | bytes 24580
  151.4 63.4 %copy-start.21 = (bf16[128,2048]{1,0:T(8,128)(2,1)S(1)}, bf16[128,2048]{1,0:T(8,128)(2,1)}, u32[]{:S(2)}) copy-start(bf16[128,2048]{1,0:T(8,128)(2,1)} %refs_1_.2) | copy-start | bytes 1572868
  211.7 4.8 %copy-start = (bf16[1024,2048]{1,0:T(8,128)(2,1)S(1)}, bf16[1024,2048]{1,0:T(8,128)(2,1)}, u32[]{:S(2)}) copy-start(bf16[1024,2048]{1,0:T(8,128)(2,1)} %refs_1_.3) | copy-start | bytes 12582916
  216.6 52.8 %copy-start.8 = (bf16[1024,256]{1,0:T(8,128)(2,1)S(1)}, bf16[1024,256]{1,0:T(8,128)(2,1)}, u32[]{:S(2)}) copy-start(bf16[1024,256]{1,0:T(8,128)(2,1)} %get-tuple-element.65.refs_6_) | copy-start | bytes 1572868
  269.4 3.0 copy-start.6
  269.4 1.6 copy-start.26
  271.0 1.4 copy-start.3
  271.0 1.6 copy-start.9
  271.0 1.8 copy-start.10
  271.0 1.8 copy-start.12
  271.0 1.8 copy-start.13
  271.0 1.8 copy-start.14
  271.0 1.8 copy-start.15
  272.3 47.4 %copy-start.27 = (bf16[2048,256]{1,0:T(8,128)(2,1)S(1)}, bf16[2048,256]{1,0:T(8,128)(2,1)}, u32[]{:S(2)}) copy-start(bf16[2048,256]{1,0:T(8,128)(2,1)} %refs_6_.1) | copy-start | bytes 3145732
  317.1 1.0 copy-start.4
  319.7 5.9 %copy-start.29 = (f32[2048]{0:T(1024)S(1)}, f32[2048]{0:T(1024)}, u32[]{:S(2)}) copy-start(f32[2048]{0:T(1024)} %param.25) | copy-start | bytes 24580
  426.3 5.3 %copy-start.5 = (bf16[256,2048]{1,0:T(8,128)(2,1)S(1)}, bf16[256,2048]{1,0:T(8,128)(2,1)}, u32[]{:S(2)}) copy-start(bf16[256,2048]{1,0:T(8,128)(2,1)} %copy-done.4) | copy-start | bytes 3145732
  428.9 4.3 copy-start.17
  428.9 4.6 %copy-start.7 = (f32[128,2048]{1,0:T(8,128)S(1)}, f32[128,2048]{1,0:T(8,128)}, u32[]{:S(2)}) copy-start(f32[128,2048]{1,0:T(8,128)} %copy-done.6) | copy-start | bytes 3145732
  428.9 4.6 %copy-start.19 = (f32[128,2048]{1,0:T(8,128)S(1)}, f32[128,2048]{1,0:T(8,128)}, u32[]{:S(2)}) copy-start(f32[128,2048]{1,0:T(8,128)} %get-tuple-element.52) | copy-start | bytes 3145732
  428.9 4.6 %copy-start.20 = (f32[128,2048]{1,0:T(8,128)S(1)}, f32[128,2048]{1,0:T(8,128)}, u32[]{:S(2)}) copy-start(f32[128,2048]{1,0:T(8,128)} %shard_map.264) | copy-start | bytes 3145732
  428.9 4.6 %copy-start.22 = (bf16[128,2048]{1,0:T(8,128)(2,1)S(1)}, bf16[128,2048]{1,0:T(8,128)(2,1)}, u32[]{:S(2)}) copy-start(bf16[128,2048]{1,0:T(8,128)(2,1)} %refs_1_.2) | copy-start | bytes 1572868
  437.3 6.8 %copy-start.24 = (bf16[2048,1024]{1,0:T(8,128)(2,1)S(1)}, bf16[2048,1024]{1,0:T(8,128)(2,1)}, u32[]{:S(2)}) copy-start(bf16[2048,1024]{1,0:T(8,128)(2,1)} %get-tuple-element.87) | copy-start | bytes 12582916
  444.1 4.4 copy-start.23
Sparse Core Ops, SparseCore 0:
  151.5 280.7 all-reduce.3

commit v9 on v8

--- a/solution.py
+++ b/solution.py
@@ -1088,6 +1088,25 @@
     return lax.optimization_barrier((first,) + later)
 
 
+def widen_kernel(*refs):
+    for low, high in zip(refs[:3], refs[3:]):
+        high[...] = low[...].astype(F32)
+
+
+def widen(*arrays):
+    steps = 8
+    specs = [pl.BlockSpec((x.shape[0] // steps, x.shape[1]), lambda i: (i, 0)) for x in arrays]
+    return pl.pallas_call(
+        widen_kernel,
+        grid=(steps,),
+        out_shape=[jax.ShapeDtypeStruct(x.shape, F32) for x in arrays],
+        in_specs=specs,
+        out_specs=specs,
+        compiler_params=pltpu.CompilerParams(vmem_limit_bytes=32 << 20),
+        cost_estimate=pl.CostEstimate(flops=1, bytes_accessed=1, transcendentals=0),
+    )(*arrays)
+
+
 def per_device(
     tokens,
     seg_ids,
@@ -1216,6 +1235,7 @@
     at = 2 * width
     residual_rms = jnp.sqrt(small_sum[at + 2 * HD : at + 2 * HD + 1] / entry_count)
 
+    grad_w_gate, grad_w_up, grad_w_down = widen(grad_w_gate, grad_w_up, grad_w_down)
     grad_tokens = (grad_mid + norm_back(grad_h_one, normed_one, inv_one, attn_gain)).astype(BF16)
     output = (residual_mid + ffn_branch).astype(BF16)
     branch_rms = jnp.stack(
@@ -1231,9 +1251,9 @@
         grad_w_key.astype(F32),
         grad_w_value.astype(F32),
         grad_w_output.astype(F32),
-        grad_w_gate.astype(F32),
-        grad_w_up.astype(F32),
-        grad_w_down.astype(F32),
+        grad_w_gate,
+        grad_w_up,
+        grad_w_down,
         small_sum[:width],
         small_sum[width:at],
         small_sum[at : at + HD],

time: 461 us -> 461 us (level)
  other arithmetic: 32.6 us -> 16.9 us
  Pallas kernels: 378 us -> 387 us
  local copies, waits for them, and re-layouts: 7.92 us -> 14.5 us
    convert_element_type x3 -> x0, other arithmetic: 15.7 us -> none  [the longest x1 6.79 us: per_device(): grad_w_gate.astype(F32)]
    pallas_call x0 -> x1, Pallas kernels: none -> 8.48 us  [widen(): pl.pallas_call(widen_kernel, grid=(steps,), out_shape=[jax.ShapeDtypeStru...]
    unnamed x60 -> x62, local copies, waits for them, and re-layouts: 2.85 us -> 9.4 us
where the time goes in v9:
time: 461 us
  Pallas kernels  387 us (84%)
  matrix products  25.9 us (6%)
  other arithmetic  16.9 us (4%)
  between operations  16.2 us (4%)
  local copies, waits for them, and re-layouts  14.5 us (3%)
    pallas_call x6, Pallas kernels, together(): pl.pallas_call(kernel, out_shape=[o for s in steps for o, _ in s.outputs]...  378 us
    dot_general x5, matrix products, matmul_left_t(): lax.dot_general(left, right, (((0,), (0,)), ((), ())), preferred_element_...  24.6 us
    unnamed x62, local copies, waits for them, and re-layouts  9.4 us
  transfers between devices with their start and end apart: 1, of which 0 were waited for; matrix products, arithmetic and copies ran while one was open for 6% of the time, Pallas kernels for 55%

profile of v9, /device:TPU:10, one launch (start us, length us, event | category | flops | bytes accessed | tf_op | source)
XLA Modules:
  0.0 460.5 jit_solution(16695239021391566358)
XLA Ops:
  7.2 89.8 %shard_map.262 = (bf16[1024,2048]{1,0:T(8,128)(2,1)}, f32[1024,384]{1,0:T(8,128)}, bf16[1024,256]{1,0:T(8,128)(2,1)}, f32[4,1,1024]{2,1,0:T(1,128)}, bf16[1024,2...) custom-call(bf16[128,2048]{1,0:T(8,128)(2,1)} %refs_0_.1, ...), custom_call_target="tpu_custom_call" | custom-call | flops 1 | bytes 1 | tf_op jit(solution)/shard_map/pallas_call | solution.py:918
  97.0 1.0 copy-done.14
  98.0 34.8 %shard_map.263 = (bf16[1024,2048]{1,0:T(8,128)(2,1)S(1)}, bf16[1024,1024]{1,0:T(8,128)(2,1)S(1)}, bf16[1024,1024]{1,0:T(8,128)(2,1)S(1)}, bf16[1024,1024]{1,0:T(8,128)(2,1)S(1)}) custom-call(bf16[128,2048]{1,0:T(8,128)(2,1)S(1)} %copy-done.14, bf16[1024,2048]{1,0:T(8,128)(2,1)} %get-tuple-element.52.refs_1_, bf16[2048,1024]{1,0:T(8,128)(2,1)} %refs_2_.3, ...), custom_call_target="tpu_custom_call" | custom-call | flops 1 | bytes 1 | tf_op jit(solution)/shard_map/pallas_call | solution.py:918
  132.9 6.1 %convolution_convert_fusion = bf16[2048,1024]{1,0:T(8,128)(2,1)} fusion(bf16[1024,2048]{1,0:T(8,128)(2,1)S(1)} %get-tuple-element.57, bf16[1024,1024]{1,0:T(8,128)(2,1)S(1)} %get-tuple-element.62.refs_1_), kind=kOutput, calls=%fused_computation | convolution fusion | flops 4297064448 | bytes 10485760 | tf_op jit(solution)/shard_map/dot_general | solution.py:1075
  139.0 6.1 %convolution_convert_fusion.1 = bf16[2048,1024]{1,0:T(8,128)(2,1)} fusion(bf16[1024,2048]{1,0:T(8,128)(2,1)S(1)} %get-tuple-element.57, bf16[1024,1024]{1,0:T(8,128)(2,1)S(1)} %get-tuple-element.61.refs_0_), kind=kOutput, calls=%fused_computation.1 | convolution fusion | flops 4297064448 | bytes 10485760 | tf_op jit(solution)/shard_map/dot_general | solution.py:1075
  145.2 6.2 %convolution_convert_fusion.2 = bf16[1024,2048]{1,0:T(8,128)(2,1)} fusion(bf16[1024,1024]{1,0:T(8,128)(2,1)S(1)} %get-tuple-element.60.refs_0_, bf16[1024,2048]{1,0:T(8,128)(2,1)S(1)} %copy-done.26), kind=kOutput, calls=%fused_computation.2 | convolution fusion | flops 4297064448 | bytes 10485760 | tf_op jit(solution)/shard_map/dot_general | solution.py:1075
  151.5 60.2 %shard_map.264 = f32[128,2048]{1,0:T(8,128)} custom-call(bf16[1024,1024]{1,0:T(8,128)(2,1)} %copy-done.4, bf16[1024,1024]{1,0:T(8,128)(2,1)} %copy-done.5, bf16[2048,1024]{1,0:T(8,128)(2,1)} %refs_2_.3, bf16[2048,1024]{1,0:T(8,128)(2,1)} %refs_3_.3), custom_call_target="tpu_custom_call" | custom-call | flops 1 | bytes 1 | tf_op jit(solution)/shard_map/pallas_call | solution.py:918
  212.0 2.9 multiply_reduce_fusion.3
  214.9 1.6 fusion.10.refs_2_
  216.5 52.8 %shard_map.265 = (f32[128,2048]{1,0:T(8,128)S(1)}, bf16[1024,2048]{1,0:T(8,128)(2,1)S(1)}) custom-call(bf16[1024,1024]{1,0:T(8,128)(2,1)S(1)} %get-tuple-element.60.refs_0_, bf16[1024,2048]{1,0:T(8,128)(2,1)S(1)} %copy-done, bf16[128,2048]{1,0:T(8,128)(2,1)S(1)} %fusion.10.refs_2_), custom_call_target="tpu_custom_call" | custom-call | flops 1 | bytes 1 | tf_op jit(solution)/shard_map/pallas_call | solution.py:918
  269.4 1.3 convolution_convert_fusion.3.refs_9_
  271.0 1.3 convolution_convert_fusion.4.refs_7_
  272.8 44.3 %shard_map.266 = (bf16[1024,384]{1,0:T(8,128)(2,1)S(1)}, f32[1,384]{1,0:T(1,128)S(1)}, bf16[256,2048]{1,0:T(8,128)(2,1)S(1)}) custom-call(f32[1024,384]{1,0:T(8,128)S(1)} %copy-done.6, f32[1024,128]{1,0:T(8,128)S(1)} %copy-done.12, f32[1024,128]{1,0:T(8,128)S(1)} %copy-done.13, f32[1,64]{1,0:T(1,128)S(1)} %bitcast.37, f32[1,64]{1,0:T(1,128)S(1)} %bitcast.39, ...), custom_call_target="tpu_custom_call" | custom-call | flops 1 | bytes 1 | tf_op jit(solution)/shard_map/pallas_call | solution.py:918
  317.0 1.0 copy-done.7
  318.0 1.6 constant_dynamic-slice_fusion
  319.6 4.9 %multiply_reduce_fusion = (f32[2048]{0:T(1024)S(1)}, bf16[2048,384]{1,0:T(8,128)(2,1)S(1)}, bf16[2048,384]{1,0:T(8,128)(2,1)S(1)}) fusion(bf16[2048,64]{1,0:T(8,128)(2,1)S(1)} %get-tuple-element.106, bf16[2048,64]{1,0:T(8,128)(2,1)S(1)} %get-tuple-element.107, bf16[2048,256]{1,0:T(8,128)(2,1)S(1)} %copy-done.28, bf16[1024,2048]{1,0:T(8,128)(2,1)} %get-tuple-element.64, ...), kind=kOutput, calls=%fused_computation.3 | convolution fusion | flops 1618475008 | bytes 9707520 | tf_op jit(solution)/shard_map/dot_general | solution.py:1075
  324.5 0.8 slice.47
  325.6 0.7 concatenate.12
  326.3 1.1 pad_maximum_fusion.1.refs_0_
  327.4 96.6 %shard_map.267 = (bf16[2048,512]{1,0:T(8,128)(2,1)S(1)}, bf16[2048,512]{1,0:T(8,128)(2,1)S(1)}, f32[64,128]{1,0:T(8,128)S(1)}, f32[128,2048]{1,0:T(8,128)S(1)}, bf16[2048,256]{1,0:T(8,128)(2,1)S(1)}) custom-call(bf16[2112,128]{1,0:T(8,128)(2,1)S(1)} %pad_maximum_fusion.1.refs_0_, bf16[1024,384]{1,0:T(8,128)(2,1)S(1)} %get-tuple-element.71.refs_1_, ...), custom_call_target="tpu_custom_call" | custom-call | flops 1 | bytes 1 | tf_op jit(solution)/shard_map/pallas_call | solution.py:918
  424.0 2.6 convert_element_type.61
  426.6 2.6 convert_element_type.62
  429.2 1.5 convert_element_type.60
  431.9 1.6 convert_element_type.63
  433.8 1.9 fusion.8
  435.8 0.6 pad_maximum_fusion.2
  436.3 0.6 fusion.11
  436.9 0.6 slice_bitcast_fusion
  437.5 2.2 copy-done.1
  439.7 2.2 copy-done.2
  441.9 2.2 copy-done.3
  444.1 8.5 %shard_map.268 = (f32[2048,1024]{1,0:T(8,128)}, f32[2048,1024]{1,0:T(8,128)}, f32[1024,2048]{1,0:T(8,128)}) custom-call(bf16[2048,1024]{1,0:T(8,128)(2,1)S(1)} %copy-done.1, bf16[2048,1024]{1,0:T(8,128)(2,1)S(1)} %copy-done.2, bf16[1024,2048]{1,0:T(8,128)(2,1)S(1)} %copy-done.3), custom_call_target="tpu_custom_call" | custom-call | flops 1 | bytes 1 | tf_op jit(solution)/shard_map/pallas_call | solution.py:1099
  (75 shorter events, 2.2 us)
Async XLA Ops:
  7.2 430.3 %all-reduce.4.cloned.1.call-start = ((), (), s32[]{:S(2)}) async-start(), calls=%async_computation | async-start | bytes 25165824 | tf_op jit(solution)/shard_map/psum | solution.py:1176
  97.0 1.0 copy-start.14
  132.9 6.2 %copy-start.5 = (bf16[1024,1024]{1,0:T(8,128)(2,1)}, bf16[1024,1024]{1,0:T(8,128)(2,1)S(1)}, u32[]{:S(2)}) copy-start(bf16[1024,1024]{1,0:T(8,128)(2,1)S(1)} %get-tuple-element.62.refs_1_) | copy-start | bytes 6291460
  132.9 6.1 %copy-start.4 = (bf16[1024,1024]{1,0:T(8,128)(2,1)}, bf16[1024,1024]{1,0:T(8,128)(2,1)S(1)}, u32[]{:S(2)}) copy-start(bf16[1024,1024]{1,0:T(8,128)(2,1)S(1)} %get-tuple-element.61.refs_0_) | copy-start | bytes 6291460
  139.0 6.1 %copy-start.26 = (bf16[1024,2048]{1,0:T(8,128)(2,1)S(1)}, bf16[1024,2048]{1,0:T(8,128)(2,1)}, u32[]{:S(2)}) copy-start(bf16[1024,2048]{1,0:T(8,128)(2,1)} %get-tuple-element.52.refs_1_) | copy-start | bytes 12582916
  151.4 60.3 %copy-start.19 = (bf16[128,2048]{1,0:T(8,128)(2,1)S(1)}, bf16[128,2048]{1,0:T(8,128)(2,1)}, u32[]{:S(2)}) copy-start(bf16[128,2048]{1,0:T(8,128)(2,1)} %refs_0_.1) | copy-start | bytes 1572868
  151.4 60.3 %copy-start.21 = (f32[128,2048]{1,0:T(8,128)S(1)}, f32[128,2048]{1,0:T(8,128)}, u32[]{:S(2)}) copy-start(f32[128,2048]{1,0:T(8,128)} %get-tuple-element.55) | copy-start | bytes 3145732
  151.4 60.5 %copy-start.29 = (f32[2048]{0:T(1024)S(1)}, f32[2048]{0:T(1024)}, u32[]{:S(2)}) copy-start(f32[2048]{0:T(1024)} %param.26) | copy-start | bytes 24580
  151.5 63.4 %copy-start.24 = (bf16[128,2048]{1,0:T(8,128)(2,1)S(1)}, bf16[128,2048]{1,0:T(8,128)(2,1)}, u32[]{:S(2)}) copy-start(bf16[128,2048]{1,0:T(8,128)(2,1)} %refs_1_.2) | copy-start | bytes 1572868
  211.7 4.8 %copy-start = (bf16[1024,2048]{1,0:T(8,128)(2,1)S(1)}, bf16[1024,2048]{1,0:T(8,128)(2,1)}, u32[]{:S(2)}) copy-start(bf16[1024,2048]{1,0:T(8,128)(2,1)} %refs_1_.3) | copy-start | bytes 12582916
  216.5 52.9 %copy-start.11 = (bf16[1024,256]{1,0:T(8,128)(2,1)S(1)}, bf16[1024,256]{1,0:T(8,128)(2,1)}, u32[]{:S(2)}) copy-start(bf16[1024,256]{1,0:T(8,128)(2,1)} %get-tuple-element.68.refs_6_) | copy-start | bytes 1572868
  269.4 3.0 copy-start.9
  269.4 1.6 copy-start.27
  271.0 1.4 copy-start.6
  271.0 1.6 copy-start.12
  271.0 1.8 copy-start.13
  271.0 1.8 copy-start.15
  271.0 1.8 copy-start.16
  271.0 1.8 copy-start.17
  271.0 1.8 copy-start.18
  272.3 47.3 %copy-start.28 = (bf16[2048,256]{1,0:T(8,128)(2,1)S(1)}, bf16[2048,256]{1,0:T(8,128)(2,1)}, u32[]{:S(2)}) copy-start(bf16[2048,256]{1,0:T(8,128)(2,1)} %refs_6_.1) | copy-start | bytes 3145732
  317.0 1.0 copy-start.7
  319.6 5.9 %copy-start.30 = (f32[2048]{0:T(1024)S(1)}, f32[2048]{0:T(1024)}, u32[]{:S(2)}) copy-start(f32[2048]{0:T(1024)} %param.25) | copy-start | bytes 24580
  426.6 5.3 %copy-start.8 = (bf16[256,2048]{1,0:T(8,128)(2,1)S(1)}, bf16[256,2048]{1,0:T(8,128)(2,1)}, u32[]{:S(2)}) copy-start(bf16[256,2048]{1,0:T(8,128)(2,1)} %copy-done.7) | copy-start | bytes 3145732
  429.2 4.3 copy-start.20
  429.2 4.6 %copy-start.10 = (f32[128,2048]{1,0:T(8,128)S(1)}, f32[128,2048]{1,0:T(8,128)}, u32[]{:S(2)}) copy-start(f32[128,2048]{1,0:T(8,128)} %copy-done.9) | copy-start | bytes 3145732
  429.2 4.6 %copy-start.22 = (f32[128,2048]{1,0:T(8,128)S(1)}, f32[128,2048]{1,0:T(8,128)}, u32[]{:S(2)}) copy-start(f32[128,2048]{1,0:T(8,128)} %get-tuple-element.55) | copy-start | bytes 3145732
  429.2 4.7 %copy-start.23 = (f32[128,2048]{1,0:T(8,128)S(1)}, f32[128,2048]{1,0:T(8,128)}, u32[]{:S(2)}) copy-start(f32[128,2048]{1,0:T(8,128)} %shard_map.264) | copy-start | bytes 3145732
  429.2 4.7 %copy-start.25 = (bf16[128,2048]{1,0:T(8,128)(2,1)S(1)}, bf16[128,2048]{1,0:T(8,128)(2,1)}, u32[]{:S(2)}) copy-start(bf16[128,2048]{1,0:T(8,128)(2,1)} %refs_1_.2) | copy-start | bytes 1572868
  437.5 2.2 copy-start.1
  439.7 2.2 copy-start.2
  441.9 2.2 copy-start.3
Sparse Core Ops, SparseCore 0:
  151.5 280.7 all-reduce.3
